TPU v7x, 256 devices: a whole 4x4x8 slice. The times are simulated.
256 devices in a mesh: patch: 64 (over y, z, core), mem: 4 (over x).
Axes of the slice: x: 4, y: 4, z: 8, core: 2. Of those that a mesh axis runs over, the one named last changes fastest.
Arguments:
- atmos: bfloat16 [128, 8, 65536], P('mem', None, 'patch'), may hold values from -6 to 6
- land: bfloat16 [128, 8, 262144], P('mem', None, 'patch'), may hold values from -6 to 6
- land_mask: int32 [262144], P('patch'), may hold values 0 or 1
- tile_owner: int32 [262144, 1], P('patch'), may hold values from 0 to 63; in each aligned block of 4096 rows (0 to 4095, 4096 to 8191, ...) at most 128 rows name the same one
- tile_column: int32 [262144], P('patch'), may hold values from 0 to 1023
- tile_weight: bfloat16 [262144], P('patch'), may hold values from 0.19921875 to 1
- obs_value: float32 [32768], P('patch'), may hold values from -12 to 12
- observation_column: int32 [32768], P('patch'), may hold values from 0 to 1023
- obs_error: float32 [32768], P('patch'), may hold values from 0.5 to 4
- loc_blocks: int32 [64, 4], P('patch'), may hold values from 0 to 63, as said below
Outputs:
- atmos_analysis: bfloat16 [128, 8, 65536], P('mem', None, 'patch')
- land_analysis: bfloat16 [128, 8, 262144], P('mem', None, 'patch')
Inputs may be any that keep to these rules, and one draw needn't show every extreme that they name: `tile_owner`: among the tiles of one tile block at most 128 have the same owner, and in some blocks exactly 128 do. `loc_blocks`: patches lie row by row on a grid 8 patches wide, indices taken modulo the number of patches. Row p begins with p and then names three different ones of its four grid neighbours p - 1, p + 1, p - 8, p + 8, in that order.
All inputs are finite; a program needn't handle non-finite values. No bound on the sum of `land_mask` on one device may be relied on, other than what follows from the above.
Results may differ from a plain program's by a relative error of at most 0.006.
Values may be sent and summed in bfloat16 or wider, within the bound.
No kernel may reach another device: no remote copies, remote signals or barrier semaphores. Data moves between devices by JAX's collectives and lax.ppermute only.
A program may use at most 128 MiB of HBM per device.

v0:
```python
import math

import jax
import jax.numpy as jnp
from jax import lax
from jax.experimental import pallas as pl
from jax.experimental.pallas import tpu as pltpu
from jax.sharding import PartitionSpec as P

SWEEPS = 10
PRECISE = lax.Precision.HIGHEST
BF = jnp.bfloat16
F32 = jnp.float32
I32 = jnp.int32

NN = (((1,), (0,)), ((), ()))
NT = (((1,), (1,)), ((), ()))


def dot(a, b, dims=NN):
    return lax.dot_general(a, b, dims, preferred_element_type=F32)


def iota(shape, axis):
    return lax.broadcasted_iota(I32, shape, axis)


VMEM = pl.BlockSpec(memory_space=pltpu.VMEM)
SMEM = pl.BlockSpec(memory_space=pltpu.SMEM)


def params():
    return pltpu.CompilerParams(vmem_limit_bytes=60 * 1024 * 1024)


def shifted(value, axis, steps):
    count = lax.axis_size(axis)
    pairs = [(source, (source + steps) % count) for source in range(count)]
    return lax.ppermute(value, axis, pairs)


def order_tiles(owners, npatch):
    tiles = owners.shape[1]
    block = 512

    def kernel(owner_ref, rank_ref, pos_ref, start_ref):
        before = (iota((block, block), 0) < iota((block, block), 1)).astype(BF)
        carry = jnp.zeros((npatch, 1), F32)
        for c in range(tiles // block):
            cut = slice(c * block, (c + 1) * block)
            hot = owner_ref[:, cut] == iota((npatch, block), 0)
            ahead = dot(hot.astype(BF), before) + carry
            hot32 = hot.astype(F32)
            rank_ref[:, cut] = jnp.sum(hot32 * ahead, axis=0, keepdims=True).astype(I32)
            carry = carry + jnp.sum(hot32, axis=1, keepdims=True)
        lower = (iota((npatch, npatch), 0) > iota((npatch, npatch), 1)).astype(BF)
        wide = dot(lower, jnp.broadcast_to(carry, (npatch, 128)).astype(BF))
        starts = wide[:, :1]
        start_ref[...] = starts.astype(I32)
        for c in range(tiles // block):
            cut = slice(c * block, (c + 1) * block)
            hot = (owner_ref[:, cut] == iota((npatch, block), 0)).astype(F32)
            first = jnp.sum(hot * starts, axis=0, keepdims=True).astype(I32)
            pos_ref[:, cut] = rank_ref[:, cut] + first

    return pl.pallas_call(
        kernel,
        out_shape=(
            jax.ShapeDtypeStruct((1, tiles), I32),
            jax.ShapeDtypeStruct((1, tiles), I32),
            jax.ShapeDtypeStruct((npatch, 1), I32),
        ),
        in_specs=[VMEM],
        out_specs=(VMEM, VMEM, VMEM),
        compiler_params=params(),
        name="order_tiles",
    )(owners)


def bucket_tiles(weighted, owners, ranks, columns, npatch, bucket):
    rows, tiles = weighted.shape
    low = 4
    high = npatch // low
    block = 1024
    steps = tiles // block

    def kernel(w_ref, owner_ref, rank_ref, col_ref, out_ref, acc_ref, cacc_ref):
        step = pl.program_id(0)
        owner = owner_ref[...]
        slot = (owner & (low - 1)) * bucket + rank_ref[...]
        hot = (iota((low * bucket, block), 0) == slot).astype(F32).astype(BF)
        group = owner >> 2
        value = w_ref[...]
        zero = jnp.zeros_like(value)
        picked = jnp.concatenate(
            [jnp.where(group == g, value, zero) for g in range(high)], axis=0
        )
        part = dot(picked, hot, NT)
        col = col_ref[...]
        half = iota((2 * high, block), 0)
        digit = jnp.where((half & 1) == 0, col >> 5, col & 31)
        digits = jnp.where((half >> 1) == group, digit, 0).astype(F32).astype(BF)
        cpart = dot(digits, hot, NT)

        @pl.when(step == 0)
        def _():
            acc_ref[...] = part
            cacc_ref[...] = cpart

        @pl.when(step > 0)
        def _():
            acc_ref[...] += part
            cacc_ref[...] += cpart

        @pl.when(step == steps - 1)
        def _():
            for o in range(npatch):
                g, b = o // low, o % low
                cut = slice(b * bucket, (b + 1) * bucket)
                out_ref[o, :rows, :] = acc_ref[g * rows : (g + 1) * rows, cut].astype(BF)
                out_ref[o, rows : rows + 2, :] = cacc_ref[2 * g : 2 * g + 2, cut].astype(BF)

    lane = pl.BlockSpec((1, block), lambda i: (0, i))
    return pl.pallas_call(
        kernel,
        grid=(steps,),
        out_shape=jax.ShapeDtypeStruct((npatch, rows + 2, bucket), BF),
        in_specs=[pl.BlockSpec((rows, block), lambda i: (0, i)), lane, lane, lane],
        out_specs=pl.BlockSpec((npatch, rows + 2, bucket), lambda i: (0, 0, 0)),
        scratch_shapes=[
            pltpu.VMEM((high * rows, low * bucket), F32),
            pltpu.VMEM((2 * high, low * bucket), F32),
        ],
        compiler_params=params(),
        name="bucket_tiles",
    )(weighted, owners, ranks, columns)


def lane_swap(rows, a, b):
    source = iota((rows, rows), 0)
    target = iota((rows, rows), 1)
    return ((source % b) * a + source // b == target).astype(F32).astype(BF)


def sort_land(pos, land_rows, levels):
    rows, tiles = land_rows.shape
    block = 512

    def kernel(pos_ref, x_ref, out_ref):
        place = iota((block, tiles), 0) + pl.program_id(0) * block
        hot = (place == pos_ref[...]).astype(F32).astype(BF)
        moved = dot(hot, x_ref[...], NT).astype(BF)
        out_ref[...] = dot(moved, lane_swap(rows, rows // levels, levels)).astype(BF)

    return pl.pallas_call(
        kernel,
        grid=(tiles // block,),
        out_shape=jax.ShapeDtypeStruct((tiles, rows), BF),
        in_specs=[
            pl.BlockSpec((1, tiles), lambda i: (0, 0)),
            pl.BlockSpec((rows, tiles), lambda i: (0, 0)),
        ],
        out_specs=pl.BlockSpec((block, rows), lambda i: (i, 0)),
        compiler_params=params(),
        name="sort_land",
    )(pos, land_rows)


def screen_forecast(received, base, obs_column):
    npatch, rows2, bucket = received.shape
    rows = rows2 - 2
    nobs = obs_column.shape[0]
    columns = base.shape[1]
    group = 8

    def kernel(in_ref, base_ref, obs_ref, out_ref):
        obs = obs_ref[...]
        place = iota((nobs, columns), 1)
        acc = dot(base_ref[...], (obs == place).astype(F32).astype(BF), NT)
        for g in range(npatch // group):
            values = jnp.concatenate(
                [in_ref[g * group + i, :rows, :] for i in range(group)], axis=1
            )
            digits = jnp.concatenate(
                [in_ref[g * group + i, rows:, :] for i in range(group)], axis=1
            ).astype(F32)
            col = (digits[0:1] * 32.0 + digits[1:2]).astype(I32)
            acc = acc + dot(values, (obs == col).astype(F32).astype(BF), NT)
        out_ref[...] = acc.astype(BF)

    return pl.pallas_call(
        kernel,
        out_shape=jax.ShapeDtypeStruct((rows, nobs), BF),
        in_specs=[VMEM, VMEM, VMEM],
        out_specs=VMEM,
        compiler_params=params(),
        name="screen_forecast",
    )(received, base, obs_column)


def mix_land(states, sources, starts, mixes, pos_col, land_rows, mask_row, levels):
    slots = len(states)
    tiles, width = states[0].shape
    local = width // levels
    npatch = mixes.shape[0]
    members = mixes.shape[2]
    window = 144
    block = 512

    def kernel(src_ref, start_ref, *refs):
        state_refs = refs[:slots]
        mix_ref, pos_ref, land_ref, mask_ref, out_ref, tiled_ref, y_ref, z_ref = refs[slots:]

        @pl.when(pl.program_id(0) == 0)
        def _():
            for s in range(slots):
                spread = (
                    iota((members, width), 0)
                    == (iota((members, width), 1) & (local - 1)) + src_ref[s] * local
                )
                tiled_ref[:, s * width : (s + 1) * width] = dot(
                    mix_ref[...], spread.astype(F32).astype(BF)
                ).astype(BF)
            y_ref[...] = jnp.zeros_like(y_ref)
            lane_level = iota((local, width), 1) // local

            def one_owner(o, unused):
                first = start_ref[o]
                base = pl.multiple_of(
                    jnp.minimum((first // 16) * 16, tiles - window), 16
                )
                acc = jnp.zeros((window, width), F32)
                for s in range(slots):
                    small = tiled_ref[
                        pl.ds(pl.multiple_of(o * local, local), local),
                        s * width : (s + 1) * width,
                    ]
                    zero = jnp.zeros_like(small)
                    weight = jnp.concatenate(
                        [jnp.where(lane_level == l, small, zero) for l in range(levels)], axis=0
                    )
                    acc = acc + dot(state_refs[s][pl.ds(base, window), :], weight, NT)
                value = acc.astype(BF)
                rest = y_ref[pl.ds(base, window), :]
                y_ref[pl.ds(base, window), :] = jnp.where(
                    iota((window, width), 0) + base >= first, value, rest
                )
                return unused

            lax.fori_loop(0, npatch, one_owner, 0)
            z_ref[...] = dot(y_ref[...], lane_swap(width, levels, local)).astype(BF)

        hot = (iota((block, tiles), 1) == pos_ref[...]).astype(F32).astype(BF)
        back = dot(hot, z_ref[...])
        out_ref[...] = jnp.where(mask_ref[...] == 1, back.T.astype(BF), land_ref[...])

    full = lambda shape: pl.BlockSpec(shape, lambda i: (0,) * len(shape))
    return pl.pallas_call(
        kernel,
        grid=(tiles // block,),
        out_shape=jax.ShapeDtypeStruct((width, tiles), BF),
        in_specs=[SMEM, SMEM]
        + [VMEM] * slots
        + [
            VMEM,
            pl.BlockSpec((block, 1), lambda i: (i, 0)),
            pl.BlockSpec((width, block), lambda i: (0, i)),
            pl.BlockSpec((1, block), lambda i: (0, i)),
        ],
        out_specs=pl.BlockSpec((width, block), lambda i: (0, i)),
        scratch_shapes=[
            pltpu.VMEM((npatch * local, slots * width), BF),
            pltpu.VMEM((tiles, width), BF),
            pltpu.VMEM((tiles, width), BF),
        ],
        compiler_params=params(),
        name="mix_land",
    )(
        sources,
        starts,
        *states,
        mixes.reshape(npatch * local, members),
        pos_col,
        land_rows,
        mask_row,
    )


def settle(local_gram, local_proj):
    members = local_gram.shape[0]
    identity = jnp.eye(members, dtype=jnp.float32)
    system = local_gram + (members - 1.0) * identity
    trace_scale = jnp.trace(system)
    upper_iter = system / trace_scale
    lower_iter = identity
    for sweep_index in range(SWEEPS):
        middle_step = 0.5 * (3.0 * identity - jnp.dot(lower_iter, upper_iter, precision=PRECISE))
        upper_iter = jnp.dot(upper_iter, middle_step, precision=PRECISE)
        lower_iter = jnp.dot(middle_step, lower_iter, precision=PRECISE)
    inv_root = lower_iter / jnp.sqrt(trace_scale)
    mean_shift = jnp.dot(
        inv_root, jnp.dot(inv_root, local_proj, precision=PRECISE), precision=PRECISE
    )
    spread = mean_shift[:, None] + math.sqrt(members - 1.0) * inv_root
    centered = spread - jnp.mean(spread, axis=0, keepdims=True)
    return (centered + 1.0 / members).astype(jnp.bfloat16)


def to_all(value, axis):
    count = lax.axis_size(axis)
    copies = jnp.broadcast_to(value[None], (count,) + value.shape)
    return lax.all_to_all(copies, axis, split_axis=0, concat_axis=0, tiled=True)


def shards(
    atmos,
    land,
    land_mask,
    tile_owner,
    tile_column,
    tile_weight,
    obs_value,
    observation_column,
    obs_error,
    loc_blocks,
):
    npatch = lax.axis_size("patch")
    mem_count = lax.axis_size("mem")
    local, levels, columns = atmos.shape
    layers, tiles = (land.shape[1], land.shape[2])
    members = local * mem_count
    bucket = 2 * tiles // npatch
    row_width = max(2, npatch // 8)
    mem_rank = lax.axis_index("mem")
    patch_rank = lax.axis_index("patch")

    atmos_rows = atmos.reshape(local * levels, columns)
    atmos_parts = [atmos_rows] + [shifted(atmos_rows, "mem", s) for s in (1, -1, 2)]

    owners = tile_owner.reshape(1, tiles)
    ranks, pos, starts = order_tiles(owners, npatch)
    keep = tile_weight.astype(F32) * land_mask.astype(F32)
    weighted = (land[:, 0, :].astype(F32) * keep[None, :]).astype(BF)
    packed = bucket_tiles(
        weighted, owners, ranks, tile_column.reshape(1, tiles), npatch, bucket
    )
    received = lax.all_to_all(packed, "patch", split_axis=0, concat_axis=0, tiled=True)

    land_rows = land.reshape(local * layers, tiles)
    mine = sort_land(pos, land_rows, layers)
    half = tiles // 2
    from_prev = shifted(mine, "mem", 1)
    from_next = shifted(mine, "mem", -1)

    forecast = screen_forecast(received, atmos[:, 0, :], observation_column.reshape(-1, 1))
    ensemble = to_all(forecast, "mem").reshape(members, -1).astype(F32)
    center = jnp.mean(ensemble, axis=0)
    inverse_sd = lax.rsqrt(obs_error)
    scaled = (ensemble - center[None, :]) * inverse_sd[None, :]
    innovation = (obs_value - center) * inverse_sd
    gram_own = jnp.dot(scaled, scaled.T, precision=PRECISE)
    proj_own = jnp.dot(scaled, innovation, precision=PRECISE)
    listed = loc_blocks[0]
    own_stats = jnp.concatenate([gram_own, proj_own[None, :]], axis=0)
    local_stats = own_stats
    for offset in (1, -1, row_width, -row_width):
        near_stats = shifted(own_stats, "patch", offset)
        source = (patch_rank - offset) % npatch
        used = jnp.sum((listed == source).astype(jnp.float32))
        local_stats = local_stats + used * near_stats
    local_stats, from_prev, from_next = lax.optimization_barrier(
        (local_stats, from_prev, from_next)
    )
    far_low = shifted(from_prev[:half], "mem", 1)
    far_high = shifted(from_next[half:], "mem", -1)
    mix = settle(local_stats[:members], local_stats[members])
    mix_t = mix.T

    own_cols = lax.dynamic_slice_in_dim(mix_t, mem_rank * local, local, 0)
    all_mixes = to_all(own_cols, "patch")

    slot_source = [mem_rank, mem_rank - 1, mem_rank + 1, mem_rank - 2]
    sources = jnp.stack([s % mem_count for s in slot_source]).astype(I32)
    atmos_out = 0.0
    for part, source in zip(atmos_parts, slot_source):
        rows = lax.dynamic_slice_in_dim(own_cols, (source % mem_count) * local, local, 1)
        atmos_out = atmos_out + jnp.einsum(
            "jk,klc->jlc", rows, part.reshape(local, levels, columns), preferred_element_type=F32
        )
    atmos_analysis = atmos_out.astype(BF)

    far = jnp.concatenate([far_low, far_high], axis=0)
    land_out = mix_land(
        [mine, from_prev, from_next, far],
        sources,
        starts.reshape(npatch),
        all_mixes,
        pos.reshape(tiles, 1),
        land_rows,
        land_mask.reshape(1, tiles),
        layers,
    )
    return (atmos_analysis, land_out.reshape(local, layers, tiles))


def solution(mesh):
    in_specs = (
        P("mem", None, "patch"),
        P("mem", None, "patch"),
        P("patch"),
        P("patch", None),
        P("patch"),
        P("patch"),
        P("patch"),
        P("patch"),
        P("patch"),
        P("patch", None),
    )
    out_specs = (P("mem", None, "patch"), P("mem", None, "patch"))
    return jax.shard_map(shards, mesh=mesh, in_specs=in_specs, out_specs=out_specs, check_vma=False)
```

profile of v0, /device:TPU:1, one launch (start us, length us, event | category | flops | bytes accessed | tf_op | source)
XLA Modules:
  0.0 195.9 jit_solution(2882154182502321791)
XLA Ops:
  0.6 2.3 %order_tiles.1 = (s32[1,4096]{1,0:T(1,128)}, s32[1,4096]{1,0:T(1,128)}, s32[64,1]{1,0:T(8,128)}) custom-call(s32[1,4096]{1,0:T(1,128)} %bitcast.124), custom_call_target="tpu_custom_call" | custom-call | tf_op jit(solution)/shard_map/order_tiles/pallas_call | solution.py:66
  3.0 2.1 %slice.18 = bf16[32,1,4096]{2,1,0:T(2,128)(2,1)S(1)} slice(bf16[32,8,4096]{2,1,0:T(8,128)(2,1)} %param.11), slice={[0:32], [0:1], [0:4096]} | slice | bytes 524288 | tf_op jit(solution)/shard_map/slice | solution.py:343
  5.0 0.7 convert_multiply_fusion.1
  5.7 1.0 fusion.12.w_ref
  6.8 6.2 %bucket_tiles.1 = bf16[64,34,128]{2,1,0:T(8,128)(2,1)} custom-call(bf16[32,4096]{1,0:T(8,128)(2,1)} %fusion.12.w_ref, s32[1,4096]{1,0:T(1,128)} %bitcast.125, s32[1,4096]{1,0:T(1,128)} %get-tuple-element.8.rank_ref, s32[1,4096]{1,0:T(1,128)} %bitcast.127), custom_call_target="tpu_custom_call" | custom-call | tf_op jit(solution)/shard_map/bucket_tiles/pallas_call | solution.py:124
  12.9 13.1 %all-to-all-start = ((bf16[64,34,128]{2,1,0:T(8,128)(2,1)}), bf16[64,34,128]{2,1,0:T(8,128)(2,1)S(1)}, u32[]{:S(2)}, u32[]{:S(2)}) async-start(bf16[64,34,128]{2,1,0:T(8,128)(2,1)} %bucket_tiles.1), calls=%async_computation | async-start | bytes 1310720 | tf_op jit(solution)/shard_map/all_to_all | solution.py:347
  26.1 14.3 %sort_land.1.refs_0_ = bf16[4096,256]{1,0:T(8,128)(2,1)} custom-call(s32[1,4096]{1,0:T(1,128)} %get-tuple-element.9.pos_ref, bf16[256,4096]{1,0:T(8,128)(2,1)} %bitcast.114), custom_call_target="tpu_custom_call" | custom-call | tf_op jit(solution)/shard_map/sort_land/pallas_call | solution.py:155
  40.4 1.2 collective-permute-start.4
  41.6 1.5 collective-permute-start.5
  43.1 1.1 copy.26
  44.2 0.9 copy.27.obs_ref
  45.1 1.5 slice_bitcast_fusion.base_ref
  46.6 0.8 copy-done.1
  47.4 4.7 %screen_forecast.1 = bf16[32,512]{1,0:T(8,128)(2,1)} custom-call(bf16[64,34,128]{2,1,0:T(8,128)(2,1)} %copy-done.1, bf16[32,1024]{1,0:T(8,128)(2,1)} %slice_bitcast_fusion.base_ref, s32[512,1]{1,0:T(8,128)} %copy.27.obs_ref), custom_call_target="tpu_custom_call" | custom-call | tf_op jit(solution)/shard_map/screen_forecast/pallas_call | solution.py:191
  52.1 1.4 broadcast_in_dim.7
  53.5 3.6 %all-to-all-start.1 = ((bf16[4,32,512]{2,1,0:T(8,128)(2,1)}), bf16[4,32,512]{2,1,0:T(8,128)(2,1)S(1)}, u32[]{:S(2)}, u32[]{:S(2)}) async-start(bf16[4,32,512]{2,1,0:T(8,128)(2,1)} %broadcast_in_dim.7), calls=%async_computation.1 | async-start | bytes 262144 | tf_op jit(solution)/shard_map/all_to_all | solution.py:312
  57.2 2.0 %copy.32.refs_5_ = s32[4096,1]{1,0:T(8,128)} copy(s32[4096,1]{0,1:T(1,128)S(1)} %bitcast.123) | data formatting | bytes 32768 | tf_op jit(solution)/shard_map/reshape | solution.py:398
  59.1 0.7 reduce.5.start_ref
  59.8 30.9 %all-to-all-done.1 = bf16[4,32,512]{2,1,0:T(8,128)(2,1)S(1)} async-done(((bf16[4,32,512]{2,1,0:T(8,128)(2,1)}), bf16[4,32,512]{2,1,0:T(8,128)(2,1)S(1)}, u32[]{:S(2)}, u32[]{:S(2)}) %all-to-all-start.1) | async-done | bytes 131104 | tf_op jit(solution)/shard_map/all_to_all | solution.py:312
  91.1 0.4 fusion.44
  91.5 2.9 %collective-permute-start = (f32[129,128]{1,0:T(8,128)S(1)}, f32[129,128]{1,0:T(8,128)S(1)}, u32[]{:S(2)}, u32[]{:S(2)}) collective-permute-start(f32[129,128]{1,0:T(8,128)S(1)} %pad_maximum_fusion.1), channel_id=1, source_target_pairs={{0,4},{4,8},{8,12},{12,16},{16,20},{20,24},{24,28},{28,32},{32,36}... | collective-permute-start | bytes 198152 | tf_op jit(solution)/shard_map/ppermute | solution.py:39
  94.5 0.6 fusion.33
  95.1 4.2 %collective-permute-start.2 = (f32[129,128]{1,0:T(8,128)S(1)}, f32[129,128]{1,0:T(8,128)S(1)}, u32[]{:S(2)}, u32[]{:S(2)}) collective-permute-start(f32[129,128]{1,0:T(8,128)S(1)} %pad_maximum_fusion.1), channel_id=1, source_target_pairs={{0,32},{4,36},{8,40},{12,44},{16,48},{20,52},{24,56},{28,60},{32,6... | collective-permute-start | bytes 198152 | tf_op jit(solution)/shard_map/ppermute | solution.py:39
  99.3 3.3 %collective-permute-start.3 = (f32[129,128]{1,0:T(8,128)S(1)}, f32[129,128]{1,0:T(8,128)S(1)}, u32[]{:S(2)}, u32[]{:S(2)}) collective-permute-start(f32[129,128]{1,0:T(8,128)S(1)} %pad_maximum_fusion.1), channel_id=1, source_target_pairs={{0,224},{4,228},{8,232},{12,236},{16,240},{20,244},{24,248},{28,25... | collective-permute-start | bytes 198152 | tf_op jit(solution)/shard_map/ppermute | solution.py:39
  102.6 0.6 pad_add_fusion.src_ref
  103.2 0.9 collective-permute-start.6
  104.4 1.7 collective-permute-start.8
  106.0 1.8 collective-permute-done.3
  107.9 1.7 collective-permute-start.7
  109.6 2.5 %multiply_add_fusion = f32[129,128]{1,0:T(8,128)S(1)} fusion(f32[129,128]{1,0:T(8,128)S(1)} %collective-permute-done.3, f32[129,128]{1,0:T(8,128)S(1)} %collective-permute-done.2, f32[129,128]{1,0:T(8,128)S(1)} %collective-permute-done.1, f32[129,128]{1,0:T(8,128)S(1)} %collective-permute-done, f32[]{:T(128)} %get-tuple-element.22, f32[]{:T(128)} %get-tuple-element.23, ...), kind=kLoop, calls=%fused_computation.40 | loop fusion | flops 148608 | bytes 396304 | tf_op jit(solution)/shard_map/add | solution.py:370
  112.1 0.7 select_reduce_fusion
  112.8 0.8 fusion.11
  113.7 0.9 fusion.21
  120.5 2.3 %slice.23 = bf16[2048,256]{1,0:T(8,128)(2,1)} slice(bf16[4096,256]{1,0:T(8,128)(2,1)} %collective-permute-done.5.refs_2_), slice={[2048:4096], [0:256]} | slice | bytes 2097152 | tf_op jit(solution)/shard_map/slice | solution.py:375
  122.8 1.1 slice.22
  123.9 1.5 collective-permute-start.9
  126.4 0.9 broadcast_in_dim.10
  127.3 12.1 %all-to-all-start.2 = ((bf16[64,32,128]{2,1,0:T(8,128)(2,1)}), bf16[64,32,128]{2,1,0:T(8,128)(2,1)S(1)}, u32[]{:S(2)}, u32[]{:S(2)}) async-start(bf16[64,32,128]{2,1,0:T(8,128)(2,1)} %broadcast_in_dim.10), calls=%async_computation.2 | async-start | bytes 1048576 | tf_op jit(solution)/shard_map/all_to_all | solution.py:312
  139.4 0.8 fusion.27
  140.2 0.8 convolution_add_fusion.1
  141.1 1.8 fusion.13
  142.9 1.8 fusion.1
  144.7 1.1 copy.33
  145.8 4.2 %collective-permute-done.10 = bf16[2048,256]{1,0:T(8,128)(2,1)} collective-permute-done((bf16[2048,256]{1,0:T(8,128)(2,1)}, bf16[2048,256]{1,0:T(8,128)(2,1)}, u32[]{:S(2)}, u32[]{:S(2)}) %collective-permute-start.10) | collective-permute-done | bytes 1048608 | tf_op jit(solution)/shard_map/ppermute | solution.py:39
  150.0 3.0 %pad_maximum_fusion.refs_3_ = bf16[4096,256]{1,0:T(8,128)(2,1)} fusion(bf16[2048,256]{1,0:T(8,128)(2,1)} %collective-permute-done.10, bf16[2048,256]{1,0:T(8,128)(2,1)} %collective-permute-done.9), kind=kLoop, calls=%fused_computation | loop fusion | flops 4194304 | bytes 4194304 | tf_op jit(solution)/shard_map/concatenate | solution.py:392
  153.0 3.7 %all-to-all-done.2 = bf16[64,32,128]{2,1,0:T(8,128)(2,1)S(1)} async-done(((bf16[64,32,128]{2,1,0:T(8,128)(2,1)}), bf16[64,32,128]{2,1,0:T(8,128)(2,1)S(1)}, u32[]{:S(2)}, u32[]{:S(2)}) %all-to-all-start.2) | async-done | bytes 524320 | tf_op jit(solution)/shard_map/all_to_all | solution.py:312
  156.7 0.8 copy-done.2
  157.5 38.3 %mix_land.1 = bf16[256,4096]{1,0:T(8,128)(2,1)} custom-call(s32[4]{0:T(128)} %pad_add_fusion.src_ref, s32[64]{0:T(128)} %reduce.5.start_ref, bf16[4096,256]{1,0:T(8,128)(2,1)} %sort_land.1.refs_0_, bf16[4096,256]{1,0:T(8,128)(2,1)} %copy-done, bf16[4096,256]{1,0:T(8,128)(2,1)} %collective-permute-done.5.refs_2_, bf16[4096,256]{1,0:T(8,128)(2,1)} %pad_maximum_fusion.refs_3_, ...), custom_call_target="tpu_custom_call" | custom-call | tf_op jit(solution)/shard_map/mix_land/pallas_call | solution.py:258
  (69 shorter events, 6.9 us)
Async XLA Ops:
  12.9 33.6 %all-to-all-start = ((bf16[64,34,128]{2,1,0:T(8,128)(2,1)}), bf16[64,34,128]{2,1,0:T(8,128)(2,1)S(1)}, u32[]{:S(2)}, u32[]{:S(2)}) async-start(bf16[64,34,128]{2,1,0:T(8,128)(2,1)} %bucket_tiles.1), calls=%async_computation | async-start | bytes 1310720 | tf_op jit(solution)/shard_map/all_to_all | solution.py:347
  26.1 17.0 %copy-start.3 = (bf16[32,8,1024]{2,1,0:T(8,128)(2,1)S(1)}, bf16[32,8,1024]{2,1,0:T(8,128)(2,1)}, u32[]{:S(2)}) copy-start(bf16[32,8,1024]{2,1,0:T(8,128)(2,1)} %param.10) | copy-start | bytes 1572868
  26.1 18.1 %copy-start.6 = (s32[512]{0:T(512)S(1)}, s32[512]{0:T(512)}, u32[]{:S(2)}) copy-start(s32[512]{0:T(512)} %param.17) | copy-start | bytes 6148
  40.4 16.7 %copy-start.4 = (s32[1,4096]{1,0:T(1,128)S(1)}, s32[1,4096]{1,0:T(1,128)}, u32[]{:S(2)}) copy-start(s32[1,4096]{1,0:T(1,128)} %get-tuple-element.9.pos_ref) | copy-start | bytes 49156
  40.4 71.6 %collective-permute-start.4 = (bf16[4096,256]{1,0:T(8,128)(2,1)}, bf16[4096,256]{1,0:T(8,128)(2,1)S(1)}, u32[]{:S(2)}, u32[]{:S(2)}) collective-permute-start(bf16[4096,256]{1,0:T(8,128)(2,1)} %sort_land.1.refs_0_), channel_id=1, source_target_pairs={{0,1},{1,2},{2,3},{3,0},{4,5},{5,6},{6,7},{7,4},{8,9},{9,10},{10,1... | collective-permute-start | bytes 6291464 | tf_op jit(solution)/shard_map/ppermute | solution.py:39
  41.6 70.5 %collective-permute-start.5 = (bf16[4096,256]{1,0:T(8,128)(2,1)}, bf16[4096,256]{1,0:T(8,128)(2,1)}, u32[]{:S(2)}, u32[]{:S(2)}) collective-permute-start(bf16[4096,256]{1,0:T(8,128)(2,1)} %sort_land.1.refs_0_), channel_id=1, source_target_pairs={{0,3},{1,0},{2,1},{3,2},{4,7},{5,4},{6,5},{7,6},{8,11},{9,8},{10,9... | collective-permute-start | bytes 6291464 | tf_op jit(solution)/shard_map/ppermute | solution.py:39
  44.2 14.9 %copy-start.5 = (s32[64,1]{1,0:T(8,128)S(1)}, s32[64,1]{1,0:T(8,128)}, u32[]{:S(2)}) copy-start(s32[64,1]{1,0:T(8,128)} %get-tuple-element.11) | copy-start | bytes 772
  45.1 45.7 %copy-start.7 = (f32[512]{0:T(512)S(1)}, f32[512]{0:T(512)}, u32[]{:S(2)}) copy-start(f32[512]{0:T(512)} %param.16) | copy-start | bytes 6148
  45.1 45.7 %copy-start.8 = (f32[512]{0:T(512)S(1)}, f32[512]{0:T(512)}, u32[]{:S(2)}) copy-start(f32[512]{0:T(512)} %param.18) | copy-start | bytes 6148
  46.6 0.8 copy-start.1
  53.5 37.1 %all-to-all-start.1 = ((bf16[4,32,512]{2,1,0:T(8,128)(2,1)}), bf16[4,32,512]{2,1,0:T(8,128)(2,1)S(1)}, u32[]{:S(2)}, u32[]{:S(2)}) async-start(bf16[4,32,512]{2,1,0:T(8,128)(2,1)} %broadcast_in_dim.7), calls=%async_computation.1 | async-start | bytes 262144 | tf_op jit(solution)/shard_map/all_to_all | solution.py:312
  57.1 37.3 %copy-start.9 = (s32[1,4]{1,0:T(1,128)S(1)}, s32[1,4]{1,0:T(1,128)}, u32[]{:S(2)}) copy-start(s32[1,4]{1,0:T(1,128)} %param.19) | copy-start | bytes 52
  91.5 7.8 %collective-permute-start = (f32[129,128]{1,0:T(8,128)S(1)}, f32[129,128]{1,0:T(8,128)S(1)}, u32[]{:S(2)}, u32[]{:S(2)}) collective-permute-start(f32[129,128]{1,0:T(8,128)S(1)} %pad_maximum_fusion.1), channel_id=1, source_target_pairs={{0,4},{4,8},{8,12},{12,16},{16,20},{20,24},{24,28},{28,32},{32,36}... | collective-permute-start | bytes 198152 | tf_op jit(solution)/shard_map/ppermute | solution.py:39
  95.1 8.1 %collective-permute-start.1 = (f32[129,128]{1,0:T(8,128)S(1)}, f32[129,128]{1,0:T(8,128)S(1)}, u32[]{:S(2)}, u32[]{:S(2)}) collective-permute-start(f32[129,128]{1,0:T(8,128)S(1)} %pad_maximum_fusion.1), channel_id=1, source_target_pairs={{0,252},{4,0},{8,4},{12,8},{16,12},{20,16},{24,20},{28,24},{32,28}... | collective-permute-start | bytes 198152 | tf_op jit(solution)/shard_map/ppermute | solution.py:39
  95.1 9.3 %collective-permute-start.2 = (f32[129,128]{1,0:T(8,128)S(1)}, f32[129,128]{1,0:T(8,128)S(1)}, u32[]{:S(2)}, u32[]{:S(2)}) collective-permute-start(f32[129,128]{1,0:T(8,128)S(1)} %pad_maximum_fusion.1), channel_id=1, source_target_pairs={{0,32},{4,36},{8,40},{12,44},{16,48},{20,52},{24,56},{28,60},{32,6... | collective-permute-start | bytes 198152 | tf_op jit(solution)/shard_map/ppermute | solution.py:39
  99.3 8.6 %collective-permute-start.3 = (f32[129,128]{1,0:T(8,128)S(1)}, f32[129,128]{1,0:T(8,128)S(1)}, u32[]{:S(2)}, u32[]{:S(2)}) collective-permute-start(f32[129,128]{1,0:T(8,128)S(1)} %pad_maximum_fusion.1), channel_id=1, source_target_pairs={{0,224},{4,228},{8,232},{12,236},{16,240},{20,244},{24,248},{28,25... | collective-permute-start | bytes 198152 | tf_op jit(solution)/shard_map/ppermute | solution.py:39
  103.2 37.1 %collective-permute-start.6 = (bf16[256,1024]{1,0:T(8,128)(2,1)S(1)}, bf16[256,1024]{1,0:T(8,128)(2,1)S(1)}, u32[]{:S(2)}, u32[]{:S(2)}) collective-permute-start(bf16[256,1024]{1,0:T(8,128)(2,1)S(1)} %bitcast.119), channel_id=1, source_target_pairs={{0,1},{1,2},{2,3},{3,0},{4,5},{5,6},{6,7},{7,4},{8,9},{9,10},{10,1... | collective-permute-start | bytes 1572872 | tf_op jit(solution)/shard_map/ppermute | solution.py:39
  104.4 36.7 %collective-permute-start.8 = (bf16[256,1024]{1,0:T(8,128)(2,1)S(1)}, bf16[256,1024]{1,0:T(8,128)(2,1)}, u32[]{:S(2)}, u32[]{:S(2)}) collective-permute-start(bf16[256,1024]{1,0:T(8,128)(2,1)S(1)} %bitcast.120), channel_id=1, source_target_pairs={{0,2},{1,3},{2,0},{3,1},{4,6},{5,7},{6,4},{7,5},{8,10},{9,11},{10,... | collective-permute-start | bytes 1572872 | tf_op jit(solution)/shard_map/ppermute | solution.py:39
  107.9 35.0 %collective-permute-start.7 = (bf16[256,1024]{1,0:T(8,128)(2,1)S(1)}, bf16[256,1024]{1,0:T(8,128)(2,1)}, u32[]{:S(2)}, u32[]{:S(2)}) collective-permute-start(bf16[256,1024]{1,0:T(8,128)(2,1)S(1)} %bitcast.121), channel_id=1, source_target_pairs={{0,3},{1,0},{2,1},{3,2},{4,7},{5,4},{6,5},{7,6},{8,11},{9,8},{10,9... | collective-permute-start | bytes 1572872 | tf_op jit(solution)/shard_map/ppermute | solution.py:39
  112.1 10.7 %copy-start = (bf16[4096,256]{1,0:T(8,128)(2,1)}, bf16[4096,256]{1,0:T(8,128)(2,1)S(1)}, u32[]{:S(2)}) copy-start(bf16[4096,256]{1,0:T(8,128)(2,1)S(1)} %collective-permute-done.4.refs_1_) | copy-start | bytes 6291460
  122.7 27.3 %collective-permute-start.10 = (bf16[2048,256]{1,0:T(8,128)(2,1)}, bf16[2048,256]{1,0:T(8,128)(2,1)}, u32[]{:S(2)}, u32[]{:S(2)}) collective-permute-start(bf16[2048,256]{1,0:T(8,128)(2,1)} %slice.23), channel_id=1, source_target_pairs={{0,3},{1,0},{2,1},{3,2},{4,7},{5,4},{6,5},{7,6},{8,11},{9,8},{10,9... | collective-permute-start | bytes 3145736 | tf_op jit(solution)/shard_map/ppermute | solution.py:39
  123.9 26.1 %collective-permute-start.9 = (bf16[2048,256]{1,0:T(8,128)(2,1)}, bf16[2048,256]{1,0:T(8,128)(2,1)}, u32[]{:S(2)}, u32[]{:S(2)}) collective-permute-start(bf16[2048,256]{1,0:T(8,128)(2,1)} %slice.22), channel_id=1, source_target_pairs={{0,1},{1,2},{2,3},{3,0},{4,5},{5,6},{6,7},{7,4},{8,9},{9,10},{10,1... | collective-permute-start | bytes 3145736 | tf_op jit(solution)/shard_map/ppermute | solution.py:39
  127.3 29.4 %all-to-all-start.2 = ((bf16[64,32,128]{2,1,0:T(8,128)(2,1)}), bf16[64,32,128]{2,1,0:T(8,128)(2,1)S(1)}, u32[]{:S(2)}, u32[]{:S(2)}) async-start(bf16[64,32,128]{2,1,0:T(8,128)(2,1)} %broadcast_in_dim.10), calls=%async_computation.2 | async-start | bytes 1048576 | tf_op jit(solution)/shard_map/all_to_all | solution.py:312
  156.7 0.8 copy-start.2
where the time goes:
time: 197 us; the launch traced here: 196 us
  Pallas kernels  65.9 us (33%)
  starting transfers between devices  47.6 us (24%)
  waiting for transfers between devices  40.9 us (21%)
  local copies, waits for them, and re-layouts  16 us (8%)
  matrix products  13.5 us (7%)
  other arithmetic  10.3 us (5%)
    pallas_call x1, Pallas kernels, mix_land(): pl.pallas_call(kernel, grid=(tiles // block,), out_shape=jax.ShapeDtypeSt...  38.3 us
    all_to_all x2, waiting for transfers between devices, to_all(): return lax.all_to_all(copies, axis, split_axis=0, concat_axis=0, tiled=True)  34.5 us
    ppermute x11, starting transfers between devices, shifted(): return lax.ppermute(value, axis, pairs)  18.8 us
    all_to_all x2, starting transfers between devices, to_all(): return lax.all_to_all(copies, axis, split_axis=0, concat_axis=0, tiled=True)  15.7 us
    pallas_call x1, Pallas kernels, sort_land(): pl.pallas_call(kernel, grid=(tiles // block,), out_shape=jax.ShapeDtypeSt...  14.3 us
    all_to_all x1, starting transfers between devices, shards(): lax.all_to_all(packed, 'patch', split_axis=0, concat_axis=0, tiled=True)  13.1 us
    ppermute x11, waiting for transfers between devices, shifted(): return lax.ppermute(value, axis, pairs)  6.38 us
    pallas_call x1, Pallas kernels, bucket_tiles(): pl.pallas_call(kernel, grid=(steps,), out_shape=jax.ShapeDtypeStruct((npa...  6.16 us
  transfers between devices with their start and end apart: 14, of which 5 were waited for; matrix products, arithmetic and copies ran while one was open for 17% of the time, Pallas kernels for 10%

commit v1 on v0

v1 whole, which is shorter than its diff:
```python
import math

import jax
import jax.numpy as jnp
from jax import lax
from jax.experimental import pallas as pl
from jax.experimental.pallas import tpu as pltpu
from jax.sharding import PartitionSpec as P

SWEEPS = 10
PRECISE = lax.Precision.HIGHEST
BF = jnp.bfloat16
F32 = jnp.float32
I32 = jnp.int32

NN = (((1,), (0,)), ((), ()))
NT = (((1,), (1,)), ((), ()))


def dot(a, b, dims=NN):
    return lax.dot_general(a, b, dims, preferred_element_type=F32)


def iota(shape, axis):
    return lax.broadcasted_iota(I32, shape, axis)


VMEM = pl.BlockSpec(memory_space=pltpu.VMEM)
SMEM = pl.BlockSpec(memory_space=pltpu.SMEM)


def params(mib):
    return pltpu.CompilerParams(vmem_limit_bytes=mib * 1024 * 1024)


def shifted(value, axis, steps):
    count = lax.axis_size(axis)
    pairs = [(source, (source + steps) % count) for source in range(count)]
    return lax.ppermute(value, axis, pairs)


PARTS = 4
UNROLL = 4


def order_tiles(owners, npatch):
    tiles = owners.shape[1]
    block = 512
    per_part = tiles // PARTS // block

    def kernel(owner_ref, rank_ref, pos_ref, start_ref):
        before = (iota((block, block), 0) < iota((block, block), 1)).astype(BF)
        lower = (iota((npatch, npatch), 0) > iota((npatch, npatch), 1)).astype(BF)
        done = jnp.zeros((npatch, 1), F32)
        for part in range(PARTS):
            carry = jnp.zeros((npatch, 1), F32)
            held = []
            for c in range(per_part):
                at = (part * per_part + c) * block
                hot = owner_ref[:, at : at + block] == iota((npatch, block), 0)
                ahead = dot(hot.astype(BF), before) + carry
                hot = hot.astype(F32)
                carry = carry + jnp.sum(hot, axis=1, keepdims=True)
                held.append((at, hot, ahead))
            starts = dot(lower, jnp.broadcast_to(carry, (npatch, 128)).astype(BF))[:, :1]
            start_ref[:, part : part + 1] = starts.astype(I32)
            for at, hot, ahead in held:
                rank = jnp.sum(hot * (ahead + done), axis=0, keepdims=True)
                pos = jnp.sum(hot * (ahead + starts), axis=0, keepdims=True)
                rank_ref[:, at : at + block] = rank.astype(I32)
                pos_ref[:, at : at + block] = pos.astype(I32)
            done = done + carry
        start_ref[:, PARTS:] = jnp.zeros((npatch, PARTS), I32)

    return pl.pallas_call(
        kernel,
        out_shape=(
            jax.ShapeDtypeStruct((1, tiles), I32),
            jax.ShapeDtypeStruct((1, tiles), I32),
            jax.ShapeDtypeStruct((npatch, 2 * PARTS), I32),
        ),
        in_specs=[VMEM],
        out_specs=(VMEM, VMEM, VMEM),
        compiler_params=params(60),
        name="order_tiles",
    )(owners)


def bucket_tiles(land_rows, levels, weight, mask, owners, ranks, columns, npatch, bucket):
    width, tiles = land_rows.shape
    rows = width // levels
    low = 4
    high = npatch // low
    block = 1024
    steps = tiles // block

    def kernel(
        x_ref, weight_ref, mask_ref, owner_ref, rank_ref, col_ref, out_ref, acc_ref, cacc_ref
    ):
        step = pl.program_id(0)
        owner = owner_ref[...]
        slot = (owner & (low - 1)) * bucket + rank_ref[...]
        hot = (iota((low * bucket, block), 0) == slot).astype(F32).astype(BF)
        group = owner >> 2
        surface = (iota((rows, width), 0) * levels == iota((rows, width), 1)).astype(F32)
        keep = weight_ref[...].astype(F32) * mask_ref[...].astype(F32)
        value = (dot(surface.astype(BF), x_ref[...]) * keep).astype(BF)
        zero = jnp.zeros_like(value)
        picked = jnp.concatenate(
            [jnp.where(group == g, value, zero) for g in range(high)], axis=0
        )
        part = dot(picked, hot, NT)
        col = col_ref[...]
        half = iota((2 * high, block), 0)
        digit = jnp.where((half & 1) == 0, col >> 5, col & 31)
        digits = jnp.where((half >> 1) == group, digit, 0).astype(F32).astype(BF)
        cpart = dot(digits, hot, NT)

        @pl.when(step == 0)
        def _():
            acc_ref[...] = part
            cacc_ref[...] = cpart

        @pl.when(step > 0)
        def _():
            acc_ref[...] += part
            cacc_ref[...] += cpart

        @pl.when(step == steps - 1)
        def _():
            for o in range(npatch):
                g, b = o // low, o % low
                cut = slice(b * bucket, (b + 1) * bucket)
                out_ref[o, :rows, :] = acc_ref[g * rows : (g + 1) * rows, cut].astype(BF)
                out_ref[o, rows : rows + 2, :] = cacc_ref[2 * g : 2 * g + 2, cut].astype(BF)

    lane = pl.BlockSpec((1, block), lambda i: (0, i))
    return pl.pallas_call(
        kernel,
        grid=(steps,),
        out_shape=jax.ShapeDtypeStruct((npatch, rows + 2, bucket), BF),
        in_specs=[pl.BlockSpec((width, block), lambda i: (0, i))] + [lane] * 5,
        out_specs=pl.BlockSpec((npatch, rows + 2, bucket), lambda i: (0, 0, 0)),
        scratch_shapes=[
            pltpu.VMEM((high * rows, low * bucket), F32),
            pltpu.VMEM((2 * high, low * bucket), F32),
        ],
        compiler_params=params(60),
        name="bucket_tiles",
    )(land_rows, weight, mask, owners, ranks, columns)


def lane_swap(rows, a, b):
    source = iota((rows, rows), 0)
    target = iota((rows, rows), 1)
    return ((source % b) * a + source // b == target).astype(F32).astype(BF)


def sort_land(pos, land_rows, levels, first):
    width, tiles = land_rows.shape
    span = tiles // PARTS
    block = 512

    def kernel(pos_ref, x_ref, low_ref, high_ref):
        swap = lane_swap(width, width // levels, levels)
        for c in range(tiles // block):
            part = c * block // span
            cut = slice(part * span, (part + 1) * span)
            place = iota((block, span), 0) + (c * block - part * span)
            hot = (place == pos_ref[:, cut]).astype(F32).astype(BF)
            moved = dot(hot, x_ref[:, cut], NT).astype(BF)
            value = dot(moved, swap).astype(BF)
            at = c * block
            if at < first:
                low_ref[at : at + block, :] = value
            else:
                high_ref[at - first : at - first + block, :] = value

    return pl.pallas_call(
        kernel,
        out_shape=(
            jax.ShapeDtypeStruct((first, width), BF),
            jax.ShapeDtypeStruct((tiles - first, width), BF),
        ),
        in_specs=[VMEM, VMEM],
        out_specs=(VMEM, VMEM),
        compiler_params=params(60),
        name="sort_land",
    )(pos, land_rows)


def screen_forecast(received, base_rows, levels, obs_column):
    npatch, rows2, _ = received.shape
    rows = rows2 - 2
    nobs = obs_column.shape[0]
    width, columns = base_rows.shape
    group = 8

    def kernel(in_ref, base_ref, obs_ref, out_ref):
        obs = obs_ref[...]
        place = iota((nobs, columns), 1)
        surface = (iota((rows, width), 0) * levels == iota((rows, width), 1)).astype(F32)
        base = dot(surface.astype(BF), base_ref[...]).astype(BF)
        acc = dot(base, (obs == place).astype(F32).astype(BF), NT)
        for g in range(npatch // group):
            values = jnp.concatenate(
                [in_ref[g * group + i, :rows, :] for i in range(group)], axis=1
            )
            digits = jnp.concatenate(
                [in_ref[g * group + i, rows:, :] for i in range(group)], axis=1
            ).astype(F32)
            col = (digits[0:1] * 32.0 + digits[1:2]).astype(I32)
            acc = acc + dot(values, (obs == col).astype(F32).astype(BF), NT)
        out_ref[...] = acc.astype(BF)

    return pl.pallas_call(
        kernel,
        out_shape=jax.ShapeDtypeStruct((rows, nobs), BF),
        in_specs=[VMEM, VMEM, VMEM],
        out_specs=VMEM,
        compiler_params=params(60),
        name="screen_forecast",
    )(received, base_rows, obs_column)


def mix_land(pieces, sources, starts, mixes, pos_col, land_rows, mask_row, levels):
    slots = len(pieces)
    flat = [piece for group in pieces for piece in group]
    places = [
        (s, sum(p.shape[0] for p in group[:i]))
        for s, group in enumerate(pieces)
        for i in range(len(group))
    ]
    width, tiles = land_rows.shape
    local = width // levels
    npatch = mixes.shape[0]
    members = mixes.shape[2]
    span = tiles // PARTS
    window = 48
    lanes = 128
    count = len(flat)

    def kernel(src_ref, start_ref, *refs):
        piece_refs = refs[:count]
        mix_ref, pos_ref, land_ref, mask_ref, out_ref = refs[count : count + 5]
        state_ref, tiled_ref, y_ref, sems = refs[count + 5 :]
        step = pl.program_id(0)

        @pl.when(step == 0)
        def _():
            copies = [
                pltpu.make_async_copy(
                    piece_refs[i],
                    state_ref.at[s, pl.ds(at, piece_refs[i].shape[0]), :],
                    sems.at[i],
                )
                for i, (s, at) in enumerate(places)
            ]
            for copy in copies:
                copy.start()
            for s in range(slots):
                spread = (
                    iota((members, lanes), 0)
                    == (iota((members, lanes), 1) & (local - 1)) + src_ref[s] * local
                )
                tiled_ref[:, s * lanes : (s + 1) * lanes] = dot(
                    mix_ref[...], spread.astype(F32).astype(BF)
                ).astype(BF)
            lane_level = iota((local, lanes), 1) // local
            y_ref[...] = jnp.zeros_like(y_ref)
            for copy in copies:
                copy.wait()

            def weight_of(o, s):
                at = pl.multiple_of(o * local, local)
                parts = []
                for t in (s, s + 1):
                    small = tiled_ref[pl.ds(at, local), t * lanes : (t + 1) * lanes]
                    zero = jnp.zeros_like(small)
                    parts += [
                        jnp.where(lane_level == l, small, zero) for l in range(lanes // local)
                    ]
                return jnp.concatenate(parts, axis=0)

            def mixed(o, cuts):
                acc = None
                for s in range(0, slots, 2):
                    rows = [
                        jnp.concatenate(
                            [
                                state_ref[t, pl.ds(at, window), h * lanes : (h + 1) * lanes]
                                for t in (s, s + 1)
                            ],
                            axis=1,
                        )
                        for h in range(width // lanes)
                        for at in cuts
                    ]
                    part = dot(jnp.concatenate(rows, axis=0), weight_of(o, s))
                    acc = part if acc is None else acc + part
                half = len(cuts) * window
                return jnp.concatenate(
                    [acc[h * half : (h + 1) * half] for h in range(width // lanes)], axis=1
                ).astype(BF)

            def put(part, base, first, end, value):
                at = pl.multiple_of(part * span + base, 16)
                row = iota((window, width), 0) + base
                keep = row >= first
                if end is not None:
                    keep = jnp.logical_and(keep, row < end)
                old = y_ref[pl.ds(at, window), :]
                y_ref[pl.ds(at, window), :] = jnp.where(keep, value, old)

            def begin(first):
                return pl.multiple_of(jnp.minimum((first // 16) * 16, span - window), 16)

            def bounds(o):
                firsts = [start_ref[o, q] for q in range(PARTS)]
                after = jnp.minimum(o + 1, npatch - 1)
                ends = [
                    jnp.where(o == npatch - 1, span, start_ref[after, q]) for q in range(PARTS)
                ]
                return firsts, ends, [begin(first) for first in firsts]

            def owners(i, unused):
                group = [i * UNROLL + u for u in range(UNROLL)]
                limits = [bounds(o) for o in group]
                values = [
                    mixed(o, [pl.multiple_of(q * span + bases[q], 16) for q in range(PARTS)])
                    for o, (firsts, ends, bases) in zip(group, limits)
                ]
                for value, (firsts, ends, bases) in zip(values, limits):
                    for q in range(PARTS):
                        put(q, bases[q], firsts[q], None, value[q * window : (q + 1) * window])
                most = 0
                for firsts, ends, bases in limits:
                    for q in range(PARTS):
                        most = jnp.maximum(most, ends[q] - bases[q] - window)

                @pl.when(most > 0)
                def _():
                    for o, (firsts, ends, bases) in zip(group, limits):
                        for q in range(PARTS):

                            def more(n, unused, o=o, q=q, first=firsts[q], end=ends[q], low=bases[q]):
                                base = begin(low + (n + 1) * window)
                                at = pl.multiple_of(q * span + base, 16)
                                put(q, base, first, end, mixed(o, [at]))
                                return unused

                            lack = jnp.maximum(ends[q] - bases[q] - window, 0)
                            lax.fori_loop(0, (lack + window - 1) // window, more, 0)

                return unused

            lax.fori_loop(0, npatch // UNROLL, owners, 0)

        hot = (iota((span, span), 1) == pos_ref[...]).astype(F32).astype(BF)
        rows = y_ref[pl.ds(pl.multiple_of(step * span, span), span), :]
        rows = dot(rows, lane_swap(width, levels, local)).astype(BF)
        back = dot(hot, rows)
        out_ref[...] = jnp.where(mask_ref[...] == 1, back.T.astype(BF), land_ref[...])

    return pl.pallas_call(
        kernel,
        grid=(PARTS,),
        out_shape=jax.ShapeDtypeStruct((width, tiles), BF),
        in_specs=[SMEM, SMEM]
        + [pl.BlockSpec(memory_space=pl.ANY)] * count
        + [
            VMEM,
            pl.BlockSpec((span, 1), lambda i: (i, 0)),
            pl.BlockSpec((width, span), lambda i: (0, i)),
            pl.BlockSpec((1, span), lambda i: (0, i)),
        ],
        out_specs=pl.BlockSpec((width, span), lambda i: (0, i)),
        scratch_shapes=[
            pltpu.VMEM((slots, tiles, width), BF),
            pltpu.VMEM((npatch * local, slots * lanes), BF),
            pltpu.VMEM((tiles, width), BF),
            pltpu.SemaphoreType.DMA((count,)),
        ],
        compiler_params=params(60),
        name="mix_land",
    )(
        sources,
        starts,
        *flat,
        mixes.reshape(npatch * local, members),
        pos_col,
        land_rows,
        mask_row,
    )


def settle(local_gram, local_proj):
    members = local_gram.shape[0]
    identity = jnp.eye(members, dtype=jnp.float32)
    system = local_gram + (members - 1.0) * identity
    trace_scale = jnp.trace(system)
    upper_iter = system / trace_scale
    lower_iter = identity
    for _ in range(SWEEPS):
        middle_step = 0.5 * (3.0 * identity - jnp.dot(lower_iter, upper_iter, precision=PRECISE))
        upper_iter = jnp.dot(upper_iter, middle_step, precision=PRECISE)
        lower_iter = jnp.dot(middle_step, lower_iter, precision=PRECISE)
    inv_root = lower_iter / jnp.sqrt(trace_scale)
    mean_shift = jnp.dot(
        inv_root, jnp.dot(inv_root, local_proj, precision=PRECISE), precision=PRECISE
    )
    spread = mean_shift[:, None] + math.sqrt(members - 1.0) * inv_root
    centered = spread - jnp.mean(spread, axis=0, keepdims=True)
    return (centered + 1.0 / members).astype(jnp.bfloat16)


def to_all(value, axis):
    count = lax.axis_size(axis)
    copies = jnp.broadcast_to(value[None], (count,) + value.shape)
    return lax.all_to_all(copies, axis, split_axis=0, concat_axis=0, tiled=True)


def analysis(
    atmos,
    land,
    land_mask,
    tile_owner,
    tile_column,
    tile_weight,
    obs_value,
    observation_column,
    obs_error,
    loc_blocks,
):
    barrier = lax.optimization_barrier
    npatch = lax.axis_size("patch")
    mem_count = lax.axis_size("mem")
    local, levels, columns = atmos.shape
    layers, tiles = (land.shape[1], land.shape[2])
    members = local * mem_count
    bucket = 2 * tiles // npatch
    row_width = max(2, npatch // 8)
    first = 3 * tiles // 8
    mem_rank = lax.axis_index("mem")
    patch_rank = lax.axis_index("patch")

    atmos_rows = atmos.reshape(local * levels, columns)
    atmos_parts = [shifted(atmos_rows, "mem", s) for s in (1, -1, 2)]

    owners = tile_owner.reshape(1, tiles)
    land_rows = land.reshape(local * layers, tiles)
    mask_row = land_mask.reshape(1, tiles)
    ranks, pos, starts = order_tiles(owners, npatch)
    packed = bucket_tiles(
        land_rows,
        layers,
        tile_weight.reshape(1, tiles),
        mask_row,
        owners,
        ranks,
        tile_column.reshape(1, tiles),
        npatch,
        bucket,
    )
    received = lax.all_to_all(packed, "patch", split_axis=0, concat_axis=0, tiled=True)

    low, high = sort_land(pos, land_rows, layers, first)
    low_prev = shifted(low, "mem", 1)
    low_next = shifted(low, "mem", -1)

    forecast = screen_forecast(received, atmos_rows, levels, observation_column.reshape(-1, 1))
    forecast, low_prev, low_next = barrier((forecast, low_prev, low_next))
    ensemble = to_all(forecast, "mem")
    ensemble, high, low_prev, low_next = barrier((ensemble, high, low_prev, low_next))
    high_prev = shifted(high, "mem", 1)
    high_next = shifted(high, "mem", -1)
    low_far = [
        shifted(low_prev[: first // 2], "mem", 1), shifted(low_next[first // 2 :], "mem", -1)
    ]

    ensemble = ensemble.reshape(members, -1).astype(F32)
    center = jnp.mean(ensemble, axis=0)
    inverse_sd = lax.rsqrt(obs_error)
    scaled = (ensemble - center[None, :]) * inverse_sd[None, :]
    innovation = (obs_value - center) * inverse_sd
    gram_own = jnp.dot(scaled, scaled.T, precision=PRECISE)
    proj_own = jnp.dot(scaled, innovation, precision=PRECISE)
    own_stats = jnp.concatenate([gram_own, proj_own[None, :]], axis=0)
    listed = loc_blocks[0]
    local_stats = own_stats
    for offset in (1, -1, row_width, -row_width):
        near_stats = shifted(own_stats, "patch", offset)
        source = (patch_rank - offset) % npatch
        used = jnp.sum((listed == source).astype(jnp.float32))
        local_stats = local_stats + used * near_stats
    mix = settle(local_stats[:members], local_stats[members])

    own_cols = lax.dynamic_slice_in_dim(mix.T, mem_rank * local, local, 0)
    blocks = own_cols.reshape(local, mem_count, local).transpose(2, 1, 0).reshape(local, members)
    all_mixes = to_all(blocks, "patch")
    own_cols, high_prev, high_next = barrier((own_cols, high_prev, high_next))
    split = high.shape[0] // 2
    high_far = [shifted(high_prev[:split], "mem", 1), shifted(high_next[split:], "mem", -1)]

    slot_source = [mem_rank, mem_rank - 1, mem_rank + 1, mem_rank - 2]
    sources = jnp.stack([s % mem_count for s in slot_source]).astype(I32)
    atmos_out = 0.0
    for part, source in zip([atmos_rows] + atmos_parts, slot_source):
        rows = lax.dynamic_slice_in_dim(own_cols, (source % mem_count) * local, local, 1)
        atmos_out = atmos_out + jnp.einsum(
            "jk,klc->jlc", rows, part.reshape(local, levels, columns), preferred_element_type=F32
        )
    atmos_analysis = atmos_out.astype(BF)

    land_out = mix_land(
        [[low, high], [low_prev, high_prev], [low_next, high_next], low_far + high_far],
        sources,
        starts,
        all_mixes,
        pos.reshape(tiles, 1),
        land_rows,
        mask_row,
        layers,
    )
    return (atmos_analysis, land_out.reshape(local, layers, tiles))


def solution(mesh):
    in_specs = (
        P("mem", None, "patch"),
        P("mem", None, "patch"),
        P("patch"),
        P("patch", None),
        P("patch"),
        P("patch"),
        P("patch"),
        P("patch"),
        P("patch"),
        P("patch", None),
    )
    out_specs = (P("mem", None, "patch"), P("mem", None, "patch"))
    return jax.shard_map(
        analysis, mesh=mesh, in_specs=in_specs, out_specs=out_specs, check_vma=False
    )
```

time: 197 us -> 186 us (0.944)
  Pallas kernels: 65.9 us -> 45.7 us
  waiting for transfers between devices: 40.9 us -> 54.9 us
  other arithmetic: 10.3 us -> 4.88 us
  local copies, waits for them, and re-layouts: 16 us -> 13.2 us
  matrix products: 13.5 us -> 15.5 us
    ppermute x11 -> x15, waiting for transfers between devices: 6.38 us -> 40.9 us  [shifted(): return lax.ppermute(value, axis, pairs)]
    all_to_all x2, waiting for transfers between devices: 34.5 us -> 7.56 us  [to_all(): return lax.all_to_all(copies, axis, split_axis=0, concat_axis=0, tiled=True)]
    pallas_call x2, Pallas kernels: 52.7 us -> 31.7 us  [the longest x1 23.7 us: mix_land(): pl.pallas_call(kernel, grid=(PARTS,), out_shape=jax.ShapeDtypeStruct((wid...]
    all_to_all x1, waiting for transfers between devices: 0.01 us -> 6.5 us  [analysis(): lax.all_to_all(packed, 'patch', split_axis=0, concat_axis=0, tiled=True)]
    concatenate x2 -> x1, other arithmetic: 3.04 us -> 0.06 us  [analysis(): own_stats = jnp.concatenate([gram_own, proj_own[None, :]], axis=0)]
    slice x3 -> x4, local copies, waits for them, and re-layouts: 5.44 us -> 2.59 us  [the longest x1 0.93 us: analysis(): high_prev[:split]]
    dot_general x6, matrix products: 5.89 us -> 7.9 us  [the longest x4 7.26 us: analysis(): jnp.einsum('jk,klc->jlc', rows, part.reshape(local, levels, columns), pre...]
    reshape x2 -> x5, local copies, waits for them, and re-layouts: 2.83 us -> 4.36 us  [the longest x1 1.99 us: analysis(): pos.reshape(tiles, 1)]
  transfers between devices with their start and end apart: 14 -> 18, of which waited for: 5 -> 7; matrix products, arithmetic and copies ran while one was open for 17% -> 16% of each run, Pallas kernels for 10% -> 7%
where the time goes in v1:
time: 186 us; the launch traced here: 185 us
  waiting for transfers between devices  54.9 us (30%)
  starting transfers between devices  49.1 us (26%)
  Pallas kernels  45.7 us (25%)
  matrix products  15.5 us (8%)
  local copies, waits for them, and re-layouts  13.2 us (7%)
  other arithmetic  4.88 us (3%)
  between operations  1.96 us (1%)
    ppermute x15, waiting for transfers between devices, shifted(): return lax.ppermute(value, axis, pairs)  40.9 us
    pallas_call x1, Pallas kernels, mix_land(): pl.pallas_call(kernel, grid=(PARTS,), out_shape=jax.ShapeDtypeStruct((wid...  23.7 us
    ppermute x15, starting transfers between devices, shifted(): return lax.ppermute(value, axis, pairs)  20.3 us
    all_to_all x2, starting transfers between devices, to_all(): return lax.all_to_all(copies, axis, split_axis=0, concat_axis=0, tiled=True)  15.5 us
    all_to_all x1, starting transfers between devices, analysis(): lax.all_to_all(packed, 'patch', split_axis=0, concat_axis=0, tiled=True)  13.3 us
    pallas_call x1, Pallas kernels, sort_land(): pl.pallas_call(kernel, out_shape=(jax.ShapeDtypeStruct((first, width), BF...  8.05 us
    all_to_all x2, waiting for transfers between devices, to_all(): return lax.all_to_all(copies, axis, split_axis=0, concat_axis=0, tiled=True)  7.56 us
    dot_general x4, matrix products, analysis(): jnp.einsum('jk,klc->jlc', rows, part.reshape(local, levels, columns), pre...  7.26 us
  transfers between devices with their start and end apart: 18, of which 7 were waited for; matrix products, arithmetic and copies ran while one was open for 16% of the time, Pallas kernels for 7%

profile of v1, /device:TPU:1, one launch (start us, length us, event | category | flops | bytes accessed | tf_op | source)
XLA Modules:
  0.0 185.3 jit_solution(11264036144649419412)
XLA Ops:
  0.6 2.3 %order_tiles.1 = (s32[1,4096]{1,0:T(1,128)}, s32[1,4096]{1,0:T(1,128)}, s32[64,8]{1,0:T(8,128)}) custom-call(s32[1,4096]{1,0:T(1,128)} %bitcast.116), custom_call_target="tpu_custom_call" | custom-call | tf_op jit(solution)/shard_map/order_tiles/pallas_call | solution.py:75
  3.0 1.3 reshape.94.weight_ref
  4.3 6.8 %bucket_tiles.1 = bf16[64,34,128]{2,1,0:T(8,128)(2,1)} custom-call(bf16[256,4096]{1,0:T(8,128)(2,1)} %bitcast.108, bf16[1,4096]{1,0:T(2,128)(2,1)} %reshape.94.weight_ref, s32[1,4096]{1,0:T(1,128)} %bitcast.118, s32[1,4096]{1,0:T(1,128)} %bitcast.117, s32[1,4096]{1,0:T(1,128)} %get-tuple-element.17.rank_ref, s32[1,4096]{1,0:T(1,128)} %bitcast.120), custom_call_target="tpu_custom_call" | custom-call | tf_op jit(solution)/shard_map/bucket_tiles/pallas_call | solution.py:138
  11.1 13.3 %all-to-all-start = ((bf16[64,34,128]{2,1,0:T(8,128)(2,1)}), bf16[64,34,128]{2,1,0:T(8,128)(2,1)S(1)}, u32[]{:S(2)}, u32[]{:S(2)}) async-start(bf16[64,34,128]{2,1,0:T(8,128)(2,1)} %bucket_tiles.1), calls=%async_computation | async-start | bytes 1310720 | tf_op jit(solution)/shard_map/all_to_all | solution.py:465
  24.4 8.1 %sort_land.1 = (bf16[1536,256]{1,0:T(8,128)(2,1)}, bf16[2560,256]{1,0:T(8,128)(2,1)}) custom-call(s32[1,4096]{1,0:T(1,128)} %get-tuple-element.18.pos_ref, bf16[256,4096]{1,0:T(8,128)(2,1)} %bitcast.109), custom_call_target="tpu_custom_call" | custom-call | tf_op jit(solution)/shard_map/sort_land/pallas_call | solution.py:179
  32.4 1.2 collective-permute-start
  33.6 1.5 collective-permute-start.1
  35.1 0.9 copy.25.obs_ref
  36.0 2.0 %copy.31.refs_11_ = s32[4096,1]{1,0:T(8,128)} copy(s32[4096,1]{0,1:T(1,128)S(1)} %bitcast.115) | data formatting | bytes 32768 | tf_op jit(solution)/shard_map/reshape | solution.py:520
  38.0 6.5 %all-to-all-done.in_ref = bf16[64,34,128]{2,1,0:T(8,128)(2,1)S(1)} async-done(((bf16[64,34,128]{2,1,0:T(8,128)(2,1)}), bf16[64,34,128]{2,1,0:T(8,128)(2,1)S(1)}, u32[]{:S(2)}, u32[]{:S(2)}) %all-to-all-start) | async-done | bytes 557088 | tf_op jit(solution)/shard_map/all_to_all | solution.py:465
  44.5 0.8 copy-done.2
  45.3 4.8 %screen_forecast.1 = bf16[32,512]{1,0:T(8,128)(2,1)} custom-call(bf16[64,34,128]{2,1,0:T(8,128)(2,1)} %copy-done.2, bf16[256,1024]{1,0:T(8,128)(2,1)} %bitcast.4.base_ref, s32[512,1]{1,0:T(8,128)} %copy.25.obs_ref), custom_call_target="tpu_custom_call" | custom-call | tf_op jit(solution)/shard_map/screen_forecast/pallas_call | solution.py:216
  50.2 2.3 %collective-permute-done.refs_2_ = bf16[1536,256]{1,0:T(8,128)(2,1)S(1)} collective-permute-done((bf16[1536,256]{1,0:T(8,128)(2,1)}, bf16[1536,256]{1,0:T(8,128)(2,1)S(1)}, u32[]{:S(2)}, u32[]{:S(2)}) %collective-permute-start) | collective-permute-done | bytes 786464 | tf_op jit(solution)/shard_map/ppermute | solution.py:39
  52.5 1.4 broadcast_in_dim.10
  53.9 3.6 %all-to-all-start.1 = ((bf16[4,32,512]{2,1,0:T(8,128)(2,1)}), bf16[4,32,512]{2,1,0:T(8,128)(2,1)S(1)}, u32[]{:S(2)}, u32[]{:S(2)}) async-start(bf16[4,32,512]{2,1,0:T(8,128)(2,1)} %broadcast_in_dim.10), calls=%async_computation.1 | async-start | bytes 262144 | tf_op jit(solution)/shard_map/all_to_all | solution.py:420
  57.6 0.7 fusion.39
  58.3 7.6 %all-to-all-done.1 = bf16[4,32,512]{2,1,0:T(8,128)(2,1)S(1)} async-done(((bf16[4,32,512]{2,1,0:T(8,128)(2,1)}), bf16[4,32,512]{2,1,0:T(8,128)(2,1)S(1)}, u32[]{:S(2)}, u32[]{:S(2)}) %all-to-all-start.1) | async-done | bytes 131104 | tf_op jit(solution)/shard_map/all_to_all | solution.py:420
  66.7 3.1 %collective-permute-start.2 = (f32[129,128]{1,0:T(8,128)S(1)}, f32[129,128]{1,0:T(8,128)S(1)}, u32[]{:S(2)}, u32[]{:S(2)}) collective-permute-start(f32[129,128]{1,0:T(8,128)S(1)} %pad_maximum_fusion), channel_id=1, source_target_pairs={{0,4},{4,8},{8,12},{12,16},{16,20},{20,24},{24,28},{28,32},{32,36}... | collective-permute-start | bytes 198152 | tf_op jit(solution)/shard_map/ppermute | solution.py:39
  69.8 4.2 %collective-permute-start.4 = (f32[129,128]{1,0:T(8,128)S(1)}, f32[129,128]{1,0:T(8,128)S(1)}, u32[]{:S(2)}, u32[]{:S(2)}) collective-permute-start(f32[129,128]{1,0:T(8,128)S(1)} %pad_maximum_fusion), channel_id=1, source_target_pairs={{0,32},{4,36},{8,40},{12,44},{16,48},{20,52},{24,56},{28,60},{32,6... | collective-permute-start | bytes 198152 | tf_op jit(solution)/shard_map/ppermute | solution.py:39
  74.0 3.3 %collective-permute-start.5 = (f32[129,128]{1,0:T(8,128)S(1)}, f32[129,128]{1,0:T(8,128)S(1)}, u32[]{:S(2)}, u32[]{:S(2)}) collective-permute-start(f32[129,128]{1,0:T(8,128)S(1)} %pad_maximum_fusion), channel_id=1, source_target_pairs={{0,224},{4,228},{8,232},{12,236},{16,240},{20,244},{24,248},{28,25... | collective-permute-start | bytes 198152 | tf_op jit(solution)/shard_map/ppermute | solution.py:39
  77.3 0.7 pad_add_fusion.src_ref
  77.9 0.8 slice.20
  78.7 0.6 collective-permute-start.10
  79.4 0.5 collective-permute-start.9
  79.9 1.0 collective-permute-start.6
  80.9 1.9 %collective-permute-done.5 = f32[129,128]{1,0:T(8,128)S(1)} collective-permute-done((f32[129,128]{1,0:T(8,128)S(1)}, f32[129,128]{1,0:T(8,128)S(1)}, u32[]{:S(2)}, u32[]{:S(2)}) %collective-permute-start.5) | collective-permute-done | bytes 66080 | tf_op jit(solution)/shard_map/ppermute | solution.py:39
  82.8 2.5 %multiply_add_fusion = f32[129,128]{1,0:T(8,128)S(1)} fusion(f32[129,128]{1,0:T(8,128)S(1)} %collective-permute-done.5, f32[129,128]{1,0:T(8,128)S(1)} %collective-permute-done.4, f32[129,128]{1,0:T(8,128)S(1)} %collective-permute-done.3, f32[129,128]{1,0:T(8,128)S(1)} %collective-permute-done.2, f32[]{:T(128)} %get-tuple-element.40, f32[]{:T(128)} %get-tuple-element.41, ...), kind=kLoop, calls=%fused_computation.38 | loop fusion | flops 148608 | bytes 396304 | tf_op jit(solution)/shard_map/add | solution.py:495
  85.3 0.6 select_reduce_fusion
  86.0 0.8 fusion.11
  86.8 0.9 fusion.23
  95.1 0.9 broadcast_in_dim.13
  95.9 11.8 %all-to-all-start.2 = ((bf16[64,32,128]{2,1,0:T(8,128)(2,1)}), bf16[64,32,128]{2,1,0:T(8,128)(2,1)S(1)}, u32[]{:S(2)}, u32[]{:S(2)}) async-start(bf16[64,32,128]{2,1,0:T(8,128)(2,1)} %broadcast_in_dim.13), calls=%async_computation.2 | async-start | bytes 1048576 | tf_op jit(solution)/shard_map/all_to_all | solution.py:420
  107.8 14.7 %collective-permute-done.6.refs_3_ = bf16[2560,256]{1,0:T(8,128)(2,1)S(1)} collective-permute-done((bf16[2560,256]{1,0:T(8,128)(2,1)}, bf16[2560,256]{1,0:T(8,128)(2,1)S(1)}, u32[]{:S(2)}, u32[]{:S(2)}) %collective-permute-start.6) | collective-permute-done | bytes 1310752 | tf_op jit(solution)/shard_map/ppermute | solution.py:39
  122.5 7.9 %collective-permute-done.7.refs_5_ = bf16[2560,256]{1,0:T(8,128)(2,1)S(1)} collective-permute-done((bf16[2560,256]{1,0:T(8,128)(2,1)}, bf16[2560,256]{1,0:T(8,128)(2,1)S(1)}, u32[]{:S(2)}, u32[]{:S(2)}) %collective-permute-start.7) | collective-permute-done | bytes 1310752 | tf_op jit(solution)/shard_map/ppermute | solution.py:39
  130.3 0.9 slice.22
  131.3 2.0 %collective-permute-start.13 = (bf16[1280,256]{1,0:T(8,128)(2,1)}, bf16[1280,256]{1,0:T(8,128)(2,1)}, u32[]{:S(2)}, u32[]{:S(2)}) collective-permute-start(bf16[1280,256]{1,0:T(8,128)(2,1)} %slice.22), channel_id=1, source_target_pairs={{0,1},{1,2},{2,3},{3,0},{4,5},{5,6},{6,7},{7,4},{8,9},{9,10},{10,1... | collective-permute-start | bytes 1966088 | tf_op jit(solution)/shard_map/ppermute | solution.py:39
  133.3 0.9 slice.23
  134.2 1.8 fusion.16
  136.0 1.4 collective-permute-start.14
  137.4 1.8 convolution_add_fusion.1
  139.2 1.5 collective-permute-start.12
  140.8 1.8 fusion.12
  142.6 1.8 fusion.1
  144.4 1.1 copy.32
  145.5 0.8 copy-done.7
  146.3 14.0 %collective-permute-done.12.refs_7_ = bf16[768,256]{1,0:T(8,128)(2,1)S(1)} collective-permute-done((bf16[768,256]{1,0:T(8,128)(2,1)S(1)}, bf16[768,256]{1,0:T(8,128)(2,1)S(1)}, u32[]{:S(2)}, u32[]{:S(2)}) %collective-permute-start.12) | collective-permute-done | bytes 393248 | tf_op jit(solution)/shard_map/ppermute | solution.py:39
  160.3 0.7 copy-done.8
  161.4 23.7 %mix_land.1 = bf16[256,4096]{1,0:T(8,128)(2,1)} custom-call(s32[4]{0:T(128)} %pad_add_fusion.src_ref, s32[64,8]{1,0:T(8,128)} %get-tuple-element.27.start_ref, bf16[1536,256]{1,0:T(8,128)(2,1)} %get-tuple-element.19.refs_0_, bf16[2560,256]{1,0:T(8,128)(2,1)} %get-tuple-element.25.refs_1_, bf16[1536,256]{1,0:T(8,128)(2,1)} %copy-done.4, ...), custom_call_target="tpu_custom_call" | custom-call | tf_op jit(solution)/shard_map/mix_land/pallas_call | solution.py:365
  (84 shorter events, 7.7 us)
Async XLA Ops:
  11.1 24.0 %copy-start.10 = (s32[512]{0:T(512)S(1)}, s32[512]{0:T(512)}, u32[]{:S(2)}) copy-start(s32[512]{0:T(512)} %param.17) | copy-start | bytes 6148
  11.1 24.9 %copy-start.9 = (s32[1,4096]{1,0:T(1,128)S(1)}, s32[1,4096]{1,0:T(1,128)}, u32[]{:S(2)}) copy-start(s32[1,4096]{1,0:T(1,128)} %get-tuple-element.18.pos_ref) | copy-start | bytes 49156
  11.1 33.4 %all-to-all-start = ((bf16[64,34,128]{2,1,0:T(8,128)(2,1)}), bf16[64,34,128]{2,1,0:T(8,128)(2,1)S(1)}, u32[]{:S(2)}, u32[]{:S(2)}) async-start(bf16[64,34,128]{2,1,0:T(8,128)(2,1)} %bucket_tiles.1), calls=%async_computation | async-start | bytes 1310720 | tf_op jit(solution)/shard_map/all_to_all | solution.py:465
  32.4 20.1 %collective-permute-start = (bf16[1536,256]{1,0:T(8,128)(2,1)}, bf16[1536,256]{1,0:T(8,128)(2,1)S(1)}, u32[]{:S(2)}, u32[]{:S(2)}) collective-permute-start(bf16[1536,256]{1,0:T(8,128)(2,1)} %get-tuple-element.19.refs_0_), channel_id=1, source_target_pairs={{0,1},{1,2},{2,3},{3,0},{4,5},{5,6},{6,7},{7,4},{8,9},{9,10},{10,1... | collective-permute-start | bytes 2359304 | tf_op jit(solution)/shard_map/ppermute | solution.py:39
  33.6 18.9 %collective-permute-start.1 = (bf16[1536,256]{1,0:T(8,128)(2,1)}, bf16[1536,256]{1,0:T(8,128)(2,1)S(1)}, u32[]{:S(2)}, u32[]{:S(2)}) collective-permute-start(bf16[1536,256]{1,0:T(8,128)(2,1)} %get-tuple-element.19.refs_0_), channel_id=1, source_target_pairs={{0,3},{1,0},{2,1},{3,2},{4,7},{5,4},{6,5},{7,6},{8,11},{9,8},{10,9... | collective-permute-start | bytes 2359304 | tf_op jit(solution)/shard_map/ppermute | solution.py:39
  35.1 100.9 %collective-permute-start.8 = (bf16[256,1024]{1,0:T(8,128)(2,1)}, bf16[256,1024]{1,0:T(8,128)(2,1)}, u32[]{:S(2)}, u32[]{:S(2)}) collective-permute-start(bf16[256,1024]{1,0:T(8,128)(2,1)} %bitcast.4.base_ref), channel_id=1, source_target_pairs={{0,1},{1,2},{2,3},{3,0},{4,5},{5,6},{6,7},{7,4},{8,9},{9,10},{10,1... | collective-permute-start | bytes 1572872 | tf_op jit(solution)/shard_map/ppermute | solution.py:39
  35.1 22.5 %copy-start.13 = (s32[1,4]{1,0:T(1,128)S(1)}, s32[1,4]{1,0:T(1,128)}, u32[]{:S(2)}) copy-start(s32[1,4]{1,0:T(1,128)} %param.19) | copy-start | bytes 52
  36.0 29.9 %copy-start.11 = (f32[512]{0:T(512)S(1)}, f32[512]{0:T(512)}, u32[]{:S(2)}) copy-start(f32[512]{0:T(512)} %param.16) | copy-start | bytes 6148
  36.0 29.9 %copy-start.12 = (f32[512]{0:T(512)S(1)}, f32[512]{0:T(512)}, u32[]{:S(2)}) copy-start(f32[512]{0:T(512)} %param.18) | copy-start | bytes 6148
  44.5 0.8 copy-start.2
  52.5 27.4 %copy-start.4 = (bf16[1536,256]{1,0:T(8,128)(2,1)}, bf16[1536,256]{1,0:T(8,128)(2,1)S(1)}, u32[]{:S(2)}) copy-start(bf16[1536,256]{1,0:T(8,128)(2,1)S(1)} %collective-permute-done.refs_2_) | copy-start | bytes 2359300
  52.5 28.4 %copy-start.5 = (bf16[1536,256]{1,0:T(8,128)(2,1)}, bf16[1536,256]{1,0:T(8,128)(2,1)S(1)}, u32[]{:S(2)}) copy-start(bf16[1536,256]{1,0:T(8,128)(2,1)S(1)} %collective-permute-done.1.refs_4_) | copy-start | bytes 2359300
  53.9 11.9 %all-to-all-start.1 = ((bf16[4,32,512]{2,1,0:T(8,128)(2,1)}), bf16[4,32,512]{2,1,0:T(8,128)(2,1)S(1)}, u32[]{:S(2)}, u32[]{:S(2)}) async-start(bf16[4,32,512]{2,1,0:T(8,128)(2,1)} %broadcast_in_dim.10), calls=%async_computation.1 | async-start | bytes 262144 | tf_op jit(solution)/shard_map/all_to_all | solution.py:420
  66.7 12.1 %collective-permute-start.2 = (f32[129,128]{1,0:T(8,128)S(1)}, f32[129,128]{1,0:T(8,128)S(1)}, u32[]{:S(2)}, u32[]{:S(2)}) collective-permute-start(f32[129,128]{1,0:T(8,128)S(1)} %pad_maximum_fusion), channel_id=1, source_target_pairs={{0,4},{4,8},{8,12},{12,16},{16,20},{20,24},{24,28},{28,32},{32,36}... | collective-permute-start | bytes 198152 | tf_op jit(solution)/shard_map/ppermute | solution.py:39
  69.8 9.6 %collective-permute-start.3 = (f32[129,128]{1,0:T(8,128)S(1)}, f32[129,128]{1,0:T(8,128)S(1)}, u32[]{:S(2)}, u32[]{:S(2)}) collective-permute-start(f32[129,128]{1,0:T(8,128)S(1)} %pad_maximum_fusion), channel_id=1, source_target_pairs={{0,252},{4,0},{8,4},{12,8},{16,12},{20,16},{24,20},{28,24},{32,28}... | collective-permute-start | bytes 198152 | tf_op jit(solution)/shard_map/ppermute | solution.py:39
  69.8 10.1 %collective-permute-start.4 = (f32[129,128]{1,0:T(8,128)S(1)}, f32[129,128]{1,0:T(8,128)S(1)}, u32[]{:S(2)}, u32[]{:S(2)}) collective-permute-start(f32[129,128]{1,0:T(8,128)S(1)} %pad_maximum_fusion), channel_id=1, source_target_pairs={{0,32},{4,36},{8,40},{12,44},{16,48},{20,52},{24,56},{28,60},{32,6... | collective-permute-start | bytes 198152 | tf_op jit(solution)/shard_map/ppermute | solution.py:39
  74.0 8.8 %collective-permute-start.5 = (f32[129,128]{1,0:T(8,128)S(1)}, f32[129,128]{1,0:T(8,128)S(1)}, u32[]{:S(2)}, u32[]{:S(2)}) collective-permute-start(f32[129,128]{1,0:T(8,128)S(1)} %pad_maximum_fusion), channel_id=1, source_target_pairs={{0,224},{4,228},{8,232},{12,236},{16,240},{20,244},{24,248},{28,25... | collective-permute-start | bytes 198152 | tf_op jit(solution)/shard_map/ppermute | solution.py:39
  78.7 60.5 %collective-permute-start.10 = (bf16[256,1024]{1,0:T(8,128)(2,1)}, bf16[256,1024]{1,0:T(8,128)(2,1)}, u32[]{:S(2)}, u32[]{:S(2)}) collective-permute-start(bf16[256,1024]{1,0:T(8,128)(2,1)} %bitcast.4.base_ref), channel_id=1, source_target_pairs={{0,2},{1,3},{2,0},{3,1},{4,6},{5,7},{6,4},{7,5},{8,10},{9,11},{10,... | collective-permute-start | bytes 1572872 | tf_op jit(solution)/shard_map/ppermute | solution.py:39
  79.4 63.2 %collective-permute-start.9 = (bf16[256,1024]{1,0:T(8,128)(2,1)}, bf16[256,1024]{1,0:T(8,128)(2,1)}, u32[]{:S(2)}, u32[]{:S(2)}) collective-permute-start(bf16[256,1024]{1,0:T(8,128)(2,1)} %bitcast.4.base_ref), channel_id=1, source_target_pairs={{0,3},{1,0},{2,1},{3,2},{4,7},{5,4},{6,5},{7,6},{8,11},{9,8},{10,9... | collective-permute-start | bytes 1572872 | tf_op jit(solution)/shard_map/ppermute | solution.py:39
  79.9 42.6 %collective-permute-start.6 = (bf16[2560,256]{1,0:T(8,128)(2,1)}, bf16[2560,256]{1,0:T(8,128)(2,1)S(1)}, u32[]{:S(2)}, u32[]{:S(2)}) collective-permute-start(bf16[2560,256]{1,0:T(8,128)(2,1)} %get-tuple-element.25.refs_1_), channel_id=1, source_target_pairs={{0,1},{1,2},{2,3},{3,0},{4,5},{5,6},{6,7},{7,4},{8,9},{9,10},{10,1... | collective-permute-start | bytes 3932168 | tf_op jit(solution)/shard_map/ppermute | solution.py:39
  82.8 47.5 %collective-permute-start.7 = (bf16[2560,256]{1,0:T(8,128)(2,1)}, bf16[2560,256]{1,0:T(8,128)(2,1)S(1)}, u32[]{:S(2)}, u32[]{:S(2)}) collective-permute-start(bf16[2560,256]{1,0:T(8,128)(2,1)} %get-tuple-element.25.refs_1_), channel_id=1, source_target_pairs={{0,3},{1,0},{2,1},{3,2},{4,7},{5,4},{6,5},{7,6},{8,11},{9,8},{10,9... | collective-permute-start | bytes 3932168 | tf_op jit(solution)/shard_map/ppermute | solution.py:39
  95.9 64.3 %all-to-all-start.2 = ((bf16[64,32,128]{2,1,0:T(8,128)(2,1)}), bf16[64,32,128]{2,1,0:T(8,128)(2,1)S(1)}, u32[]{:S(2)}, u32[]{:S(2)}) async-start(bf16[64,32,128]{2,1,0:T(8,128)(2,1)} %broadcast_in_dim.13), calls=%async_computation.2 | async-start | bytes 1048576 | tf_op jit(solution)/shard_map/all_to_all | solution.py:420
  122.5 13.5 %copy-start = (bf16[2560,256]{1,0:T(8,128)(2,1)}, bf16[2560,256]{1,0:T(8,128)(2,1)S(1)}, u32[]{:S(2)}) copy-start(bf16[2560,256]{1,0:T(8,128)(2,1)S(1)} %collective-permute-done.6.refs_3_) | copy-start | bytes 3932164
  122.5 23.0 %collective-permute-start.11 = (bf16[768,256]{1,0:T(8,128)(2,1)}, bf16[768,256]{1,0:T(8,128)(2,1)S(1)}, u32[]{:S(2)}, u32[]{:S(2)}) collective-permute-start(bf16[768,256]{1,0:T(8,128)(2,1)} %slice.20), channel_id=1, source_target_pairs={{0,1},{1,2},{2,3},{3,0},{4,5},{5,6},{6,7},{7,4},{8,9},{9,10},{10,1... | collective-permute-start | bytes 1179656 | tf_op jit(solution)/shard_map/ppermute | solution.py:39
  130.3 5.7 %copy-start.1 = (bf16[2560,256]{1,0:T(8,128)(2,1)}, bf16[2560,256]{1,0:T(8,128)(2,1)S(1)}, u32[]{:S(2)}) copy-start(bf16[2560,256]{1,0:T(8,128)(2,1)S(1)} %collective-permute-done.7.refs_5_) | copy-start | bytes 3932164
  131.3 29.0 %collective-permute-start.13 = (bf16[1280,256]{1,0:T(8,128)(2,1)}, bf16[1280,256]{1,0:T(8,128)(2,1)}, u32[]{:S(2)}, u32[]{:S(2)}) collective-permute-start(bf16[1280,256]{1,0:T(8,128)(2,1)} %slice.22), channel_id=1, source_target_pairs={{0,1},{1,2},{2,3},{3,0},{4,5},{5,6},{6,7},{7,4},{8,9},{9,10},{10,1... | collective-permute-start | bytes 1966088 | tf_op jit(solution)/shard_map/ppermute | solution.py:39
  136.0 24.2 %collective-permute-start.14 = (bf16[1280,256]{1,0:T(8,128)(2,1)}, bf16[1280,256]{1,0:T(8,128)(2,1)S(1)}, u32[]{:S(2)}, u32[]{:S(2)}) collective-permute-start(bf16[1280,256]{1,0:T(8,128)(2,1)} %slice.23), channel_id=1, source_target_pairs={{0,3},{1,0},{2,1},{3,2},{4,7},{5,4},{6,5},{7,6},{8,11},{9,8},{10,9... | collective-permute-start | bytes 1966088 | tf_op jit(solution)/shard_map/ppermute | solution.py:39
  139.2 21.0 %collective-permute-start.12 = (bf16[768,256]{1,0:T(8,128)(2,1)S(1)}, bf16[768,256]{1,0:T(8,128)(2,1)S(1)}, u32[]{:S(2)}, u32[]{:S(2)}) collective-permute-start(bf16[768,256]{1,0:T(8,128)(2,1)S(1)} %slice.21), channel_id=1, source_target_pairs={{0,3},{1,0},{2,1},{3,2},{4,7},{5,4},{6,5},{7,6},{8,11},{9,8},{10,9... | collective-permute-start | bytes 1179656 | tf_op jit(solution)/shard_map/ppermute | solution.py:39
  145.5 0.8 copy-start.7
  160.3 0.8 copy-start.8
  160.3 0.9 copy-start.3
  160.3 1.1 copy-start.6

commit v2 on v1

--- a/solution.py
+++ b/solution.py
@@ -86,7 +86,7 @@
     )(owners)
 
 
-def bucket_tiles(land_rows, levels, weight, mask, owners, ranks, columns, npatch, bucket):
+def bucket_tiles(land_rows, levels, weight, owners, ranks, columns, npatch, bucket):
     width, tiles = land_rows.shape
     rows = width // levels
     low = 4
@@ -95,7 +95,7 @@
     steps = tiles // block
 
     def kernel(
-        x_ref, weight_ref, mask_ref, owner_ref, rank_ref, col_ref, out_ref, acc_ref, cacc_ref
+        x_ref, weight_ref, owner_ref, rank_ref, col_ref, out_ref, acc_ref, cacc_ref
     ):
         step = pl.program_id(0)
         owner = owner_ref[...]
@@ -103,8 +103,7 @@
         hot = (iota((low * bucket, block), 0) == slot).astype(F32).astype(BF)
         group = owner >> 2
         surface = (iota((rows, width), 0) * levels == iota((rows, width), 1)).astype(F32)
-        keep = weight_ref[...].astype(F32) * mask_ref[...].astype(F32)
-        value = (dot(surface.astype(BF), x_ref[...]) * keep).astype(BF)
+        value = (dot(surface.astype(BF), x_ref[...]) * weight_ref[...]).astype(BF)
         zero = jnp.zeros_like(value)
         picked = jnp.concatenate(
             [jnp.where(group == g, value, zero) for g in range(high)], axis=0
@@ -139,7 +138,7 @@
         kernel,
         grid=(steps,),
         out_shape=jax.ShapeDtypeStruct((npatch, rows + 2, bucket), BF),
-        in_specs=[pl.BlockSpec((width, block), lambda i: (0, i))] + [lane] * 5,
+        in_specs=[pl.BlockSpec((width, block), lambda i: (0, i))] + [lane] * 4,
         out_specs=pl.BlockSpec((npatch, rows + 2, bucket), lambda i: (0, 0, 0)),
         scratch_shapes=[
             pltpu.VMEM((high * rows, low * bucket), F32),
@@ -147,7 +146,7 @@
         ],
         compiler_params=params(60),
         name="bucket_tiles",
-    )(land_rows, weight, mask, owners, ranks, columns)
+    )(land_rows, weight, owners, ranks, columns)
 
 
 def lane_swap(rows, a, b):
@@ -189,7 +188,7 @@
     )(pos, land_rows)
 
 
-def screen_forecast(received, base_rows, levels, obs_column):
+def screen_forecast(received, base_rows, levels, obs_column, copies):
     npatch, rows2, _ = received.shape
     rows = rows2 - 2
     nobs = obs_column.shape[0]
@@ -211,19 +210,21 @@
             ).astype(F32)
             col = (digits[0:1] * 32.0 + digits[1:2]).astype(I32)
             acc = acc + dot(values, (obs == col).astype(F32).astype(BF), NT)
-        out_ref[...] = acc.astype(BF)
+        value = acc.astype(BF)
+        for m in range(copies):
+            out_ref[m] = value
 
     return pl.pallas_call(
         kernel,
-        out_shape=jax.ShapeDtypeStruct((rows, nobs), BF),
+        out_shape=jax.ShapeDtypeStruct((copies, rows, nobs), BF),
         in_specs=[VMEM, VMEM, VMEM],
         out_specs=VMEM,
-        compiler_params=params(60),
+        compiler_params=params(24),
         name="screen_forecast",
     )(received, base_rows, obs_column)
 
 
-def mix_land(pieces, sources, starts, mixes, pos_col, land_rows, mask_row, levels):
+def mix_land(pieces, sources, starts, mixes, pos, land_rows, mask_row, levels):
     slots = len(pieces)
     flat = [piece for group in pieces for piece in group]
     places = [
@@ -356,11 +357,11 @@
 
             lax.fori_loop(0, npatch // UNROLL, owners, 0)
 
-        hot = (iota((span, span), 1) == pos_ref[...]).astype(F32).astype(BF)
+        hot = (iota((span, span), 0) == pos_ref[...]).astype(F32).astype(BF)
         rows = y_ref[pl.ds(pl.multiple_of(step * span, span), span), :]
-        rows = dot(rows, lane_swap(width, levels, local)).astype(BF)
-        back = dot(hot, rows)
-        out_ref[...] = jnp.where(mask_ref[...] == 1, back.T.astype(BF), land_ref[...])
+        turned = dot(lane_swap(width, local, levels), rows, NT).astype(BF)
+        back = dot(turned, hot).astype(BF)
+        out_ref[...] = jnp.where(mask_ref[...] == 1, back, land_ref[...])
 
     return pl.pallas_call(
         kernel,
@@ -370,7 +371,7 @@
         + [pl.BlockSpec(memory_space=pl.ANY)] * count
         + [
             VMEM,
-            pl.BlockSpec((span, 1), lambda i: (i, 0)),
+            pl.BlockSpec((1, span), lambda i: (0, i)),
             pl.BlockSpec((width, span), lambda i: (0, i)),
             pl.BlockSpec((1, span), lambda i: (0, i)),
         ],
@@ -388,36 +389,111 @@
         starts,
         *flat,
         mixes.reshape(npatch * local, members),
-        pos_col,
+        pos,
         land_rows,
         mask_row,
     )
 
 
-def settle(local_gram, local_proj):
-    members = local_gram.shape[0]
-    identity = jnp.eye(members, dtype=jnp.float32)
-    system = local_gram + (members - 1.0) * identity
-    trace_scale = jnp.trace(system)
-    upper_iter = system / trace_scale
-    lower_iter = identity
-    for _ in range(SWEEPS):
-        middle_step = 0.5 * (3.0 * identity - jnp.dot(lower_iter, upper_iter, precision=PRECISE))
-        upper_iter = jnp.dot(upper_iter, middle_step, precision=PRECISE)
-        lower_iter = jnp.dot(middle_step, lower_iter, precision=PRECISE)
-    inv_root = lower_iter / jnp.sqrt(trace_scale)
-    mean_shift = jnp.dot(
-        inv_root, jnp.dot(inv_root, local_proj, precision=PRECISE), precision=PRECISE
-    )
-    spread = mean_shift[:, None] + math.sqrt(members - 1.0) * inv_root
-    centered = spread - jnp.mean(spread, axis=0, keepdims=True)
-    return (centered + 1.0 / members).astype(jnp.bfloat16)
-
-
-def to_all(value, axis):
-    count = lax.axis_size(axis)
-    copies = jnp.broadcast_to(value[None], (count,) + value.shape)
-    return lax.all_to_all(copies, axis, split_axis=0, concat_axis=0, tiled=True)
+def exact(a, b, dims=NN):
+    return lax.dot_general(a, b, dims, precision=PRECISE, preferred_element_type=F32)
+
+
+def screen_stats(ensemble, obs_value, obs_error):
+    count, local, nobs = ensemble.shape
+    members = count * local
+    half = members // 2
+
+    def kernel(in_ref, value_ref, error_ref, out_ref):
+        rows = jnp.concatenate([in_ref[m].astype(F32) for m in range(count)], axis=0)
+        center = jnp.mean(rows, axis=0, keepdims=True)
+        inverse_sd = lax.rsqrt(error_ref[...])
+        scaled = (rows - center) * inverse_sd
+        innovation = (value_ref[...] - center) * inverse_sd
+        gram = exact(scaled, scaled, NT)
+        proj = exact(jnp.broadcast_to(innovation, (8, nobs)), scaled, NT)
+        row, lane = iota((half, members), 0), iota((half, members), 1)
+        top = gram[:half]
+        from_low = jnp.logical_and(lane < half, lane >= row)
+        out_ref[:half, :] = jnp.where(from_low, pltpu.roll(gram[half:], half, 1), top)
+        diag = jnp.sum(jnp.where(row == lane, top, 0.0), axis=0, keepdims=True)
+        tail = iota((8, members), 0)
+        out_ref[half:, :] = jnp.where(tail == 0, diag, jnp.where(tail == 1, proj, 0.0))
+
+    return pl.pallas_call(
+        kernel,
+        out_shape=jax.ShapeDtypeStruct((half + 8, members), F32),
+        in_specs=[VMEM, VMEM, VMEM],
+        out_specs=VMEM,
+        compiler_params=params(16),
+        name="screen_stats",
+    )(ensemble, obs_value, obs_error)
+
+
+def settle(own, near, listed, places, local, npatch):
+    members = own.shape[1]
+    half = members // 2
+    count = members // local
+    names = listed.shape[1]
+
+    def kernel(list_ref, place_ref, own_ref, *refs):
+        near_refs = refs[: len(near)]
+        cols_ref, out_ref, hold_ref = refs[len(near) :]
+        total = own_ref[...]
+        for d in range(len(near)):
+            used = 0
+            for i in range(names):
+                used = used + jnp.where(list_ref[0, i] == place_ref[d], 1, 0)
+            total = total + used.astype(F32) * near_refs[d][...]
+        packed = total[:half]
+        row, lane = iota((half, members), 0), iota((half, members), 1)
+        left = lane < half
+        upper = jnp.logical_and(left, lane >= row)
+        strict = jnp.logical_and(left, lane > row)
+        top = jnp.where(upper, 0.0, packed)
+        low = pltpu.roll(jnp.where(strict, packed, 0.0), half, 1)
+        sides = jnp.concatenate([top, low], axis=0)
+        on_diag = jnp.where(jnp.logical_and(left, lane == row), packed, 0.0)
+        top_diag = jnp.where(row == lane, total[half : half + 1], 0.0)
+        diag = jnp.concatenate([top_diag, pltpu.roll(on_diag, half, 1)], axis=0)
+        eye = (iota((members, members), 0) == iota((members, members), 1)).astype(F32)
+        system = sides + sides.T + diag + (members - 1.0) * eye
+        scale = jnp.sum(jnp.sum(system * eye, axis=1, keepdims=True), axis=0, keepdims=True)
+        upper_iter = system / scale
+        middle = 1.5 * eye - 0.5 * upper_iter
+        upper_iter = exact(upper_iter, middle)
+        lower_iter = middle
+        for step in range(SWEEPS - 1):
+            middle = 1.5 * eye - 0.5 * exact(lower_iter, upper_iter)
+            if step < SWEEPS - 2:
+                upper_iter = exact(upper_iter, middle)
+            lower_iter = exact(middle, lower_iter)
+        inv_root = lower_iter * lax.rsqrt(scale)
+        proj = jnp.broadcast_to(total[half + 1 : half + 2], (8, members))
+        shift = exact(exact(proj, inv_root, NT), inv_root, NT)[:1]
+        spread = shift + math.sqrt(members - 1.0) * inv_root
+        hold_ref[...] = spread - jnp.mean(spread, axis=1, keepdims=True) + 1.0 / members
+        mine = hold_ref[pl.ds(pl.multiple_of(place_ref[len(near)] * local, local), local), :]
+        cols_ref[...] = mine.astype(BF)
+        flipped = mine.T
+        blocks = jnp.concatenate(
+            [flipped[m * local : (m + 1) * local] for m in range(count)], axis=1
+        ).astype(BF)
+        for p in range(npatch):
+            out_ref[p] = blocks
+
+    return pl.pallas_call(
+        kernel,
+        out_shape=(
+            jax.ShapeDtypeStruct((local, members), BF),
+            jax.ShapeDtypeStruct((npatch, local, members), BF),
+        ),
+        in_specs=[SMEM, SMEM] + [VMEM] * (1 + len(near)),
+        out_specs=(VMEM, VMEM),
+        scratch_shapes=[pltpu.VMEM((members, members), F32)],
+        compiler_params=params(16),
+        name="settle",
+    )(listed, places, own, *near)
 
 
 def analysis(
@@ -437,7 +513,6 @@
     mem_count = lax.axis_size("mem")
     local, levels, columns = atmos.shape
     layers, tiles = (land.shape[1], land.shape[2])
-    members = local * mem_count
     bucket = 2 * tiles // npatch
     row_width = max(2, npatch // 8)
     first = 3 * tiles // 8
@@ -454,8 +529,7 @@
     packed = bucket_tiles(
         land_rows,
         layers,
-        tile_weight.reshape(1, tiles),
-        mask_row,
+        (tile_weight.astype(F32) * land_mask.astype(F32)).reshape(1, tiles),
         owners,
         ranks,
         tile_column.reshape(1, tiles),
@@ -468,9 +542,11 @@
     low_prev = shifted(low, "mem", 1)
     low_next = shifted(low, "mem", -1)
 
-    forecast = screen_forecast(received, atmos_rows, levels, observation_column.reshape(-1, 1))
+    forecast = screen_forecast(
+        received, atmos_rows, levels, observation_column.reshape(-1, 1), mem_count
+    )
     forecast, low_prev, low_next = barrier((forecast, low_prev, low_next))
-    ensemble = to_all(forecast, "mem")
+    ensemble = lax.all_to_all(forecast, "mem", split_axis=0, concat_axis=0, tiled=True)
     ensemble, high, low_prev, low_next = barrier((ensemble, high, low_prev, low_next))
     high_prev = shifted(high, "mem", 1)
     high_next = shifted(high, "mem", -1)
@@ -478,26 +554,13 @@
         shifted(low_prev[: first // 2], "mem", 1), shifted(low_next[first // 2 :], "mem", -1)
     ]
 
-    ensemble = ensemble.reshape(members, -1).astype(F32)
-    center = jnp.mean(ensemble, axis=0)
-    inverse_sd = lax.rsqrt(obs_error)
-    scaled = (ensemble - center[None, :]) * inverse_sd[None, :]
-    innovation = (obs_value - center) * inverse_sd
-    gram_own = jnp.dot(scaled, scaled.T, precision=PRECISE)
-    proj_own = jnp.dot(scaled, innovation, precision=PRECISE)
-    own_stats = jnp.concatenate([gram_own, proj_own[None, :]], axis=0)
-    listed = loc_blocks[0]
-    local_stats = own_stats
-    for offset in (1, -1, row_width, -row_width):
-        near_stats = shifted(own_stats, "patch", offset)
-        source = (patch_rank - offset) % npatch
-        used = jnp.sum((listed == source).astype(jnp.float32))
-        local_stats = local_stats + used * near_stats
-    mix = settle(local_stats[:members], local_stats[members])
-
-    own_cols = lax.dynamic_slice_in_dim(mix.T, mem_rank * local, local, 0)
-    blocks = own_cols.reshape(local, mem_count, local).transpose(2, 1, 0).reshape(local, members)
-    all_mixes = to_all(blocks, "patch")
+    own_stats = screen_stats(ensemble, obs_value.reshape(1, -1), obs_error.reshape(1, -1))
+    offsets = (row_width, -row_width, 1, -1)
+    near = [shifted(own_stats, "patch", o) for o in offsets]
+    places = [(patch_rank - o) % npatch for o in offsets]
+    places = jnp.stack(places + [mem_rank]).astype(I32)
+    own_cols, mixes = settle(own_stats, near, loc_blocks, places, local, npatch)
+    all_mixes = lax.all_to_all(mixes, "patch", split_axis=0, concat_axis=0, tiled=True)
     own_cols, high_prev, high_next = barrier((own_cols, high_prev, high_next))
     split = high.shape[0] // 2
     high_far = [shifted(high_prev[:split], "mem", 1), shifted(high_next[split:], "mem", -1)]
@@ -517,7 +580,7 @@
         sources,
         starts,
         all_mixes,
-        pos.reshape(tiles, 1),
+        pos,
         land_rows,
         mask_row,
         layers,

time: 186 us -> 163 us (0.88)
  waiting for transfers between devices: 54.9 us -> 35.1 us
  matrix products: 15.5 us -> 6.29 us
  blocking collectives: 0 us -> 8.38 us
  local copies, waits for them, and re-layouts: 13.2 us -> 8.44 us
  Pallas kernels: 45.7 us -> 50.3 us
  other arithmetic: 4.88 us -> 1.99 us
    ppermute x15, waiting for transfers between devices: 40.9 us -> 25.9 us  [shifted(): return lax.ppermute(value, axis, pairs)]
    all_to_all x0 -> x1, blocking collectives: none -> 8.38 us  [analysis(): lax.all_to_all(forecast, 'mem', split_axis=0, concat_axis=0, tiled=True)]
    dot_general x33 -> x0, matrix products: 8.21 us -> none  [the longest x10 2.68 us: settle(): jnp.dot(lower_iter, upper_iter, precision=PRECISE)]
    ppermute x15, starting transfers between devices: 20.3 us -> 28.4 us  [shifted(): return lax.ppermute(value, axis, pairs)]
    all_to_all x2 -> x1, starting transfers between devices: 15.5 us -> 7.77 us  [analysis(): lax.all_to_all(mixes, 'patch', split_axis=0, concat_axis=0, tiled=True)]
    all_to_all x2 -> x1, waiting for transfers between devices: 7.56 us -> 0.01 us  [analysis(): lax.all_to_all(mixes, 'patch', split_axis=0, concat_axis=0, tiled=True)]
    pallas_call x1 -> x3, Pallas kernels: 4.85 us -> 10.4 us  [the longest x1 6.74 us: settle(): pl.pallas_call(kernel, out_shape=(jax.ShapeDtypeStruct((local, members),...]
    reshape x4 -> x0, local copies, waits for them, and re-layouts: 3.5 us -> none  [the longest x1 1.99 us: analysis(): pos.reshape(tiles, 1)]
  transfers between devices with their start and end apart: 18 -> 17, of which waited for: 7 -> 7; matrix products, arithmetic and copies ran while one was open for 16% -> 9% of each run, Pallas kernels for 7% -> 11%
where the time goes in v2:
time: 163 us; the launch traced here: 161 us
  Pallas kernels  50.3 us (31%)
  starting transfers between devices  49.3 us (30%)
  waiting for transfers between devices  35.1 us (22%)
  local copies, waits for them, and re-layouts  8.44 us (5%)
  blocking collectives  8.38 us (5%)
  matrix products  6.29 us (4%)
  other arithmetic  1.99 us (1%)
    ppermute x15, starting transfers between devices, shifted(): return lax.ppermute(value, axis, pairs)  28.4 us
    ppermute x15, waiting for transfers between devices, shifted(): return lax.ppermute(value, axis, pairs)  25.9 us
    pallas_call x1, Pallas kernels, mix_land(): pl.pallas_call(kernel, grid=(PARTS,), out_shape=jax.ShapeDtypeStruct((wid...  22.7 us
    all_to_all x1, starting transfers between devices, analysis(): lax.all_to_all(packed, 'patch', split_axis=0, concat_axis=0, tiled=True)  13.1 us
    all_to_all x1, waiting for transfers between devices, analysis(): lax.all_to_all(packed, 'patch', split_axis=0, concat_axis=0, tiled=True)  9.13 us
    all_to_all x1, blocking collectives, analysis(): lax.all_to_all(forecast, 'mem', split_axis=0, concat_axis=0, tiled=True)  8.38 us
    pallas_call x1, Pallas kernels, sort_land(): pl.pallas_call(kernel, out_shape=(jax.ShapeDtypeStruct((first, width), BF...  8.1 us
    all_to_all x1, starting transfers between devices, analysis(): lax.all_to_all(mixes, 'patch', split_axis=0, concat_axis=0, tiled=True)  7.77 us
  transfers between devices with their start and end apart: 17, of which 7 were waited for; matrix products, arithmetic and copies ran while one was open for 9% of the time, Pallas kernels for 11%

profile of v2, /device:TPU:1, one launch (start us, length us, event | category | flops | bytes accessed | tf_op | source)
XLA Modules:
  0.0 160.7 jit_solution(257914194003266594)
XLA Ops:
  0.6 2.3 %order_tiles.1 = (s32[1,4096]{1,0:T(1,128)}, s32[1,4096]{1,0:T(1,128)}, s32[64,8]{1,0:T(8,128)}) custom-call(s32[1,4096]{1,0:T(1,128)} %bitcast.46), custom_call_target="tpu_custom_call" | custom-call | tf_op jit(solution)/shard_map/order_tiles/pallas_call | solution.py:75
  2.9 1.3 convert_multiply_fusion
  4.3 6.8 %bucket_tiles.1 = bf16[64,34,128]{2,1,0:T(8,128)(2,1)} custom-call(bf16[256,4096]{1,0:T(8,128)(2,1)} %bitcast.41, f32[1,4096]{1,0:T(1,128)} %bitcast.49, s32[1,4096]{1,0:T(1,128)} %bitcast.47, s32[1,4096]{1,0:T(1,128)} %get-tuple-element.19.rank_ref, s32[1,4096]{1,0:T(1,128)} %bitcast.50), custom_call_target="tpu_custom_call" | custom-call | tf_op jit(solution)/shard_map/bucket_tiles/pallas_call | solution.py:137
  11.0 13.1 %all-to-all-start = ((bf16[64,34,128]{2,1,0:T(8,128)(2,1)}), bf16[64,34,128]{2,1,0:T(8,128)(2,1)S(1)}, u32[]{:S(2)}, u32[]{:S(2)}) async-start(bf16[64,34,128]{2,1,0:T(8,128)(2,1)} %bucket_tiles.1), calls=%async_computation | async-start | bytes 1310720 | tf_op jit(solution)/shard_map/all_to_all | solution.py:539
  24.2 0.0 copy-start
  24.2 8.1 %sort_land.1 = (bf16[1536,256]{1,0:T(8,128)(2,1)}, bf16[2560,256]{1,0:T(8,128)(2,1)}) custom-call(s32[1,4096]{1,0:T(1,128)} %get-tuple-element.20.pos_ref.refs_11_, bf16[256,4096]{1,0:T(8,128)(2,1)} %bitcast.42), custom_call_target="tpu_custom_call" | custom-call | tf_op jit(solution)/shard_map/sort_land/pallas_call | solution.py:178
  32.3 1.2 collective-permute-start
  33.5 1.5 collective-permute-start.1
  35.0 0.1 copy.17.obs_ref
  35.1 9.1 %all-to-all-done.in_ref = bf16[64,34,128]{2,1,0:T(8,128)(2,1)S(1)} async-done(((bf16[64,34,128]{2,1,0:T(8,128)(2,1)}), bf16[64,34,128]{2,1,0:T(8,128)(2,1)S(1)}, u32[]{:S(2)}, u32[]{:S(2)}) %all-to-all-start) | async-done | bytes 557088 | tf_op jit(solution)/shard_map/all_to_all | solution.py:539
  44.3 3.0 %screen_forecast.1 = bf16[4,32,512]{2,1,0:T(8,128)(2,1)S(1)} custom-call(bf16[64,34,128]{2,1,0:T(8,128)(2,1)S(1)} %all-to-all-done.in_ref, bf16[256,1024]{1,0:T(8,128)(2,1)S(1)} %bitcast.35, s32[512,1]{1,0:T(8,128)S(1)} %copy.17.obs_ref), custom_call_target="tpu_custom_call" | custom-call | tf_op jit(solution)/shard_map/screen_forecast/pallas_call | solution.py:217
  47.3 0.0 copy-start.3
  47.3 5.1 %collective-permute-done.refs_2_ = bf16[1536,256]{1,0:T(8,128)(2,1)S(1)} collective-permute-done((bf16[1536,256]{1,0:T(8,128)(2,1)}, bf16[1536,256]{1,0:T(8,128)(2,1)S(1)}, u32[]{:S(2)}, u32[]{:S(2)}) %collective-permute-start) | collective-permute-done | bytes 786464 | tf_op jit(solution)/shard_map/ppermute | solution.py:39
  52.4 8.4 %all_to_all.15.in_ref = bf16[4,32,512]{2,1,0:T(8,128)(2,1)S(1)} all-to-all(bf16[4,32,512]{2,1,0:T(8,128)(2,1)S(1)} %screen_forecast.1), channel_id=1, replica_groups=mesh['patch'=64,'mem'=4] {'mem'}, dimensions={0} | all-to-all | bytes 262144 | tf_op jit(solution)/shard_map/all_to_all | solution.py:549
  60.8 0.3 collective-permute-start.6
  61.1 2.4 %collective-permute-start.7 = (bf16[2560,256]{1,0:T(8,128)(2,1)}, bf16[2560,256]{1,0:T(8,128)(2,1)}, u32[]{:S(2)}, u32[]{:S(2)}) collective-permute-start(bf16[2560,256]{1,0:T(8,128)(2,1)} %get-tuple-element.28.refs_1_), channel_id=1, source_target_pairs={{0,3},{1,0},{2,1},{3,2},{4,7},{5,4},{6,5},{7,6},{8,11},{9,8},{10,9... | collective-permute-start | bytes 3932168 | tf_op jit(solution)/shard_map/ppermute | solution.py:39
  63.5 0.7 screen_stats.1.own_ref
  64.1 5.4 %collective-permute-start.2 = (f32[72,128]{1,0:T(8,128)S(1)}, f32[72,128]{1,0:T(8,128)S(1)}, u32[]{:S(2)}, u32[]{:S(2)}) collective-permute-start(f32[72,128]{1,0:T(8,128)S(1)} %screen_stats.1.own_ref), channel_id=1, source_target_pairs={{0,32},{4,36},{8,40},{12,44},{16,48},{20,52},{24,56},{28,60},{32,6... | collective-permute-start | bytes 110600 | tf_op jit(solution)/shard_map/ppermute | solution.py:39
  69.5 2.5 %collective-permute-start.3 = (f32[72,128]{1,0:T(8,128)S(1)}, f32[72,128]{1,0:T(8,128)S(1)}, u32[]{:S(2)}, u32[]{:S(2)}) collective-permute-start(f32[72,128]{1,0:T(8,128)S(1)} %screen_stats.1.own_ref), channel_id=1, source_target_pairs={{0,224},{4,228},{8,232},{12,236},{16,240},{20,244},{24,248},{28,25... | collective-permute-start | bytes 110600 | tf_op jit(solution)/shard_map/ppermute | solution.py:39
  72.0 1.4 collective-permute-done.2.refs_0_
  73.4 5.7 %collective-permute-start.4 = (f32[72,128]{1,0:T(8,128)S(1)}, f32[72,128]{1,0:T(8,128)S(1)}, u32[]{:S(2)}, u32[]{:S(2)}) collective-permute-start(f32[72,128]{1,0:T(8,128)S(1)} %screen_stats.1.own_ref), channel_id=1, source_target_pairs={{0,4},{4,8},{8,12},{12,16},{16,20},{20,24},{24,28},{28,32},{32,36}... | collective-permute-start | bytes 110600 | tf_op jit(solution)/shard_map/ppermute | solution.py:39
  79.0 2.2 %collective-permute-start.5 = (f32[72,128]{1,0:T(8,128)S(1)}, f32[72,128]{1,0:T(8,128)S(1)}, u32[]{:S(2)}, u32[]{:S(2)}) collective-permute-start(f32[72,128]{1,0:T(8,128)S(1)} %screen_stats.1.own_ref), channel_id=1, source_target_pairs={{0,252},{4,0},{8,4},{12,8},{16,12},{20,16},{24,20},{28,24},{32,28}... | collective-permute-start | bytes 110600 | tf_op jit(solution)/shard_map/ppermute | solution.py:39
  81.2 0.7 pad_add_fusion.src_ref
  81.9 0.1 stack.38.place_ref
  82.0 0.8 slice.12
  82.8 1.8 %slice.13 = bf16[768,256]{1,0:T(8,128)(2,1)} slice(bf16[1536,256]{1,0:T(8,128)(2,1)} %collective-permute-done.1.refs_4_), slice={[768:1536], [0:256]} | slice | bytes 786432 | tf_op jit(solution)/shard_map/slice | solution.py:554
  84.5 1.2 collective-permute-start.10
  85.7 1.9 %collective-permute-start.9 = (bf16[256,1024]{1,0:T(8,128)(2,1)S(1)}, bf16[256,1024]{1,0:T(8,128)(2,1)}, u32[]{:S(2)}, u32[]{:S(2)}) collective-permute-start(bf16[256,1024]{1,0:T(8,128)(2,1)S(1)} %bitcast.38), channel_id=1, source_target_pairs={{0,3},{1,0},{2,1},{3,2},{4,7},{5,4},{6,5},{7,6},{8,11},{9,8},{10,9... | collective-permute-start | bytes 1572872 | tf_op jit(solution)/shard_map/ppermute | solution.py:39
  87.6 6.7 %settle.1 = (bf16[32,128]{1,0:T(8,128)(2,1)S(1)}, bf16[64,32,128]{2,1,0:T(8,128)(2,1)}) custom-call(s32[1,4]{1,0:T(1,128)S(1)} %copy-done.3, s32[5]{0:T(128)S(1)} %stack.38.place_ref, f32[72,128]{1,0:T(8,128)S(1)} %screen_stats.1.own_ref, f32[72,128]{1,0:T(8,128)S(1)} %collective-permute-done.2.refs_0_, f32[72,128]{1,0:T(8,128)S(1)} %collective-permute-done.3.refs_1_, ...), custom_call_target="tpu_custom_call" | custom-call | tf_op jit(solution)/shard_map/settle/pallas_call | solution.py:485
  94.3 7.8 %all-to-all-start.2 = ((bf16[64,32,128]{2,1,0:T(8,128)(2,1)}), bf16[64,32,128]{2,1,0:T(8,128)(2,1)S(1)}, u32[]{:S(2)}, u32[]{:S(2)}) async-start(bf16[64,32,128]{2,1,0:T(8,128)(2,1)} %get-tuple-element.35), calls=%async_computation.2 | async-start | bytes 1048576 | tf_op jit(solution)/shard_map/all_to_all | solution.py:563
  102.1 0.6 collective-permute-start.11
  102.7 0.9 slice.14
  103.6 1.7 %collective-permute-start.13 = (bf16[1280,256]{1,0:T(8,128)(2,1)}, bf16[1280,256]{1,0:T(8,128)(2,1)S(1)}, u32[]{:S(2)}, u32[]{:S(2)}) collective-permute-start(bf16[1280,256]{1,0:T(8,128)(2,1)} %slice.14), channel_id=1, source_target_pairs={{0,1},{1,2},{2,3},{3,0},{4,5},{5,6},{6,7},{7,4},{8,9},{9,10},{10,1... | collective-permute-start | bytes 1966088 | tf_op jit(solution)/shard_map/ppermute | solution.py:39
  105.3 2.0 %slice.15 = bf16[1280,256]{1,0:T(8,128)(2,1)} slice(bf16[2560,256]{1,0:T(8,128)(2,1)} %collective-permute-done.7.refs_5_), slice={[1280:2560], [0:256]} | slice | bytes 1310720 | tf_op jit(solution)/shard_map/slice | solution.py:566
  107.3 0.8 fusion.6
  108.1 1.2 collective-permute-start.14
  109.3 1.9 %convolution_add_fusion.1 = f32[32,8,1024]{2,0,1:T(8,128)S(1)} fusion(f32[32,8,1024]{2,0,1:T(8,128)S(1)} %fusion.6, bf16[32,8,1024]{2,1,0:T(8,128)(2,1)} %bitcast.15, bf16[32,128]{1,0:T(8,128)(2,1)S(1)} %get-tuple-element.29, s32[]{:T(128)S(6)} %select_n.62), kind=kOutput, calls=%fused_computation.2 | convolution fusion | flops 17039360 | bytes 2629636 | tf_op jit(solution)/shard_map/jk,klc->jlc/dot_general | solution.py:573
  111.2 0.3 collective-permute-done.10
  111.5 0.8 collective-permute-start.12
  112.3 1.8 %fusion.2 = f32[32,8,1024]{2,0,1:T(8,128)S(1)} fusion(bf16[32,8,1024]{2,1,0:T(8,128)(2,1)} %bitcast.19, bf16[32,128]{1,0:T(8,128)(2,1)S(1)} %get-tuple-element.29, s32[]{:T(128)S(6)} %select_n.66), kind=kOutput, calls=%fused_computation.4 | convolution fusion | flops 16777216 | bytes 1581060 | tf_op jit(solution)/shard_map/jk,klc->jlc/dot_general | solution.py:573
  114.1 1.8 %fusion.1 = bf16[32,8,1024]{2,0,1:T(8,128)(2,1)S(1)} fusion(f32[32,8,1024]{2,0,1:T(8,128)S(1)} %fusion.2, f32[32,8,1024]{2,0,1:T(8,128)S(1)} %convolution_add_fusion.1, bf16[32,8,1024]{2,1,0:T(8,128)(2,1)} %bitcast.17, bf16[32,128]{1,0:T(8,128)(2,1)S(1)} %get-tuple-element.29, s32[]{:T(128)S(6)} %select_n.64), kind=kOutput, calls=%fused_computation.3 | convolution fusion | flops 17563648 | bytes 3153924 | tf_op jit(solution)/shard_map/jk,klc->jlc/dot_general | solution.py:573
  115.9 1.1 copy.22
  117.0 5.9 %collective-permute-done.11.refs_6_ = bf16[768,256]{1,0:T(8,128)(2,1)S(1)} collective-permute-done((bf16[768,256]{1,0:T(8,128)(2,1)}, bf16[768,256]{1,0:T(8,128)(2,1)S(1)}, u32[]{:S(2)}, u32[]{:S(2)}) %collective-permute-start.11) | collective-permute-done | bytes 393248 | tf_op jit(solution)/shard_map/ppermute | solution.py:39
  122.9 0.8 copy-done.8
  123.7 9.8 %collective-permute-done.12.refs_7_ = bf16[768,256]{1,0:T(8,128)(2,1)} collective-permute-done((bf16[768,256]{1,0:T(8,128)(2,1)S(1)}, bf16[768,256]{1,0:T(8,128)(2,1)}, u32[]{:S(2)}, u32[]{:S(2)}) %collective-permute-start.12) | collective-permute-done | bytes 393248 | tf_op jit(solution)/shard_map/ppermute | solution.py:39
  133.4 3.5 %collective-permute-done.13.refs_8_ = bf16[1280,256]{1,0:T(8,128)(2,1)S(1)} collective-permute-done((bf16[1280,256]{1,0:T(8,128)(2,1)}, bf16[1280,256]{1,0:T(8,128)(2,1)S(1)}, u32[]{:S(2)}, u32[]{:S(2)}) %collective-permute-start.13) | collective-permute-done | bytes 655392 | tf_op jit(solution)/shard_map/ppermute | solution.py:39
  136.9 0.9 copy-done.7
  137.8 22.7 %mix_land.1 = bf16[256,4096]{1,0:T(8,128)(2,1)} custom-call(s32[4]{0:T(128)} %pad_add_fusion.src_ref, s32[64,8]{1,0:T(8,128)} %get-tuple-element.30.start_ref, bf16[1536,256]{1,0:T(8,128)(2,1)} %get-tuple-element.21.refs_0_, bf16[2560,256]{1,0:T(8,128)(2,1)} %get-tuple-element.28.refs_1_, bf16[1536,256]{1,0:T(8,128)(2,1)} %copy-done.6, ...), custom_call_target="tpu_custom_call" | custom-call | tf_op jit(solution)/shard_map/mix_land/pallas_call | solution.py:366
  (29 shorter events, 0.1 us)
Async XLA Ops:
  11.0 33.2 %all-to-all-start = ((bf16[64,34,128]{2,1,0:T(8,128)(2,1)}), bf16[64,34,128]{2,1,0:T(8,128)(2,1)S(1)}, u32[]{:S(2)}, u32[]{:S(2)}) async-start(bf16[64,34,128]{2,1,0:T(8,128)(2,1)} %bucket_tiles.1), calls=%async_computation | async-start | bytes 1310720 | tf_op jit(solution)/shard_map/all_to_all | solution.py:539
  24.2 10.8 %copy-start.10 = (s32[512]{0:T(512)S(1)}, s32[512]{0:T(512)}, u32[]{:S(2)}) copy-start(s32[512]{0:T(512)} %param.17) | copy-start | bytes 6148
  24.2 20.1 %copy-start = (bf16[32,8,1024]{2,1,0:T(8,128)(2,1)S(1)}, bf16[32,8,1024]{2,1,0:T(8,128)(2,1)}, u32[]{:S(2)}) copy-start(bf16[32,8,1024]{2,1,0:T(8,128)(2,1)} %param.10) | copy-start | bytes 1572868
  32.3 31.1 %copy-start.1 = (f32[512]{0:T(512)S(1)}, f32[512]{0:T(512)}, u32[]{:S(2)}) copy-start(f32[512]{0:T(512)} %param.16) | copy-start | bytes 6148
  32.3 31.1 %copy-start.2 = (f32[512]{0:T(512)S(1)}, f32[512]{0:T(512)}, u32[]{:S(2)}) copy-start(f32[512]{0:T(512)} %param.18) | copy-start | bytes 6148
  32.3 20.1 %collective-permute-start = (bf16[1536,256]{1,0:T(8,128)(2,1)}, bf16[1536,256]{1,0:T(8,128)(2,1)S(1)}, u32[]{:S(2)}, u32[]{:S(2)}) collective-permute-start(bf16[1536,256]{1,0:T(8,128)(2,1)} %get-tuple-element.21.refs_0_), channel_id=1, source_target_pairs={{0,1},{1,2},{2,3},{3,0},{4,5},{5,6},{6,7},{7,4},{8,9},{9,10},{10,1... | collective-permute-start | bytes 2359304 | tf_op jit(solution)/shard_map/ppermute | solution.py:39
  33.5 18.9 %collective-permute-start.1 = (bf16[1536,256]{1,0:T(8,128)(2,1)}, bf16[1536,256]{1,0:T(8,128)(2,1)}, u32[]{:S(2)}, u32[]{:S(2)}) collective-permute-start(bf16[1536,256]{1,0:T(8,128)(2,1)} %get-tuple-element.21.refs_0_), channel_id=1, source_target_pairs={{0,3},{1,0},{2,1},{3,2},{4,7},{5,4},{6,5},{7,6},{8,11},{9,8},{10,9... | collective-permute-start | bytes 2359304 | tf_op jit(solution)/shard_map/ppermute | solution.py:39
  47.3 40.3 %copy-start.3 = (s32[1,4]{1,0:T(1,128)S(1)}, s32[1,4]{1,0:T(1,128)}, u32[]{:S(2)}) copy-start(s32[1,4]{1,0:T(1,128)} %list_ref.1) | copy-start | bytes 52
  52.4 41.9 %copy-start.6 = (bf16[1536,256]{1,0:T(8,128)(2,1)}, bf16[1536,256]{1,0:T(8,128)(2,1)S(1)}, u32[]{:S(2)}) copy-start(bf16[1536,256]{1,0:T(8,128)(2,1)S(1)} %collective-permute-done.refs_2_) | copy-start | bytes 2359300
  60.8 41.3 %collective-permute-start.6 = (bf16[2560,256]{1,0:T(8,128)(2,1)}, bf16[2560,256]{1,0:T(8,128)(2,1)S(1)}, u32[]{:S(2)}, u32[]{:S(2)}) collective-permute-start(bf16[2560,256]{1,0:T(8,128)(2,1)} %get-tuple-element.28.refs_1_), channel_id=1, source_target_pairs={{0,1},{1,2},{2,3},{3,0},{4,5},{5,6},{6,7},{7,4},{8,9},{9,10},{10,1... | collective-permute-start | bytes 3932168 | tf_op jit(solution)/shard_map/ppermute | solution.py:39
  61.1 41.7 %collective-permute-start.7 = (bf16[2560,256]{1,0:T(8,128)(2,1)}, bf16[2560,256]{1,0:T(8,128)(2,1)}, u32[]{:S(2)}, u32[]{:S(2)}) collective-permute-start(bf16[2560,256]{1,0:T(8,128)(2,1)} %get-tuple-element.28.refs_1_), channel_id=1, source_target_pairs={{0,3},{1,0},{2,1},{3,2},{4,7},{5,4},{6,5},{7,6},{8,11},{9,8},{10,9... | collective-permute-start | bytes 3932168 | tf_op jit(solution)/shard_map/ppermute | solution.py:39
  63.4 44.7 %collective-permute-start.8 = (bf16[256,1024]{1,0:T(8,128)(2,1)S(1)}, bf16[256,1024]{1,0:T(8,128)(2,1)}, u32[]{:S(2)}, u32[]{:S(2)}) collective-permute-start(bf16[256,1024]{1,0:T(8,128)(2,1)S(1)} %bitcast.36), channel_id=1, source_target_pairs={{0,1},{1,2},{2,3},{3,0},{4,5},{5,6},{6,7},{7,4},{8,9},{9,10},{10,1... | collective-permute-start | bytes 1572872 | tf_op jit(solution)/shard_map/ppermute | solution.py:39
  64.1 9.2 %collective-permute-start.2 = (f32[72,128]{1,0:T(8,128)S(1)}, f32[72,128]{1,0:T(8,128)S(1)}, u32[]{:S(2)}, u32[]{:S(2)}) collective-permute-start(f32[72,128]{1,0:T(8,128)S(1)} %screen_stats.1.own_ref), channel_id=1, source_target_pairs={{0,32},{4,36},{8,40},{12,44},{16,48},{20,52},{24,56},{28,60},{32,6... | collective-permute-start | bytes 110600 | tf_op jit(solution)/shard_map/ppermute | solution.py:39
  69.5 9.5 %collective-permute-start.3 = (f32[72,128]{1,0:T(8,128)S(1)}, f32[72,128]{1,0:T(8,128)S(1)}, u32[]{:S(2)}, u32[]{:S(2)}) collective-permute-start(f32[72,128]{1,0:T(8,128)S(1)} %screen_stats.1.own_ref), channel_id=1, source_target_pairs={{0,224},{4,228},{8,232},{12,236},{16,240},{20,244},{24,248},{28,25... | collective-permute-start | bytes 110600 | tf_op jit(solution)/shard_map/ppermute | solution.py:39
  73.4 11.2 %collective-permute-start.4 = (f32[72,128]{1,0:T(8,128)S(1)}, f32[72,128]{1,0:T(8,128)S(1)}, u32[]{:S(2)}, u32[]{:S(2)}) collective-permute-start(f32[72,128]{1,0:T(8,128)S(1)} %screen_stats.1.own_ref), channel_id=1, source_target_pairs={{0,4},{4,8},{8,12},{12,16},{16,20},{20,24},{24,28},{28,32},{32,36}... | collective-permute-start | bytes 110600 | tf_op jit(solution)/shard_map/ppermute | solution.py:39
  79.0 6.7 %collective-permute-start.5 = (f32[72,128]{1,0:T(8,128)S(1)}, f32[72,128]{1,0:T(8,128)S(1)}, u32[]{:S(2)}, u32[]{:S(2)}) collective-permute-start(f32[72,128]{1,0:T(8,128)S(1)} %screen_stats.1.own_ref), channel_id=1, source_target_pairs={{0,252},{4,0},{8,4},{12,8},{16,12},{20,16},{24,20},{28,24},{32,28}... | collective-permute-start | bytes 110600 | tf_op jit(solution)/shard_map/ppermute | solution.py:39
  84.5 27.0 %collective-permute-start.10 = (bf16[256,1024]{1,0:T(8,128)(2,1)S(1)}, bf16[256,1024]{1,0:T(8,128)(2,1)}, u32[]{:S(2)}, u32[]{:S(2)}) collective-permute-start(bf16[256,1024]{1,0:T(8,128)(2,1)S(1)} %bitcast.37), channel_id=1, source_target_pairs={{0,2},{1,3},{2,0},{3,1},{4,6},{5,7},{6,4},{7,5},{8,10},{9,11},{10,... | collective-permute-start | bytes 1572872 | tf_op jit(solution)/shard_map/ppermute | solution.py:39
  85.7 28.4 %collective-permute-start.9 = (bf16[256,1024]{1,0:T(8,128)(2,1)S(1)}, bf16[256,1024]{1,0:T(8,128)(2,1)}, u32[]{:S(2)}, u32[]{:S(2)}) collective-permute-start(bf16[256,1024]{1,0:T(8,128)(2,1)S(1)} %bitcast.38), channel_id=1, source_target_pairs={{0,3},{1,0},{2,1},{3,2},{4,7},{5,4},{6,5},{7,6},{8,11},{9,8},{10,9... | collective-permute-start | bytes 1572872 | tf_op jit(solution)/shard_map/ppermute | solution.py:39
  94.3 39.1 %all-to-all-start.2 = ((bf16[64,32,128]{2,1,0:T(8,128)(2,1)}), bf16[64,32,128]{2,1,0:T(8,128)(2,1)S(1)}, u32[]{:S(2)}, u32[]{:S(2)}) async-start(bf16[64,32,128]{2,1,0:T(8,128)(2,1)} %get-tuple-element.35), calls=%async_computation.2 | async-start | bytes 1048576 | tf_op jit(solution)/shard_map/all_to_all | solution.py:563
  102.1 5.2 %copy-start.4 = (bf16[2560,256]{1,0:T(8,128)(2,1)}, bf16[2560,256]{1,0:T(8,128)(2,1)S(1)}, u32[]{:S(2)}) copy-start(bf16[2560,256]{1,0:T(8,128)(2,1)S(1)} %collective-permute-done.6.refs_3_) | copy-start | bytes 3932164
  102.1 20.8 %collective-permute-start.11 = (bf16[768,256]{1,0:T(8,128)(2,1)}, bf16[768,256]{1,0:T(8,128)(2,1)S(1)}, u32[]{:S(2)}, u32[]{:S(2)}) collective-permute-start(bf16[768,256]{1,0:T(8,128)(2,1)} %slice.12), channel_id=1, source_target_pairs={{0,1},{1,2},{2,3},{3,0},{4,5},{5,6},{6,7},{7,4},{8,9},{9,10},{10,1... | collective-permute-start | bytes 1179656 | tf_op jit(solution)/shard_map/ppermute | solution.py:39
  103.6 33.3 %collective-permute-start.13 = (bf16[1280,256]{1,0:T(8,128)(2,1)}, bf16[1280,256]{1,0:T(8,128)(2,1)S(1)}, u32[]{:S(2)}, u32[]{:S(2)}) collective-permute-start(bf16[1280,256]{1,0:T(8,128)(2,1)} %slice.14), channel_id=1, source_target_pairs={{0,1},{1,2},{2,3},{3,0},{4,5},{5,6},{6,7},{7,4},{8,9},{9,10},{10,1... | collective-permute-start | bytes 1966088 | tf_op jit(solution)/shard_map/ppermute | solution.py:39
  108.1 28.8 %collective-permute-start.14 = (bf16[1280,256]{1,0:T(8,128)(2,1)}, bf16[1280,256]{1,0:T(8,128)(2,1)}, u32[]{:S(2)}, u32[]{:S(2)}) collective-permute-start(bf16[1280,256]{1,0:T(8,128)(2,1)} %slice.15), channel_id=1, source_target_pairs={{0,3},{1,0},{2,1},{3,2},{4,7},{5,4},{6,5},{7,6},{8,11},{9,8},{10,9... | collective-permute-start | bytes 1966088 | tf_op jit(solution)/shard_map/ppermute | solution.py:39
  109.3 2.2 %copy-start.9 = (bf16[768,256]{1,0:T(8,128)(2,1)S(1)}, bf16[768,256]{1,0:T(8,128)(2,1)}, u32[]{:S(2)}) copy-start(bf16[768,256]{1,0:T(8,128)(2,1)} %slice.13) | copy-start | bytes 1179652
  111.5 21.9 %collective-permute-start.12 = (bf16[768,256]{1,0:T(8,128)(2,1)S(1)}, bf16[768,256]{1,0:T(8,128)(2,1)}, u32[]{:S(2)}, u32[]{:S(2)}) collective-permute-start(bf16[768,256]{1,0:T(8,128)(2,1)S(1)} %copy-done.9), channel_id=1, source_target_pairs={{0,3},{1,0},{2,1},{3,2},{4,7},{5,4},{6,5},{7,6},{8,11},{9,8},{10,9... | collective-permute-start | bytes 1179656 | tf_op jit(solution)/shard_map/ppermute | solution.py:39
  122.9 0.8 copy-start.8
  133.4 3.5 %copy-start.5 = (bf16[64,32,128]{2,1,0:T(8,128)(2,1)}, bf16[64,32,128]{2,1,0:T(8,128)(2,1)S(1)}, u32[]{:S(2)}) copy-start(bf16[64,32,128]{2,1,0:T(8,128)(2,1)S(1)} %all-to-all-done.2) | copy-start | bytes 1572868
  136.9 0.9 copy-start.7

commit v3 on v2

--- a/solution.py
+++ b/solution.py
@@ -155,34 +155,36 @@
     return ((source % b) * a + source // b == target).astype(F32).astype(BF)
 
 
-def sort_land(pos, land_rows, levels, first):
+def sort_land(pos, land_rows, levels, skip, shares):
     width, tiles = land_rows.shape
     span = tiles // PARTS
     block = 512
-
-    def kernel(pos_ref, x_ref, low_ref, high_ref):
+    whole = [sum(shares[:i]) * span for i in range(len(shares))]
+
+    def kernel(pos_ref, x_ref, *out_refs):
         swap = lane_swap(width, width // levels, levels)
-        for c in range(tiles // block):
-            part = c * block // span
-            cut = slice(part * span, (part + 1) * span)
-            place = iota((block, span), 0) + (c * block - part * span)
-            hot = (place == pos_ref[:, cut]).astype(F32).astype(BF)
-            moved = dot(hot, x_ref[:, cut], NT).astype(BF)
-            value = dot(moved, swap).astype(BF)
-            at = c * block
-            if at < first:
-                low_ref[at : at + block, :] = value
-            else:
-                high_ref[at - first : at - first + block, :] = value
-
+        for out_ref, begin in zip(out_refs, whole):
+            for at in range(0, out_ref.shape[0], block):
+                part = (begin + at) // span
+                cut = slice((skip + part) * span, (skip + part + 1) * span)
+                place = iota((block, span), 0) + (begin + at - part * span)
+                hot = (place == pos_ref[:, cut]).astype(F32).astype(BF)
+                moved = dot(hot, x_ref[:, (cut.start - low) : (cut.stop - low)], NT).astype(BF)
+                out_ref[at : at + block, :] = dot(moved, swap).astype(BF)
+
+    count = sum(shares)
+    low = skip * span if skip == 0 else 0
+    taken = (
+        pl.BlockSpec((width, count * span), lambda i: (0, 0))
+        if skip == 0
+        else pl.BlockSpec((width, tiles), lambda i: (0, 0))
+    )
     return pl.pallas_call(
         kernel,
-        out_shape=(
-            jax.ShapeDtypeStruct((first, width), BF),
-            jax.ShapeDtypeStruct((tiles - first, width), BF),
-        ),
-        in_specs=[VMEM, VMEM],
-        out_specs=(VMEM, VMEM),
+        grid=(1,),
+        out_shape=[jax.ShapeDtypeStruct((n * span, width), BF) for n in shares],
+        in_specs=[pl.BlockSpec((1, tiles), lambda i: (0, 0)), taken],
+        out_specs=[pl.BlockSpec((n * span, width), lambda i: (0, 0)) for n in shares],
         compiler_params=params(60),
         name="sort_land",
     )(pos, land_rows)
@@ -224,7 +226,7 @@
     )(received, base_rows, obs_column)
 
 
-def mix_land(pieces, sources, starts, mixes, pos, land_rows, mask_row, levels):
+def mix_land(pieces, ids, starts, mixes, pos, land_rows, mask_row, levels):
     slots = len(pieces)
     flat = [piece for group in pieces for piece in group]
     places = [
@@ -241,7 +243,7 @@
     lanes = 128
     count = len(flat)
 
-    def kernel(src_ref, start_ref, *refs):
+    def kernel(id_ref, start_ref, *refs):
         piece_refs = refs[:count]
         mix_ref, pos_ref, land_ref, mask_ref, out_ref = refs[count : count + 5]
         state_ref, tiled_ref, y_ref, sems = refs[count + 5 :]
@@ -262,7 +264,7 @@
             for s in range(slots):
                 spread = (
                     iota((members, lanes), 0)
-                    == (iota((members, lanes), 1) & (local - 1)) + src_ref[s] * local
+                    == (iota((members, lanes), 1) & (local - 1)) + (id_ref[1] + (0, slots - 1, 1, 2)[s]) % slots * local
                 )
                 tiled_ref[:, s * lanes : (s + 1) * lanes] = dot(
                     mix_ref[...], spread.astype(F32).astype(BF)
@@ -385,7 +387,7 @@
         compiler_params=params(60),
         name="mix_land",
     )(
-        sources,
+        ids,
         starts,
         *flat,
         mixes.reshape(npatch * local, members),
@@ -430,20 +432,21 @@
     )(ensemble, obs_value, obs_error)
 
 
-def settle(own, near, listed, places, local, npatch):
+def settle(own, near, listed, ids, offsets, local, npatch):
     members = own.shape[1]
     half = members // 2
     count = members // local
     names = listed.shape[1]
 
-    def kernel(list_ref, place_ref, own_ref, *refs):
+    def kernel(list_ref, id_ref, own_ref, *refs):
         near_refs = refs[: len(near)]
         cols_ref, out_ref, hold_ref = refs[len(near) :]
         total = own_ref[...]
         for d in range(len(near)):
+            source = (id_ref[0] - offsets[d] + npatch) % npatch
             used = 0
             for i in range(names):
-                used = used + jnp.where(list_ref[0, i] == place_ref[d], 1, 0)
+                used = used + jnp.where(list_ref[0, i] == source, 1, 0)
             total = total + used.astype(F32) * near_refs[d][...]
         packed = total[:half]
         row, lane = iota((half, members), 0), iota((half, members), 1)
@@ -473,7 +476,7 @@
         shift = exact(exact(proj, inv_root, NT), inv_root, NT)[:1]
         spread = shift + math.sqrt(members - 1.0) * inv_root
         hold_ref[...] = spread - jnp.mean(spread, axis=1, keepdims=True) + 1.0 / members
-        mine = hold_ref[pl.ds(pl.multiple_of(place_ref[len(near)] * local, local), local), :]
+        mine = hold_ref[pl.ds(pl.multiple_of(id_ref[1] * local, local), local), :]
         cols_ref[...] = mine.astype(BF)
         flipped = mine.T
         blocks = jnp.concatenate(
@@ -493,7 +496,7 @@
         scratch_shapes=[pltpu.VMEM((members, members), F32)],
         compiler_params=params(16),
         name="settle",
-    )(listed, places, own, *near)
+    )(listed, ids, own, *near)
 
 
 def analysis(
@@ -515,9 +518,8 @@
     layers, tiles = (land.shape[1], land.shape[2])
     bucket = 2 * tiles // npatch
     row_width = max(2, npatch // 8)
-    first = 3 * tiles // 8
     mem_rank = lax.axis_index("mem")
-    patch_rank = lax.axis_index("patch")
+    ids = jnp.stack([lax.axis_index("patch"), mem_rank]).astype(I32)
 
     atmos_rows = atmos.reshape(local * levels, columns)
     atmos_parts = [shifted(atmos_rows, "mem", s) for s in (1, -1, 2)]
@@ -538,35 +540,34 @@
     )
     received = lax.all_to_all(packed, "patch", split_axis=0, concat_axis=0, tiled=True)
 
-    low, high = sort_land(pos, land_rows, layers, first)
-    low_prev = shifted(low, "mem", 1)
-    low_next = shifted(low, "mem", -1)
+    (first,) = sort_land(pos, land_rows, layers, 0, (1,))
+    first_prev = shifted(first, "mem", 1)
+    first_next = shifted(first, "mem", -1)
+    second, rest = sort_land(pos, land_rows, layers, 1, (1, PARTS - 2))
+    second_prev = shifted(second, "mem", 1)
+    second_next = shifted(second, "mem", -1)
 
     forecast = screen_forecast(
         received, atmos_rows, levels, observation_column.reshape(-1, 1), mem_count
     )
-    forecast, low_prev, low_next = barrier((forecast, low_prev, low_next))
+    forecast, first_prev, first_next, second_prev, second_next, rest = barrier(
+        (forecast, first_prev, first_next, second_prev, second_next, rest)
+    )
     ensemble = lax.all_to_all(forecast, "mem", split_axis=0, concat_axis=0, tiled=True)
-    ensemble, high, low_prev, low_next = barrier((ensemble, high, low_prev, low_next))
-    high_prev = shifted(high, "mem", 1)
-    high_next = shifted(high, "mem", -1)
-    low_far = [
-        shifted(low_prev[: first // 2], "mem", 1), shifted(low_next[first // 2 :], "mem", -1)
-    ]
+    rest_prev = shifted(rest, "mem", 1)
+    rest_next = shifted(rest, "mem", -1)
+    first_far = shifted(first_prev, "mem", 1)
+    second_far = shifted(second_prev, "mem", 1)
 
     own_stats = screen_stats(ensemble, obs_value.reshape(1, -1), obs_error.reshape(1, -1))
     offsets = (row_width, -row_width, 1, -1)
     near = [shifted(own_stats, "patch", o) for o in offsets]
-    places = [(patch_rank - o) % npatch for o in offsets]
-    places = jnp.stack(places + [mem_rank]).astype(I32)
-    own_cols, mixes = settle(own_stats, near, loc_blocks, places, local, npatch)
+    own_cols, mixes = settle(own_stats, near, loc_blocks, ids, offsets, local, npatch)
+    own_cols, rest_next = barrier((own_cols, rest_next))
+    rest_far = shifted(rest_next, "mem", -1)
     all_mixes = lax.all_to_all(mixes, "patch", split_axis=0, concat_axis=0, tiled=True)
-    own_cols, high_prev, high_next = barrier((own_cols, high_prev, high_next))
-    split = high.shape[0] // 2
-    high_far = [shifted(high_prev[:split], "mem", 1), shifted(high_next[split:], "mem", -1)]
 
     slot_source = [mem_rank, mem_rank - 1, mem_rank + 1, mem_rank - 2]
-    sources = jnp.stack([s % mem_count for s in slot_source]).astype(I32)
     atmos_out = 0.0
     for part, source in zip([atmos_rows] + atmos_parts, slot_source):
         rows = lax.dynamic_slice_in_dim(own_cols, (source % mem_count) * local, local, 1)
@@ -576,8 +577,13 @@
     atmos_analysis = atmos_out.astype(BF)
 
     land_out = mix_land(
-        [[low, high], [low_prev, high_prev], [low_next, high_next], low_far + high_far],
-        sources,
+        [
+            [first, second, rest],
+            [first_prev, second_prev, rest_prev],
+            [first_next, second_next, rest_next],
+            [first_far, second_far, rest_far],
+        ],
+        ids,
         starts,
         all_mixes,
         pos,

time: 163 us -> 181 us (1.11)
  blocking collectives: 8.38 us -> 21.8 us
  waiting for transfers between devices: 35.1 us -> 41.7 us
  local copies, waits for them, and re-layouts: 8.44 us -> 2.95 us
  starting transfers between devices: 49.3 us -> 52.6 us
  Pallas kernels: 50.3 us -> 52.2 us
    all_to_all x1, blocking collectives: 8.38 us -> 21.8 us  [analysis(): lax.all_to_all(forecast, 'mem', split_axis=0, concat_axis=0, tiled=True)]
    ppermute x15 -> x16, waiting for transfers between devices: 25.9 us -> 37.3 us  [shifted(): return lax.ppermute(value, axis, pairs)]
    slice x4 -> x0, local copies, waits for them, and re-layouts: 5.44 us -> none  [the longest x1 1.98 us: analysis(): high_next[split:]]
    all_to_all x1, waiting for transfers between devices: 9.13 us -> 4.42 us  [analysis(): lax.all_to_all(packed, 'patch', split_axis=0, concat_axis=0, tiled=True)]
    all_to_all x1, starting transfers between devices: 7.77 us -> 10.5 us  [analysis(): lax.all_to_all(mixes, 'patch', split_axis=0, concat_axis=0, tiled=True)]
    pallas_call x1 -> x2, Pallas kernels: 8.1 us -> 10.1 us  [sort_land(): pl.pallas_call(kernel, grid=(1,), out_shape=[jax.ShapeDtypeStruct((n * sp...]
    ppermute x15 -> x16, starting transfers between devices: 28.4 us -> 28.9 us  [shifted(): return lax.ppermute(value, axis, pairs)]
  transfers between devices with their start and end apart: 17 -> 18, of which waited for: 7 -> 4; matrix products, arithmetic and copies ran while one was open for 9% -> 4% of each run, Pallas kernels for 11% -> 11%
where the time goes in v3:
time: 181 us; the launch traced here: 180 us
  starting transfers between devices  52.6 us (29%)
  Pallas kernels  52.2 us (29%)
  waiting for transfers between devices  41.7 us (23%)
  blocking collectives  21.8 us (12%)
  matrix products  6.25 us (3%)
  local copies, waits for them, and re-layouts  2.95 us (2%)
    ppermute x16, waiting for transfers between devices, shifted(): return lax.ppermute(value, axis, pairs)  37.3 us
    ppermute x16, starting transfers between devices, shifted(): return lax.ppermute(value, axis, pairs)  28.9 us
    pallas_call x1, Pallas kernels, mix_land(): pl.pallas_call(kernel, grid=(PARTS,), out_shape=jax.ShapeDtypeStruct((wid...  22.8 us
    all_to_all x1, blocking collectives, analysis(): lax.all_to_all(forecast, 'mem', split_axis=0, concat_axis=0, tiled=True)  21.8 us
    all_to_all x1, starting transfers between devices, analysis(): lax.all_to_all(packed, 'patch', split_axis=0, concat_axis=0, tiled=True)  13.1 us
    all_to_all x1, starting transfers between devices, analysis(): lax.all_to_all(mixes, 'patch', split_axis=0, concat_axis=0, tiled=True)  10.5 us
    pallas_call x2, Pallas kernels, sort_land(): pl.pallas_call(kernel, grid=(1,), out_shape=[jax.ShapeDtypeStruct((n * sp...  10.1 us
    pallas_call x1, Pallas kernels, bucket_tiles(): pl.pallas_call(kernel, grid=(steps,), out_shape=jax.ShapeDtypeStruct((npa...  6.76 us
  transfers between devices with their start and end apart: 18, of which 4 were waited for; matrix products, arithmetic and copies ran while one was open for 4% of the time, Pallas kernels for 11%

profile of v3, /device:TPU:1, one launch (start us, length us, event | category | flops | bytes accessed | tf_op | source)
XLA Modules:
  0.0 180.0 jit_solution(1176262447826419532)
XLA Ops:
  0.6 2.3 %order_tiles.1 = (s32[1,4096]{1,0:T(1,128)}, s32[1,4096]{1,0:T(1,128)}, s32[64,8]{1,0:T(8,128)}) custom-call(s32[1,4096]{1,0:T(1,128)} %bitcast.40), custom_call_target="tpu_custom_call" | custom-call | tf_op jit(solution)/shard_map/order_tiles/pallas_call | solution.py:75
  2.9 1.3 convert_multiply_fusion
  4.3 6.8 %bucket_tiles.1 = bf16[64,34,128]{2,1,0:T(8,128)(2,1)} custom-call(bf16[256,4096]{1,0:T(8,128)(2,1)} %bitcast.34, f32[1,4096]{1,0:T(1,128)} %bitcast.43, s32[1,4096]{1,0:T(1,128)} %bitcast.41, s32[1,4096]{1,0:T(1,128)} %get-tuple-element.17.rank_ref, s32[1,4096]{1,0:T(1,128)} %bitcast.44), custom_call_target="tpu_custom_call" | custom-call | tf_op jit(solution)/shard_map/bucket_tiles/pallas_call | solution.py:137
  11.0 13.1 %all-to-all-start = ((bf16[64,34,128]{2,1,0:T(8,128)(2,1)}), bf16[64,34,128]{2,1,0:T(8,128)(2,1)S(1)}, u32[]{:S(2)}, u32[]{:S(2)}) async-start(bf16[64,34,128]{2,1,0:T(8,128)(2,1)} %bucket_tiles.1), calls=%async_computation | async-start | bytes 1310720 | tf_op jit(solution)/shard_map/all_to_all | solution.py:541
  24.2 0.0 copy-start.10
  24.2 0.0 copy-start
  24.2 6.7 %sort_land.3 = (bf16[1024,256]{1,0:T(8,128)(2,1)}, bf16[2048,256]{1,0:T(8,128)(2,1)}) custom-call(s32[1,4096]{1,0:T(1,128)} %get-tuple-element.18.pos_ref.refs_13_, bf16[256,4096]{1,0:T(8,128)(2,1)} %bitcast.35), custom_call_target="tpu_custom_call" | custom-call | tf_op jit(solution)/shard_map/sort_land/pallas_call | solution.py:182
  30.9 1.3 collective-permute-start.2
  32.2 1.5 collective-permute-start.3
  33.6 3.4 %sort_land.2.refs_0_ = bf16[1024,256]{1,0:T(8,128)(2,1)} custom-call(s32[1,4096]{1,0:T(1,128)} %get-tuple-element.18.pos_ref.refs_13_, bf16[256,4096]{1,0:T(8,128)(2,1)} %bitcast.36), custom_call_target="tpu_custom_call" | custom-call | tf_op jit(solution)/shard_map/sort_land/pallas_call | solution.py:182
  37.0 0.0 collective-permute-start
  37.0 2.7 %collective-permute-start.1 = (bf16[1024,256]{1,0:T(8,128)(2,1)}, bf16[1024,256]{1,0:T(8,128)(2,1)}, u32[]{:S(2)}, u32[]{:S(2)}) collective-permute-start(bf16[1024,256]{1,0:T(8,128)(2,1)} %sort_land.2.refs_0_), channel_id=1, source_target_pairs={{0,3},{1,0},{2,1},{3,2},{4,7},{5,4},{6,5},{7,6},{8,11},{9,8},{10,9... | collective-permute-start | bytes 1572872 | tf_op jit(solution)/shard_map/ppermute | solution.py:39
  39.7 0.1 copy.17.obs_ref
  39.9 4.4 %all-to-all-done.in_ref = bf16[64,34,128]{2,1,0:T(8,128)(2,1)S(1)} async-done(((bf16[64,34,128]{2,1,0:T(8,128)(2,1)}), bf16[64,34,128]{2,1,0:T(8,128)(2,1)S(1)}, u32[]{:S(2)}, u32[]{:S(2)}) %all-to-all-start) | async-done | bytes 557088 | tf_op jit(solution)/shard_map/all_to_all | solution.py:541
  44.3 3.0 %screen_forecast.1 = bf16[4,32,512]{2,1,0:T(8,128)(2,1)S(1)} custom-call(bf16[64,34,128]{2,1,0:T(8,128)(2,1)S(1)} %all-to-all-done.in_ref, bf16[256,1024]{1,0:T(8,128)(2,1)S(1)} %bitcast.28, s32[512,1]{1,0:T(8,128)S(1)} %copy.17.obs_ref), custom_call_target="tpu_custom_call" | custom-call | tf_op jit(solution)/shard_map/screen_forecast/pallas_call | solution.py:219
  47.3 0.0 collective-permute-done.2.refs_4_
  47.3 0.0 collective-permute-done.3.refs_7_
  47.3 9.5 %collective-permute-done.refs_3_ = bf16[1024,256]{1,0:T(8,128)(2,1)} collective-permute-done((bf16[1024,256]{1,0:T(8,128)(2,1)}, bf16[1024,256]{1,0:T(8,128)(2,1)}, u32[]{:S(2)}, u32[]{:S(2)}) %collective-permute-start) | collective-permute-done | bytes 524320 | tf_op jit(solution)/shard_map/ppermute | solution.py:39
  56.8 0.0 collective-permute-done.1.refs_6_
  56.8 2.4 %collective-permute-start.8 = (bf16[2048,256]{1,0:T(8,128)(2,1)S(1)}, bf16[2048,256]{1,0:T(8,128)(2,1)}, u32[]{:S(2)}, u32[]{:S(2)}) collective-permute-start(bf16[2048,256]{1,0:T(8,128)(2,1)S(1)} %copy-done.6), channel_id=1, source_target_pairs={{0,3},{1,0},{2,1},{3,2},{4,7},{5,4},{6,5},{7,6},{8,11},{9,8},{10,9... | collective-permute-start | bytes 3145736 | tf_op jit(solution)/shard_map/ppermute | solution.py:39
  59.2 21.8 %all_to_all.15.in_ref = bf16[4,32,512]{2,1,0:T(8,128)(2,1)S(1)} all-to-all(bf16[4,32,512]{2,1,0:T(8,128)(2,1)S(1)} %screen_forecast.1), channel_id=1, replica_groups=mesh['patch'=64,'mem'=4] {'mem'}, dimensions={0} | all-to-all | bytes 262144 | tf_op jit(solution)/shard_map/all_to_all | solution.py:556
  81.0 0.6 screen_stats.1.own_ref
  81.7 5.5 %collective-permute-start.4 = (f32[72,128]{1,0:T(8,128)S(1)}, f32[72,128]{1,0:T(8,128)S(1)}, u32[]{:S(2)}, u32[]{:S(2)}) collective-permute-start(f32[72,128]{1,0:T(8,128)S(1)} %screen_stats.1.own_ref), channel_id=1, source_target_pairs={{0,32},{4,36},{8,40},{12,44},{16,48},{20,52},{24,56},{28,60},{32,6... | collective-permute-start | bytes 110600 | tf_op jit(solution)/shard_map/ppermute | solution.py:39
  87.1 2.5 %collective-permute-start.5 = (f32[72,128]{1,0:T(8,128)S(1)}, f32[72,128]{1,0:T(8,128)S(1)}, u32[]{:S(2)}, u32[]{:S(2)}) collective-permute-start(f32[72,128]{1,0:T(8,128)S(1)} %screen_stats.1.own_ref), channel_id=1, source_target_pairs={{0,224},{4,228},{8,232},{12,236},{16,240},{20,244},{24,248},{28,25... | collective-permute-start | bytes 110600 | tf_op jit(solution)/shard_map/ppermute | solution.py:39
  89.6 4.4 %collective-permute-start.6 = (f32[72,128]{1,0:T(8,128)S(1)}, f32[72,128]{1,0:T(8,128)S(1)}, u32[]{:S(2)}, u32[]{:S(2)}) collective-permute-start(f32[72,128]{1,0:T(8,128)S(1)} %screen_stats.1.own_ref), channel_id=1, source_target_pairs={{0,4},{4,8},{8,12},{12,16},{16,20},{20,24},{24,28},{28,32},{32,36}... | collective-permute-start | bytes 110600 | tf_op jit(solution)/shard_map/ppermute | solution.py:39
  94.1 1.0 collective-permute-start.7
  95.1 0.1 pad_add_fusion.id_ref
  95.2 1.3 collective-permute-start.11
  96.5 2.1 %collective-permute-start.10 = (bf16[256,1024]{1,0:T(8,128)(2,1)S(1)}, bf16[256,1024]{1,0:T(8,128)(2,1)}, u32[]{:S(2)}, u32[]{:S(2)}) collective-permute-start(bf16[256,1024]{1,0:T(8,128)(2,1)S(1)} %bitcast.31), channel_id=1, source_target_pairs={{0,3},{1,0},{2,1},{3,2},{4,7},{5,4},{6,5},{7,6},{8,11},{9,8},{10,9... | collective-permute-start | bytes 1572872 | tf_op jit(solution)/shard_map/ppermute | solution.py:39
  98.6 0.7 collective-permute-start.12
  99.3 6.7 %settle.1 = (bf16[32,128]{1,0:T(8,128)(2,1)S(1)}, bf16[64,32,128]{2,1,0:T(8,128)(2,1)}) custom-call(s32[1,4]{1,0:T(1,128)S(1)} %copy-done.4, s32[2]{0:T(128)S(1)} %pad_add_fusion.id_ref, f32[72,128]{1,0:T(8,128)S(1)} %screen_stats.1.own_ref, f32[72,128]{1,0:T(8,128)S(1)} %collective-permute-done.4.refs_0_, f32[72,128]{1,0:T(8,128)S(1)} %collective-permute-done.5.refs_1_, ...), custom_call_target="tpu_custom_call" | custom-call | tf_op jit(solution)/shard_map/settle/pallas_call | solution.py:488
  106.0 10.5 %all-to-all-start.2 = ((bf16[64,32,128]{2,1,0:T(8,128)(2,1)}), bf16[64,32,128]{2,1,0:T(8,128)(2,1)S(1)}, u32[]{:S(2)}, u32[]{:S(2)}) async-start(bf16[64,32,128]{2,1,0:T(8,128)(2,1)} %get-tuple-element.31), calls=%async_computation.2 | async-start | bytes 1048576 | tf_op jit(solution)/shard_map/all_to_all | solution.py:568
  116.6 2.7 %collective-permute-start.15 = (bf16[2048,256]{1,0:T(8,128)(2,1)}, bf16[2048,256]{1,0:T(8,128)(2,1)}, u32[]{:S(2)}, u32[]{:S(2)}) collective-permute-start(bf16[2048,256]{1,0:T(8,128)(2,1)} %collective-permute-done.8.refs_8_), channel_id=1, source_target_pairs={{0,3},{1,0},{2,1},{3,2},{4,7},{5,4},{6,5},{7,6},{8,11},{9,8},{10,9... | collective-permute-start | bytes 3145736 | tf_op jit(solution)/shard_map/ppermute | solution.py:39
  119.3 0.8 fusion.6
  120.1 0.0 collective-permute-done.9
  120.1 0.3 collective-permute-start.13
  120.4 1.8 %convolution_add_fusion.1 = f32[32,8,1024]{2,0,1:T(8,128)S(1)} fusion(f32[32,8,1024]{2,0,1:T(8,128)S(1)} %fusion.6, bf16[32,8,1024]{2,1,0:T(8,128)(2,1)} %bitcast.12, bf16[32,128]{1,0:T(8,128)(2,1)S(1)} %get-tuple-element.24, s32[]{:T(128)S(6)} %select_n.34), kind=kOutput, calls=%fused_computation.2 | convolution fusion | flops 17039360 | bytes 2629636 | tf_op jit(solution)/shard_map/jk,klc->jlc/dot_general | solution.py:574
  122.3 0.5 collective-permute-start.14
  122.8 1.8 %fusion.2 = f32[32,8,1024]{2,0,1:T(8,128)S(1)} fusion(bf16[32,8,1024]{2,1,0:T(8,128)(2,1)} %bitcast.16, bf16[32,128]{1,0:T(8,128)(2,1)S(1)} %get-tuple-element.24, s32[]{:T(128)S(6)} %select_n.38), kind=kOutput, calls=%fused_computation.4 | convolution fusion | flops 16777216 | bytes 1581060 | tf_op jit(solution)/shard_map/jk,klc->jlc/dot_general | solution.py:574
  124.6 0.0 collective-permute-done.10
  124.6 1.8 %fusion.1 = bf16[32,8,1024]{2,0,1:T(8,128)(2,1)S(1)} fusion(f32[32,8,1024]{2,0,1:T(8,128)S(1)} %fusion.2, f32[32,8,1024]{2,0,1:T(8,128)S(1)} %convolution_add_fusion.1, bf16[32,8,1024]{2,1,0:T(8,128)(2,1)} %bitcast.14, bf16[32,128]{1,0:T(8,128)(2,1)S(1)} %get-tuple-element.24, s32[]{:T(128)S(6)} %select_n.36), kind=kOutput, calls=%fused_computation.3 | convolution fusion | flops 17563648 | bytes 3153924 | tf_op jit(solution)/shard_map/jk,klc->jlc/dot_general | solution.py:574
  126.5 1.1 copy.22
  127.5 16.5 %collective-permute-done.13.refs_9_ = bf16[1024,256]{1,0:T(8,128)(2,1)S(1)} collective-permute-done((bf16[1024,256]{1,0:T(8,128)(2,1)}, bf16[1024,256]{1,0:T(8,128)(2,1)S(1)}, u32[]{:S(2)}, u32[]{:S(2)}) %collective-permute-start.13) | collective-permute-done | bytes 524320 | tf_op jit(solution)/shard_map/ppermute | solution.py:39
  144.1 11.2 %collective-permute-done.14.refs_10_ = bf16[1024,256]{1,0:T(8,128)(2,1)S(1)} collective-permute-done((bf16[1024,256]{1,0:T(8,128)(2,1)S(1)}, bf16[1024,256]{1,0:T(8,128)(2,1)S(1)}, u32[]{:S(2)}, u32[]{:S(2)}) %collective-permute-start.14) | collective-permute-done | bytes 524320 | tf_op jit(solution)/shard_map/ppermute | solution.py:39
  155.3 0.8 copy-done.9
  156.2 0.0 collective-permute-done.12.refs_5_
  156.2 0.8 copy-done.5
  157.0 22.8 %mix_land.1 = bf16[256,4096]{1,0:T(8,128)(2,1)} custom-call(s32[2]{0:T(128)} %copy-done.3, s32[64,8]{1,0:T(8,128)} %get-tuple-element.25.start_ref, bf16[1024,256]{1,0:T(8,128)(2,1)} %sort_land.2.refs_0_, bf16[1024,256]{1,0:T(8,128)(2,1)} %get-tuple-element.19.refs_1_, bf16[2048,256]{1,0:T(8,128)(2,1)} %get-tuple-element.23.refs_2_, ...), custom_call_target="tpu_custom_call" | custom-call | tf_op jit(solution)/shard_map/mix_land/pallas_call | solution.py:368
  (27 shorter events, 0.1 us)
Async XLA Ops:
  11.0 33.2 %all-to-all-start = ((bf16[64,34,128]{2,1,0:T(8,128)(2,1)}), bf16[64,34,128]{2,1,0:T(8,128)(2,1)S(1)}, u32[]{:S(2)}, u32[]{:S(2)}) async-start(bf16[64,34,128]{2,1,0:T(8,128)(2,1)} %bucket_tiles.1), calls=%async_computation | async-start | bytes 1310720 | tf_op jit(solution)/shard_map/all_to_all | solution.py:541
  24.2 15.5 %copy-start.10 = (s32[512]{0:T(512)S(1)}, s32[512]{0:T(512)}, u32[]{:S(2)}) copy-start(s32[512]{0:T(512)} %param.17) | copy-start | bytes 6148
  24.2 20.1 %copy-start = (bf16[32,8,1024]{2,1,0:T(8,128)(2,1)S(1)}, bf16[32,8,1024]{2,1,0:T(8,128)(2,1)}, u32[]{:S(2)}) copy-start(bf16[32,8,1024]{2,1,0:T(8,128)(2,1)} %param.10) | copy-start | bytes 1572868
  30.9 25.9 %copy-start.6 = (bf16[2048,256]{1,0:T(8,128)(2,1)S(1)}, bf16[2048,256]{1,0:T(8,128)(2,1)}, u32[]{:S(2)}) copy-start(bf16[2048,256]{1,0:T(8,128)(2,1)} %get-tuple-element.23.refs_2_) | copy-start | bytes 3145732
  30.9 50.1 %copy-start.1 = (f32[512]{0:T(512)S(1)}, f32[512]{0:T(512)}, u32[]{:S(2)}) copy-start(f32[512]{0:T(512)} %param.16) | copy-start | bytes 6148
  30.9 50.1 %copy-start.2 = (f32[512]{0:T(512)S(1)}, f32[512]{0:T(512)}, u32[]{:S(2)}) copy-start(f32[512]{0:T(512)} %param.18) | copy-start | bytes 6148
  30.9 68.4 %copy-start.4 = (s32[1,4]{1,0:T(1,128)S(1)}, s32[1,4]{1,0:T(1,128)}, u32[]{:S(2)}) copy-start(s32[1,4]{1,0:T(1,128)} %list_ref.1) | copy-start | bytes 52
  30.9 16.4 %collective-permute-start.2 = (bf16[1024,256]{1,0:T(8,128)(2,1)}, bf16[1024,256]{1,0:T(8,128)(2,1)S(1)}, u32[]{:S(2)}, u32[]{:S(2)}) collective-permute-start(bf16[1024,256]{1,0:T(8,128)(2,1)} %get-tuple-element.19.refs_1_), channel_id=1, source_target_pairs={{0,1},{1,2},{2,3},{3,0},{4,5},{5,6},{6,7},{7,4},{8,9},{9,10},{10,1... | collective-permute-start | bytes 1572872 | tf_op jit(solution)/shard_map/ppermute | solution.py:39
  32.2 15.1 %collective-permute-start.3 = (bf16[1024,256]{1,0:T(8,128)(2,1)}, bf16[1024,256]{1,0:T(8,128)(2,1)}, u32[]{:S(2)}, u32[]{:S(2)}) collective-permute-start(bf16[1024,256]{1,0:T(8,128)(2,1)} %get-tuple-element.19.refs_1_), channel_id=1, source_target_pairs={{0,3},{1,0},{2,1},{3,2},{4,7},{5,4},{6,5},{7,6},{8,11},{9,8},{10,9... | collective-permute-start | bytes 1572872 | tf_op jit(solution)/shard_map/ppermute | solution.py:39
  37.0 19.7 %collective-permute-start = (bf16[1024,256]{1,0:T(8,128)(2,1)}, bf16[1024,256]{1,0:T(8,128)(2,1)}, u32[]{:S(2)}, u32[]{:S(2)}) collective-permute-start(bf16[1024,256]{1,0:T(8,128)(2,1)} %sort_land.2.refs_0_), channel_id=1, source_target_pairs={{0,1},{1,2},{2,3},{3,0},{4,5},{5,6},{6,7},{7,4},{8,9},{9,10},{10,1... | collective-permute-start | bytes 1572872 | tf_op jit(solution)/shard_map/ppermute | solution.py:39
  37.0 19.7 %collective-permute-start.1 = (bf16[1024,256]{1,0:T(8,128)(2,1)}, bf16[1024,256]{1,0:T(8,128)(2,1)}, u32[]{:S(2)}, u32[]{:S(2)}) collective-permute-start(bf16[1024,256]{1,0:T(8,128)(2,1)} %sort_land.2.refs_0_), channel_id=1, source_target_pairs={{0,3},{1,0},{2,1},{3,2},{4,7},{5,4},{6,5},{7,6},{8,11},{9,8},{10,9... | collective-permute-start | bytes 1572872 | tf_op jit(solution)/shard_map/ppermute | solution.py:39
  47.3 75.0 %copy-start.7 = (bf16[1024,256]{1,0:T(8,128)(2,1)}, bf16[1024,256]{1,0:T(8,128)(2,1)S(1)}, u32[]{:S(2)}) copy-start(bf16[1024,256]{1,0:T(8,128)(2,1)S(1)} %collective-permute-done.2.refs_4_) | copy-start | bytes 1572868
  56.8 59.8 %collective-permute-start.8 = (bf16[2048,256]{1,0:T(8,128)(2,1)S(1)}, bf16[2048,256]{1,0:T(8,128)(2,1)}, u32[]{:S(2)}, u32[]{:S(2)}) collective-permute-start(bf16[2048,256]{1,0:T(8,128)(2,1)S(1)} %copy-done.6), channel_id=1, source_target_pairs={{0,3},{1,0},{2,1},{3,2},{4,7},{5,4},{6,5},{7,6},{8,11},{9,8},{10,9... | collective-permute-start | bytes 3145736 | tf_op jit(solution)/shard_map/ppermute | solution.py:39
  59.2 60.9 %collective-permute-start.9 = (bf16[256,1024]{1,0:T(8,128)(2,1)S(1)}, bf16[256,1024]{1,0:T(8,128)(2,1)}, u32[]{:S(2)}, u32[]{:S(2)}) collective-permute-start(bf16[256,1024]{1,0:T(8,128)(2,1)S(1)} %bitcast.29), channel_id=1, source_target_pairs={{0,1},{1,2},{2,3},{3,0},{4,5},{5,6},{6,7},{7,4},{8,9},{9,10},{10,1... | collective-permute-start | bytes 1572872 | tf_op jit(solution)/shard_map/ppermute | solution.py:39
  81.7 12.4 %collective-permute-start.4 = (f32[72,128]{1,0:T(8,128)S(1)}, f32[72,128]{1,0:T(8,128)S(1)}, u32[]{:S(2)}, u32[]{:S(2)}) collective-permute-start(f32[72,128]{1,0:T(8,128)S(1)} %screen_stats.1.own_ref), channel_id=1, source_target_pairs={{0,32},{4,36},{8,40},{12,44},{16,48},{20,52},{24,56},{28,60},{32,6... | collective-permute-start | bytes 110600 | tf_op jit(solution)/shard_map/ppermute | solution.py:39
  87.1 8.1 %collective-permute-start.5 = (f32[72,128]{1,0:T(8,128)S(1)}, f32[72,128]{1,0:T(8,128)S(1)}, u32[]{:S(2)}, u32[]{:S(2)}) collective-permute-start(f32[72,128]{1,0:T(8,128)S(1)} %screen_stats.1.own_ref), channel_id=1, source_target_pairs={{0,224},{4,228},{8,232},{12,236},{16,240},{20,244},{24,248},{28,25... | collective-permute-start | bytes 110600 | tf_op jit(solution)/shard_map/ppermute | solution.py:39
  89.6 6.9 %collective-permute-start.6 = (f32[72,128]{1,0:T(8,128)S(1)}, f32[72,128]{1,0:T(8,128)S(1)}, u32[]{:S(2)}, u32[]{:S(2)}) collective-permute-start(f32[72,128]{1,0:T(8,128)S(1)} %screen_stats.1.own_ref), channel_id=1, source_target_pairs={{0,4},{4,8},{8,12},{12,16},{16,20},{20,24},{24,28},{28,32},{32,36}... | collective-permute-start | bytes 110600 | tf_op jit(solution)/shard_map/ppermute | solution.py:39
  94.1 4.6 %collective-permute-start.7 = (f32[72,128]{1,0:T(8,128)S(1)}, f32[72,128]{1,0:T(8,128)S(1)}, u32[]{:S(2)}, u32[]{:S(2)}) collective-permute-start(f32[72,128]{1,0:T(8,128)S(1)} %screen_stats.1.own_ref), channel_id=1, source_target_pairs={{0,252},{4,0},{8,4},{12,8},{16,12},{20,16},{24,20},{28,24},{32,28}... | collective-permute-start | bytes 110600 | tf_op jit(solution)/shard_map/ppermute | solution.py:39
  95.2 27.1 %copy-start.3 = (s32[2]{0:T(128)}, s32[2]{0:T(128)S(1)}, u32[]{:S(2)}) copy-start(s32[2]{0:T(128)S(1)} %pad_add_fusion.id_ref) | copy-start | bytes 28
  95.2 27.1 %collective-permute-start.11 = (bf16[256,1024]{1,0:T(8,128)(2,1)S(1)}, bf16[256,1024]{1,0:T(8,128)(2,1)}, u32[]{:S(2)}, u32[]{:S(2)}) collective-permute-start(bf16[256,1024]{1,0:T(8,128)(2,1)S(1)} %bitcast.30), channel_id=1, source_target_pairs={{0,2},{1,3},{2,0},{3,1},{4,6},{5,7},{6,4},{7,5},{8,10},{9,11},{10,... | collective-permute-start | bytes 1572872 | tf_op jit(solution)/shard_map/ppermute | solution.py:39
  96.5 28.1 %collective-permute-start.10 = (bf16[256,1024]{1,0:T(8,128)(2,1)S(1)}, bf16[256,1024]{1,0:T(8,128)(2,1)}, u32[]{:S(2)}, u32[]{:S(2)}) collective-permute-start(bf16[256,1024]{1,0:T(8,128)(2,1)S(1)} %bitcast.31), channel_id=1, source_target_pairs={{0,3},{1,0},{2,1},{3,2},{4,7},{5,4},{6,5},{7,6},{8,11},{9,8},{10,9... | collective-permute-start | bytes 1572872 | tf_op jit(solution)/shard_map/ppermute | solution.py:39
  98.6 57.5 %collective-permute-start.12 = (bf16[2048,256]{1,0:T(8,128)(2,1)S(1)}, bf16[2048,256]{1,0:T(8,128)(2,1)}, u32[]{:S(2)}, u32[]{:S(2)}) collective-permute-start(bf16[2048,256]{1,0:T(8,128)(2,1)S(1)} %copy-done.6), channel_id=1, source_target_pairs={{0,1},{1,2},{2,3},{3,0},{4,5},{5,6},{6,7},{7,4},{8,9},{9,10},{10,1... | collective-permute-start | bytes 3145736 | tf_op jit(solution)/shard_map/ppermute | solution.py:39
  106.0 50.2 %all-to-all-start.2 = ((bf16[64,32,128]{2,1,0:T(8,128)(2,1)}), bf16[64,32,128]{2,1,0:T(8,128)(2,1)S(1)}, u32[]{:S(2)}, u32[]{:S(2)}) async-start(bf16[64,32,128]{2,1,0:T(8,128)(2,1)} %get-tuple-element.31), calls=%async_computation.2 | async-start | bytes 1048576 | tf_op jit(solution)/shard_map/all_to_all | solution.py:568
  116.6 39.6 %collective-permute-start.15 = (bf16[2048,256]{1,0:T(8,128)(2,1)}, bf16[2048,256]{1,0:T(8,128)(2,1)}, u32[]{:S(2)}, u32[]{:S(2)}) collective-permute-start(bf16[2048,256]{1,0:T(8,128)(2,1)} %collective-permute-done.8.refs_8_), channel_id=1, source_target_pairs={{0,3},{1,0},{2,1},{3,2},{4,7},{5,4},{6,5},{7,6},{8,11},{9,8},{10,9... | collective-permute-start | bytes 3145736 | tf_op jit(solution)/shard_map/ppermute | solution.py:39
  120.1 24.0 %collective-permute-start.13 = (bf16[1024,256]{1,0:T(8,128)(2,1)}, bf16[1024,256]{1,0:T(8,128)(2,1)S(1)}, u32[]{:S(2)}, u32[]{:S(2)}) collective-permute-start(bf16[1024,256]{1,0:T(8,128)(2,1)} %collective-permute-done.refs_3_), channel_id=1, source_target_pairs={{0,1},{1,2},{2,3},{3,0},{4,5},{5,6},{6,7},{7,4},{8,9},{9,10},{10,1... | collective-permute-start | bytes 1572872 | tf_op jit(solution)/shard_map/ppermute | solution.py:39
  122.3 33.0 %collective-permute-start.14 = (bf16[1024,256]{1,0:T(8,128)(2,1)S(1)}, bf16[1024,256]{1,0:T(8,128)(2,1)S(1)}, u32[]{:S(2)}, u32[]{:S(2)}) collective-permute-start(bf16[1024,256]{1,0:T(8,128)(2,1)S(1)} %collective-permute-done.2.refs_4_), channel_id=1, source_target_pairs={{0,1},{1,2},{2,3},{3,0},{4,5},{5,6},{6,7},{7,4},{8,9},{9,10},{10,1... | collective-permute-start | bytes 1572872 | tf_op jit(solution)/shard_map/ppermute | solution.py:39
  144.1 11.2 %copy-start.8 = (bf16[1024,256]{1,0:T(8,128)(2,1)}, bf16[1024,256]{1,0:T(8,128)(2,1)S(1)}, u32[]{:S(2)}) copy-start(bf16[1024,256]{1,0:T(8,128)(2,1)S(1)} %collective-permute-done.13.refs_9_) | copy-start | bytes 1572868
  155.3 0.9 copy-start.9
  156.2 0.8 copy-start.5

commit v4 on v3

--- a/solution.py
+++ b/solution.py
@@ -86,7 +86,7 @@
     )(owners)
 
 
-def bucket_tiles(land_rows, levels, weight, owners, ranks, columns, npatch, bucket):
+def bucket_tiles(land_rows, levels, weight, mask, owners, ranks, columns, npatch, bucket):
     width, tiles = land_rows.shape
     rows = width // levels
     low = 4
@@ -95,7 +95,16 @@
     steps = tiles // block
 
     def kernel(
-        x_ref, weight_ref, owner_ref, rank_ref, col_ref, out_ref, acc_ref, cacc_ref
+        x_ref,
+        weight_ref,
+        mask_ref,
+        owner_ref,
+        rank_ref,
+        col_ref,
+        out_ref,
+        acc_ref,
+        cacc_ref,
+        keep_ref,
     ):
         step = pl.program_id(0)
         owner = owner_ref[...]
@@ -103,7 +112,15 @@
         hot = (iota((low * bucket, block), 0) == slot).astype(F32).astype(BF)
         group = owner >> 2
         surface = (iota((rows, width), 0) * levels == iota((rows, width), 1)).astype(F32)
-        value = (dot(surface.astype(BF), x_ref[...]) * weight_ref[...]).astype(BF)
+
+        @pl.when(step == 0)
+        def _():
+            keep_ref[...] = weight_ref[...].astype(F32) * mask_ref[...].astype(F32)
+
+        per_step = block // 128
+        keep = keep_ref[pl.ds(pl.multiple_of(step * per_step, per_step), per_step), :]
+        keep = jnp.concatenate([keep[c : c + 1] for c in range(per_step)], axis=1)
+        value = (dot(surface.astype(BF), x_ref[...]) * keep).astype(BF)
         zero = jnp.zeros_like(value)
         picked = jnp.concatenate(
             [jnp.where(group == g, value, zero) for g in range(high)], axis=0
@@ -138,15 +155,16 @@
         kernel,
         grid=(steps,),
         out_shape=jax.ShapeDtypeStruct((npatch, rows + 2, bucket), BF),
-        in_specs=[pl.BlockSpec((width, block), lambda i: (0, i))] + [lane] * 4,
+        in_specs=[pl.BlockSpec((width, block), lambda i: (0, i)), VMEM, VMEM] + [lane] * 3,
         out_specs=pl.BlockSpec((npatch, rows + 2, bucket), lambda i: (0, 0, 0)),
         scratch_shapes=[
             pltpu.VMEM((high * rows, low * bucket), F32),
             pltpu.VMEM((2 * high, low * bucket), F32),
+            pltpu.VMEM((tiles // 128, 128), F32),
         ],
         compiler_params=params(60),
         name="bucket_tiles",
-    )(land_rows, weight, owners, ranks, columns)
+    )(land_rows, weight, mask, owners, ranks, columns)
 
 
 def lane_swap(rows, a, b):
@@ -155,36 +173,30 @@
     return ((source % b) * a + source // b == target).astype(F32).astype(BF)
 
 
-def sort_land(pos, land_rows, levels, skip, shares):
+def sort_land(pos, land_rows, levels, skip, count):
     width, tiles = land_rows.shape
     span = tiles // PARTS
     block = 512
-    whole = [sum(shares[:i]) * span for i in range(len(shares))]
-
-    def kernel(pos_ref, x_ref, *out_refs):
+
+    def kernel(pos_ref, x_ref, out_ref):
         swap = lane_swap(width, width // levels, levels)
-        for out_ref, begin in zip(out_refs, whole):
-            for at in range(0, out_ref.shape[0], block):
-                part = (begin + at) // span
-                cut = slice((skip + part) * span, (skip + part + 1) * span)
-                place = iota((block, span), 0) + (begin + at - part * span)
-                hot = (place == pos_ref[:, cut]).astype(F32).astype(BF)
-                moved = dot(hot, x_ref[:, (cut.start - low) : (cut.stop - low)], NT).astype(BF)
-                out_ref[at : at + block, :] = dot(moved, swap).astype(BF)
-
-    count = sum(shares)
-    low = skip * span if skip == 0 else 0
-    taken = (
-        pl.BlockSpec((width, count * span), lambda i: (0, 0))
-        if skip == 0
-        else pl.BlockSpec((width, tiles), lambda i: (0, 0))
-    )
+        for at in range(0, count * span, block):
+            part = at // span
+            cut = slice(part * span, (part + 1) * span)
+            place = iota((block, span), 0) + (at - part * span)
+            hot = (place == pos_ref[:, cut]).astype(F32).astype(BF)
+            moved = dot(hot, x_ref[:, cut], NT).astype(BF)
+            out_ref[at : at + block, :] = dot(moved, swap).astype(BF)
+
     return pl.pallas_call(
         kernel,
         grid=(1,),
-        out_shape=[jax.ShapeDtypeStruct((n * span, width), BF) for n in shares],
-        in_specs=[pl.BlockSpec((1, tiles), lambda i: (0, 0)), taken],
-        out_specs=[pl.BlockSpec((n * span, width), lambda i: (0, 0)) for n in shares],
+        out_shape=[jax.ShapeDtypeStruct((count * span, width), BF)],
+        in_specs=[
+            pl.BlockSpec((1, count * span), lambda i: (0, skip // count)),
+            pl.BlockSpec((width, count * span), lambda i: (0, skip // count)),
+        ],
+        out_specs=[pl.BlockSpec((count * span, width), lambda i: (0, 0))],
         compiler_params=params(60),
         name="sort_land",
     )(pos, land_rows)
@@ -270,7 +282,6 @@
                     mix_ref[...], spread.astype(F32).astype(BF)
                 ).astype(BF)
             lane_level = iota((local, lanes), 1) // local
-            y_ref[...] = jnp.zeros_like(y_ref)
             for copy in copies:
                 copy.wait()
 
@@ -531,7 +542,8 @@
     packed = bucket_tiles(
         land_rows,
         layers,
-        (tile_weight.astype(F32) * land_mask.astype(F32)).reshape(1, tiles),
+        tile_weight.reshape(tiles // 128, 128),
+        land_mask.reshape(tiles // 128, 128),
         owners,
         ranks,
         tile_column.reshape(1, tiles),
@@ -540,12 +552,13 @@
     )
     received = lax.all_to_all(packed, "patch", split_axis=0, concat_axis=0, tiled=True)
 
-    (first,) = sort_land(pos, land_rows, layers, 0, (1,))
+    (first,) = sort_land(pos, land_rows, layers, 0, 1)
     first_prev = shifted(first, "mem", 1)
     first_next = shifted(first, "mem", -1)
-    second, rest = sort_land(pos, land_rows, layers, 1, (1, PARTS - 2))
+    (second,) = sort_land(pos, land_rows, layers, 1, 1)
     second_prev = shifted(second, "mem", 1)
     second_next = shifted(second, "mem", -1)
+    (rest,) = sort_land(pos, land_rows, layers, PARTS // 2, PARTS // 2)
 
     forecast = screen_forecast(
         received, atmos_rows, levels, observation_column.reshape(-1, 1), mem_count

time: 181 us -> 177 us (0.978)
  waiting for transfers between devices: 41.7 us -> 36.6 us
  Pallas kernels: 52.2 us -> 54.8 us
    ppermute x16, waiting for transfers between devices: 37.3 us -> 33.7 us  [shifted(): return lax.ppermute(value, axis, pairs)]
    pallas_call x2 -> x3, Pallas kernels: 10.1 us -> 11.7 us  [sort_land(): pl.pallas_call(kernel, grid=(1,), out_shape=[jax.ShapeDtypeStruct((count...]
  transfers between devices with their start and end apart: 18 -> 18, of which waited for: 4 -> 4; matrix products, arithmetic and copies ran while one was open for 4% -> 4% of each run, Pallas kernels for 11% -> 12%
where the time goes in v4:
time: 177 us; the launch traced here: 176 us
  Pallas kernels  54.8 us (31%)
  starting transfers between devices  52.7 us (30%)
  waiting for transfers between devices  36.6 us (21%)
  blocking collectives  22 us (12%)
  matrix products  6.24 us (4%)
  local copies, waits for them, and re-layouts  2.95 us (2%)
    ppermute x16, waiting for transfers between devices, shifted(): return lax.ppermute(value, axis, pairs)  33.7 us
    ppermute x16, starting transfers between devices, shifted(): return lax.ppermute(value, axis, pairs)  29.1 us
    pallas_call x1, Pallas kernels, mix_land(): pl.pallas_call(kernel, grid=(PARTS,), out_shape=jax.ShapeDtypeStruct((wid...  22.8 us
    all_to_all x1, blocking collectives, analysis(): lax.all_to_all(forecast, 'mem', split_axis=0, concat_axis=0, tiled=True)  22 us
    all_to_all x1, starting transfers between devices, analysis(): lax.all_to_all(packed, 'patch', split_axis=0, concat_axis=0, tiled=True)  13.1 us
    pallas_call x3, Pallas kernels, sort_land(): pl.pallas_call(kernel, grid=(1,), out_shape=[jax.ShapeDtypeStruct((count...  11.7 us
    all_to_all x1, starting transfers between devices, analysis(): lax.all_to_all(mixes, 'patch', split_axis=0, concat_axis=0, tiled=True)  10.5 us
    pallas_call x1, Pallas kernels, bucket_tiles(): pl.pallas_call(kernel, grid=(steps,), out_shape=jax.ShapeDtypeStruct((npa...  7.76 us
  transfers between devices with their start and end apart: 18, of which 4 were waited for; matrix products, arithmetic and copies ran while one was open for 4% of the time, Pallas kernels for 12%

profile of v4, /device:TPU:1, one launch (start us, length us, event | category | flops | bytes accessed | tf_op | source)
XLA Modules:
  0.0 176.5 jit_solution(6317271801817968625)
XLA Ops:
  0.6 2.3 %order_tiles.1 = (s32[1,4096]{1,0:T(1,128)}, s32[1,4096]{1,0:T(1,128)}, s32[64,8]{1,0:T(8,128)}) custom-call(s32[1,4096]{1,0:T(1,128)} %bitcast.44), custom_call_target="tpu_custom_call" | custom-call | tf_op jit(solution)/shard_map/order_tiles/pallas_call | solution.py:75
  2.9 7.8 %bucket_tiles.1 = bf16[64,34,128]{2,1,0:T(8,128)(2,1)} custom-call(bf16[256,4096]{1,0:T(8,128)(2,1)} %bitcast.35, bf16[32,128]{1,0:T(8,128)(2,1)} %bitcast.47, s32[32,128]{1,0:T(8,128)} %bitcast.42, s32[1,4096]{1,0:T(1,128)} %bitcast.45, s32[1,4096]{1,0:T(1,128)} %get-tuple-element.15.rank_ref, s32[1,4096]{1,0:T(1,128)} %bitcast.46), custom_call_target="tpu_custom_call" | custom-call | tf_op jit(solution)/shard_map/bucket_tiles/pallas_call | solution.py:154
  10.7 13.1 %all-to-all-start = ((bf16[64,34,128]{2,1,0:T(8,128)(2,1)}), bf16[64,34,128]{2,1,0:T(8,128)(2,1)S(1)}, u32[]{:S(2)}, u32[]{:S(2)}) async-start(bf16[64,34,128]{2,1,0:T(8,128)(2,1)} %bucket_tiles.1), calls=%async_computation | async-start | bytes 1310720 | tf_op jit(solution)/shard_map/all_to_all | solution.py:553
  23.9 3.4 %sort_land.3.refs_0_ = bf16[1024,256]{1,0:T(8,128)(2,1)} custom-call(s32[1,4096]{1,0:T(1,128)} %get-tuple-element.16.pos_ref.refs_13_, bf16[256,4096]{1,0:T(8,128)(2,1)} %bitcast.36), custom_call_target="tpu_custom_call" | custom-call | tf_op jit(solution)/shard_map/sort_land/pallas_call | solution.py:191
  27.2 1.2 collective-permute-start
  28.4 1.5 collective-permute-start.1
  29.9 3.4 %sort_land.4.refs_1_ = bf16[1024,256]{1,0:T(8,128)(2,1)} custom-call(s32[1,4096]{1,0:T(1,128)} %get-tuple-element.16.pos_ref.refs_13_, bf16[256,4096]{1,0:T(8,128)(2,1)} %bitcast.37), custom_call_target="tpu_custom_call" | custom-call | tf_op jit(solution)/shard_map/sort_land/pallas_call | solution.py:191
  33.3 0.0 copy-start.4
  33.3 0.1 collective-permute-start.2
  33.4 2.7 %collective-permute-start.3 = (bf16[1024,256]{1,0:T(8,128)(2,1)}, bf16[1024,256]{1,0:T(8,128)(2,1)}, u32[]{:S(2)}, u32[]{:S(2)}) collective-permute-start(bf16[1024,256]{1,0:T(8,128)(2,1)} %sort_land.4.refs_1_), channel_id=1, source_target_pairs={{0,3},{1,0},{2,1},{3,2},{4,7},{5,4},{6,5},{7,6},{8,11},{9,8},{10,9... | collective-permute-start | bytes 1572872 | tf_op jit(solution)/shard_map/ppermute | solution.py:39
  36.0 4.9 %sort_land.5.refs_2_ = bf16[2048,256]{1,0:T(8,128)(2,1)} custom-call(s32[1,4096]{1,0:T(1,128)} %get-tuple-element.16.pos_ref.refs_13_, bf16[256,4096]{1,0:T(8,128)(2,1)} %bitcast.38), custom_call_target="tpu_custom_call" | custom-call | tf_op jit(solution)/shard_map/sort_land/pallas_call | solution.py:191
  41.0 0.1 copy.17.obs_ref
  41.1 2.8 %all-to-all-done.in_ref = bf16[64,34,128]{2,1,0:T(8,128)(2,1)S(1)} async-done(((bf16[64,34,128]{2,1,0:T(8,128)(2,1)}), bf16[64,34,128]{2,1,0:T(8,128)(2,1)S(1)}, u32[]{:S(2)}, u32[]{:S(2)}) %all-to-all-start) | async-done | bytes 557088 | tf_op jit(solution)/shard_map/all_to_all | solution.py:553
  44.0 3.0 %screen_forecast.1 = bf16[4,32,512]{2,1,0:T(8,128)(2,1)S(1)} custom-call(bf16[64,34,128]{2,1,0:T(8,128)(2,1)S(1)} %all-to-all-done.in_ref, bf16[256,1024]{1,0:T(8,128)(2,1)S(1)} %bitcast.29, s32[512,1]{1,0:T(8,128)S(1)} %copy.17.obs_ref), custom_call_target="tpu_custom_call" | custom-call | tf_op jit(solution)/shard_map/screen_forecast/pallas_call | solution.py:231
  46.9 0.0 collective-permute-done.refs_3_
  47.0 0.0 collective-permute-done.1.refs_6_
  47.0 6.0 %collective-permute-done.2.refs_4_ = bf16[1024,256]{1,0:T(8,128)(2,1)} collective-permute-done((bf16[1024,256]{1,0:T(8,128)(2,1)}, bf16[1024,256]{1,0:T(8,128)(2,1)}, u32[]{:S(2)}, u32[]{:S(2)}) %collective-permute-start.2) | collective-permute-done | bytes 524320 | tf_op jit(solution)/shard_map/ppermute | solution.py:39
  53.0 2.4 %collective-permute-start.8 = (bf16[2048,256]{1,0:T(8,128)(2,1)}, bf16[2048,256]{1,0:T(8,128)(2,1)S(1)}, u32[]{:S(2)}, u32[]{:S(2)}) collective-permute-start(bf16[2048,256]{1,0:T(8,128)(2,1)} %sort_land.5.refs_2_), channel_id=1, source_target_pairs={{0,3},{1,0},{2,1},{3,2},{4,7},{5,4},{6,5},{7,6},{8,11},{9,8},{10,9... | collective-permute-start | bytes 3145736 | tf_op jit(solution)/shard_map/ppermute | solution.py:39
  55.4 0.0 collective-permute-start.9
  55.4 22.0 %all_to_all.15.in_ref = bf16[4,32,512]{2,1,0:T(8,128)(2,1)S(1)} all-to-all(bf16[4,32,512]{2,1,0:T(8,128)(2,1)S(1)} %screen_forecast.1), channel_id=1, replica_groups=mesh['patch'=64,'mem'=4] {'mem'}, dimensions={0} | all-to-all | bytes 262144 | tf_op jit(solution)/shard_map/all_to_all | solution.py:569
  77.5 0.6 screen_stats.1.own_ref
  78.1 5.4 %collective-permute-start.4 = (f32[72,128]{1,0:T(8,128)S(1)}, f32[72,128]{1,0:T(8,128)S(1)}, u32[]{:S(2)}, u32[]{:S(2)}) collective-permute-start(f32[72,128]{1,0:T(8,128)S(1)} %screen_stats.1.own_ref), channel_id=1, source_target_pairs={{0,32},{4,36},{8,40},{12,44},{16,48},{20,52},{24,56},{28,60},{32,6... | collective-permute-start | bytes 110600 | tf_op jit(solution)/shard_map/ppermute | solution.py:39
  83.6 2.5 %collective-permute-start.5 = (f32[72,128]{1,0:T(8,128)S(1)}, f32[72,128]{1,0:T(8,128)S(1)}, u32[]{:S(2)}, u32[]{:S(2)}) collective-permute-start(f32[72,128]{1,0:T(8,128)S(1)} %screen_stats.1.own_ref), channel_id=1, source_target_pairs={{0,224},{4,228},{8,232},{12,236},{16,240},{20,244},{24,248},{28,25... | collective-permute-start | bytes 110600 | tf_op jit(solution)/shard_map/ppermute | solution.py:39
  86.1 4.4 %collective-permute-start.6 = (f32[72,128]{1,0:T(8,128)S(1)}, f32[72,128]{1,0:T(8,128)S(1)}, u32[]{:S(2)}, u32[]{:S(2)}) collective-permute-start(f32[72,128]{1,0:T(8,128)S(1)} %screen_stats.1.own_ref), channel_id=1, source_target_pairs={{0,4},{4,8},{8,12},{12,16},{16,20},{20,24},{24,28},{28,32},{32,36}... | collective-permute-start | bytes 110600 | tf_op jit(solution)/shard_map/ppermute | solution.py:39
  90.5 0.0 collective-permute-done.4.refs_0_
  90.5 1.0 collective-permute-start.7
  91.5 0.1 pad_add_fusion.id_ref
  91.6 1.3 collective-permute-start.11
  92.9 0.0 collective-permute-done.6.refs_2_
  92.9 2.1 %collective-permute-start.10 = (bf16[256,1024]{1,0:T(8,128)(2,1)S(1)}, bf16[256,1024]{1,0:T(8,128)(2,1)}, u32[]{:S(2)}, u32[]{:S(2)}) collective-permute-start(bf16[256,1024]{1,0:T(8,128)(2,1)S(1)} %bitcast.32), channel_id=1, source_target_pairs={{0,3},{1,0},{2,1},{3,2},{4,7},{5,4},{6,5},{7,6},{8,11},{9,8},{10,9... | collective-permute-start | bytes 1572872 | tf_op jit(solution)/shard_map/ppermute | solution.py:39
  95.0 0.0 collective-permute-done.7.refs_3_
  95.1 1.0 collective-permute-start.12
  96.1 6.7 %settle.1 = (bf16[32,128]{1,0:T(8,128)(2,1)S(1)}, bf16[64,32,128]{2,1,0:T(8,128)(2,1)}) custom-call(s32[1,4]{1,0:T(1,128)S(1)} %copy-done.4, s32[2]{0:T(128)S(1)} %pad_add_fusion.id_ref, f32[72,128]{1,0:T(8,128)S(1)} %screen_stats.1.own_ref, f32[72,128]{1,0:T(8,128)S(1)} %collective-permute-done.4.refs_0_, f32[72,128]{1,0:T(8,128)S(1)} %collective-permute-done.5.refs_1_, ...), custom_call_target="tpu_custom_call" | custom-call | tf_op jit(solution)/shard_map/settle/pallas_call | solution.py:499
  102.8 10.5 %all-to-all-start.2 = ((bf16[64,32,128]{2,1,0:T(8,128)(2,1)}), bf16[64,32,128]{2,1,0:T(8,128)(2,1)S(1)}, u32[]{:S(2)}, u32[]{:S(2)}) async-start(bf16[64,32,128]{2,1,0:T(8,128)(2,1)} %get-tuple-element.27), calls=%async_computation.2 | async-start | bytes 1048576 | tf_op jit(solution)/shard_map/all_to_all | solution.py:581
  113.3 2.5 %collective-permute-start.15 = (bf16[2048,256]{1,0:T(8,128)(2,1)S(1)}, bf16[2048,256]{1,0:T(8,128)(2,1)}, u32[]{:S(2)}, u32[]{:S(2)}) collective-permute-start(bf16[2048,256]{1,0:T(8,128)(2,1)S(1)} %collective-permute-done.8.refs_8_), channel_id=1, source_target_pairs={{0,3},{1,0},{2,1},{3,2},{4,7},{5,4},{6,5},{7,6},{8,11},{9,8},{10,9... | collective-permute-start | bytes 3145736 | tf_op jit(solution)/shard_map/ppermute | solution.py:39
  115.8 0.8 fusion.6
  116.6 0.0 collective-permute-done.9
  116.6 0.1 collective-permute-start.13
  116.7 1.8 %convolution_add_fusion.1 = f32[32,8,1024]{2,0,1:T(8,128)S(1)} fusion(f32[32,8,1024]{2,0,1:T(8,128)S(1)} %fusion.6, bf16[32,8,1024]{2,1,0:T(8,128)(2,1)} %bitcast.13, bf16[32,128]{1,0:T(8,128)(2,1)S(1)} %get-tuple-element.20, s32[]{:T(128)S(6)} %select_n.34), kind=kOutput, calls=%fused_computation.2 | convolution fusion | flops 17039360 | bytes 2629636 | tf_op jit(solution)/shard_map/jk,klc->jlc/dot_general | solution.py:587
  118.5 0.8 collective-permute-start.14
  119.3 1.8 %fusion.2 = f32[32,8,1024]{2,0,1:T(8,128)S(1)} fusion(bf16[32,8,1024]{2,1,0:T(8,128)(2,1)} %bitcast.17, bf16[32,128]{1,0:T(8,128)(2,1)S(1)} %get-tuple-element.20, s32[]{:T(128)S(6)} %select_n.38), kind=kOutput, calls=%fused_computation.4 | convolution fusion | flops 16777216 | bytes 1581060 | tf_op jit(solution)/shard_map/jk,klc->jlc/dot_general | solution.py:587
  121.2 1.8 %fusion.1 = bf16[32,8,1024]{2,0,1:T(8,128)(2,1)S(1)} fusion(f32[32,8,1024]{2,0,1:T(8,128)S(1)} %fusion.2, f32[32,8,1024]{2,0,1:T(8,128)S(1)} %convolution_add_fusion.1, bf16[32,8,1024]{2,1,0:T(8,128)(2,1)} %bitcast.15, bf16[32,128]{1,0:T(8,128)(2,1)S(1)} %get-tuple-element.20, s32[]{:T(128)S(6)} %select_n.36), kind=kOutput, calls=%fused_computation.3 | convolution fusion | flops 17563648 | bytes 3153924 | tf_op jit(solution)/shard_map/jk,klc->jlc/dot_general | solution.py:587
  123.0 1.1 copy.22
  124.1 16.4 %collective-permute-done.13.refs_9_ = bf16[1024,256]{1,0:T(8,128)(2,1)S(1)} collective-permute-done((bf16[1024,256]{1,0:T(8,128)(2,1)}, bf16[1024,256]{1,0:T(8,128)(2,1)S(1)}, u32[]{:S(2)}, u32[]{:S(2)}) %collective-permute-start.13) | collective-permute-done | bytes 524320 | tf_op jit(solution)/shard_map/ppermute | solution.py:39
  140.5 11.2 %collective-permute-done.14.refs_10_ = bf16[1024,256]{1,0:T(8,128)(2,1)S(1)} collective-permute-done((bf16[1024,256]{1,0:T(8,128)(2,1)}, bf16[1024,256]{1,0:T(8,128)(2,1)S(1)}, u32[]{:S(2)}, u32[]{:S(2)}) %collective-permute-start.14) | collective-permute-done | bytes 524320 | tf_op jit(solution)/shard_map/ppermute | solution.py:39
  151.8 0.8 copy-done.10
  152.6 0.8 copy-done.6
  153.5 22.8 %mix_land.1 = bf16[256,4096]{1,0:T(8,128)(2,1)} custom-call(s32[2]{0:T(128)} %copy-done.3, s32[64,8]{1,0:T(8,128)} %get-tuple-element.21.start_ref, bf16[1024,256]{1,0:T(8,128)(2,1)} %sort_land.3.refs_0_, bf16[1024,256]{1,0:T(8,128)(2,1)} %sort_land.4.refs_1_, bf16[2048,256]{1,0:T(8,128)(2,1)} %sort_land.5.refs_2_, bf16[1024,256]{1,0:T(8,128)(2,1)} %copy-done.8, ...), custom_call_target="tpu_custom_call" | custom-call | tf_op jit(solution)/shard_map/mix_land/pallas_call | solution.py:379
  (29 shorter events, 0.1 us)
Async XLA Ops:
  10.7 33.2 %all-to-all-start = ((bf16[64,34,128]{2,1,0:T(8,128)(2,1)}), bf16[64,34,128]{2,1,0:T(8,128)(2,1)S(1)}, u32[]{:S(2)}, u32[]{:S(2)}) async-start(bf16[64,34,128]{2,1,0:T(8,128)(2,1)} %bucket_tiles.1), calls=%async_computation | async-start | bytes 1310720 | tf_op jit(solution)/shard_map/all_to_all | solution.py:553
  27.2 19.7 %collective-permute-start = (bf16[1024,256]{1,0:T(8,128)(2,1)}, bf16[1024,256]{1,0:T(8,128)(2,1)S(1)}, u32[]{:S(2)}, u32[]{:S(2)}) collective-permute-start(bf16[1024,256]{1,0:T(8,128)(2,1)} %sort_land.3.refs_0_), channel_id=1, source_target_pairs={{0,1},{1,2},{2,3},{3,0},{4,5},{5,6},{6,7},{7,4},{8,9},{9,10},{10,1... | collective-permute-start | bytes 1572872 | tf_op jit(solution)/shard_map/ppermute | solution.py:39
  28.4 18.5 %collective-permute-start.1 = (bf16[1024,256]{1,0:T(8,128)(2,1)}, bf16[1024,256]{1,0:T(8,128)(2,1)}, u32[]{:S(2)}, u32[]{:S(2)}) collective-permute-start(bf16[1024,256]{1,0:T(8,128)(2,1)} %sort_land.3.refs_0_), channel_id=1, source_target_pairs={{0,3},{1,0},{2,1},{3,2},{4,7},{5,4},{6,5},{7,6},{8,11},{9,8},{10,9... | collective-permute-start | bytes 1572872 | tf_op jit(solution)/shard_map/ppermute | solution.py:39
  33.3 7.7 %copy-start.11 = (s32[512]{0:T(512)S(1)}, s32[512]{0:T(512)}, u32[]{:S(2)}) copy-start(s32[512]{0:T(512)} %param.17) | copy-start | bytes 6148
  33.3 10.7 %copy-start = (bf16[32,8,1024]{2,1,0:T(8,128)(2,1)S(1)}, bf16[32,8,1024]{2,1,0:T(8,128)(2,1)}, u32[]{:S(2)}) copy-start(bf16[32,8,1024]{2,1,0:T(8,128)(2,1)} %param.10) | copy-start | bytes 1572868
  33.3 44.2 %copy-start.1 = (f32[512]{0:T(512)S(1)}, f32[512]{0:T(512)}, u32[]{:S(2)}) copy-start(f32[512]{0:T(512)} %param.16) | copy-start | bytes 6148
  33.3 44.2 %copy-start.2 = (f32[512]{0:T(512)S(1)}, f32[512]{0:T(512)}, u32[]{:S(2)}) copy-start(f32[512]{0:T(512)} %param.18) | copy-start | bytes 6148
  33.3 62.8 %copy-start.4 = (s32[1,4]{1,0:T(1,128)S(1)}, s32[1,4]{1,0:T(1,128)}, u32[]{:S(2)}) copy-start(s32[1,4]{1,0:T(1,128)} %list_ref.1) | copy-start | bytes 52
  33.3 19.7 %collective-permute-start.2 = (bf16[1024,256]{1,0:T(8,128)(2,1)}, bf16[1024,256]{1,0:T(8,128)(2,1)}, u32[]{:S(2)}, u32[]{:S(2)}) collective-permute-start(bf16[1024,256]{1,0:T(8,128)(2,1)} %sort_land.4.refs_1_), channel_id=1, source_target_pairs={{0,1},{1,2},{2,3},{3,0},{4,5},{5,6},{6,7},{7,4},{8,9},{9,10},{10,1... | collective-permute-start | bytes 1572872 | tf_op jit(solution)/shard_map/ppermute | solution.py:39
  33.4 19.6 %collective-permute-start.3 = (bf16[1024,256]{1,0:T(8,128)(2,1)}, bf16[1024,256]{1,0:T(8,128)(2,1)}, u32[]{:S(2)}, u32[]{:S(2)}) collective-permute-start(bf16[1024,256]{1,0:T(8,128)(2,1)} %sort_land.4.refs_1_), channel_id=1, source_target_pairs={{0,3},{1,0},{2,1},{3,2},{4,7},{5,4},{6,5},{7,6},{8,11},{9,8},{10,9... | collective-permute-start | bytes 1572872 | tf_op jit(solution)/shard_map/ppermute | solution.py:39
  41.0 54.1 %copy-start.5 = (bf16[2048,256]{1,0:T(8,128)(2,1)S(1)}, bf16[2048,256]{1,0:T(8,128)(2,1)}, u32[]{:S(2)}) copy-start(bf16[2048,256]{1,0:T(8,128)(2,1)} %sort_land.5.refs_2_) | copy-start | bytes 3145732
  46.9 36.6 %copy-start.8 = (bf16[1024,256]{1,0:T(8,128)(2,1)}, bf16[1024,256]{1,0:T(8,128)(2,1)S(1)}, u32[]{:S(2)}) copy-start(bf16[1024,256]{1,0:T(8,128)(2,1)S(1)} %collective-permute-done.refs_3_) | copy-start | bytes 1572868
  53.0 60.3 %collective-permute-start.8 = (bf16[2048,256]{1,0:T(8,128)(2,1)}, bf16[2048,256]{1,0:T(8,128)(2,1)S(1)}, u32[]{:S(2)}, u32[]{:S(2)}) collective-permute-start(bf16[2048,256]{1,0:T(8,128)(2,1)} %sort_land.5.refs_2_), channel_id=1, source_target_pairs={{0,3},{1,0},{2,1},{3,2},{4,7},{5,4},{6,5},{7,6},{8,11},{9,8},{10,9... | collective-permute-start | bytes 3145736 | tf_op jit(solution)/shard_map/ppermute | solution.py:39
  55.4 61.2 %collective-permute-start.9 = (bf16[256,1024]{1,0:T(8,128)(2,1)S(1)}, bf16[256,1024]{1,0:T(8,128)(2,1)}, u32[]{:S(2)}, u32[]{:S(2)}) collective-permute-start(bf16[256,1024]{1,0:T(8,128)(2,1)S(1)} %bitcast.30), channel_id=1, source_target_pairs={{0,1},{1,2},{2,3},{3,0},{4,5},{5,6},{6,7},{7,4},{8,9},{9,10},{10,1... | collective-permute-start | bytes 1572872 | tf_op jit(solution)/shard_map/ppermute | solution.py:39
  78.1 12.4 %collective-permute-start.4 = (f32[72,128]{1,0:T(8,128)S(1)}, f32[72,128]{1,0:T(8,128)S(1)}, u32[]{:S(2)}, u32[]{:S(2)}) collective-permute-start(f32[72,128]{1,0:T(8,128)S(1)} %screen_stats.1.own_ref), channel_id=1, source_target_pairs={{0,32},{4,36},{8,40},{12,44},{16,48},{20,52},{24,56},{28,60},{32,6... | collective-permute-start | bytes 110600 | tf_op jit(solution)/shard_map/ppermute | solution.py:39
  83.6 8.1 %collective-permute-start.5 = (f32[72,128]{1,0:T(8,128)S(1)}, f32[72,128]{1,0:T(8,128)S(1)}, u32[]{:S(2)}, u32[]{:S(2)}) collective-permute-start(f32[72,128]{1,0:T(8,128)S(1)} %screen_stats.1.own_ref), channel_id=1, source_target_pairs={{0,224},{4,228},{8,232},{12,236},{16,240},{20,244},{24,248},{28,25... | collective-permute-start | bytes 110600 | tf_op jit(solution)/shard_map/ppermute | solution.py:39
  86.1 6.8 %collective-permute-start.6 = (f32[72,128]{1,0:T(8,128)S(1)}, f32[72,128]{1,0:T(8,128)S(1)}, u32[]{:S(2)}, u32[]{:S(2)}) collective-permute-start(f32[72,128]{1,0:T(8,128)S(1)} %screen_stats.1.own_ref), channel_id=1, source_target_pairs={{0,4},{4,8},{8,12},{12,16},{16,20},{20,24},{24,28},{28,32},{32,36}... | collective-permute-start | bytes 110600 | tf_op jit(solution)/shard_map/ppermute | solution.py:39
  90.5 4.5 %collective-permute-start.7 = (f32[72,128]{1,0:T(8,128)S(1)}, f32[72,128]{1,0:T(8,128)S(1)}, u32[]{:S(2)}, u32[]{:S(2)}) collective-permute-start(f32[72,128]{1,0:T(8,128)S(1)} %screen_stats.1.own_ref), channel_id=1, source_target_pairs={{0,252},{4,0},{8,4},{12,8},{16,12},{20,16},{24,20},{28,24},{32,28}... | collective-permute-start | bytes 110600 | tf_op jit(solution)/shard_map/ppermute | solution.py:39
  91.6 26.9 %copy-start.3 = (s32[2]{0:T(128)}, s32[2]{0:T(128)S(1)}, u32[]{:S(2)}) copy-start(s32[2]{0:T(128)S(1)} %pad_add_fusion.id_ref) | copy-start | bytes 28
  91.6 26.9 %collective-permute-start.11 = (bf16[256,1024]{1,0:T(8,128)(2,1)S(1)}, bf16[256,1024]{1,0:T(8,128)(2,1)}, u32[]{:S(2)}, u32[]{:S(2)}) collective-permute-start(bf16[256,1024]{1,0:T(8,128)(2,1)S(1)} %bitcast.31), channel_id=1, source_target_pairs={{0,2},{1,3},{2,0},{3,1},{4,6},{5,7},{6,4},{7,5},{8,10},{9,11},{10,... | collective-permute-start | bytes 1572872 | tf_op jit(solution)/shard_map/ppermute | solution.py:39
  92.9 28.3 %collective-permute-start.10 = (bf16[256,1024]{1,0:T(8,128)(2,1)S(1)}, bf16[256,1024]{1,0:T(8,128)(2,1)}, u32[]{:S(2)}, u32[]{:S(2)}) collective-permute-start(bf16[256,1024]{1,0:T(8,128)(2,1)S(1)} %bitcast.32), channel_id=1, source_target_pairs={{0,3},{1,0},{2,1},{3,2},{4,7},{5,4},{6,5},{7,6},{8,11},{9,8},{10,9... | collective-permute-start | bytes 1572872 | tf_op jit(solution)/shard_map/ppermute | solution.py:39
  95.1 57.6 %collective-permute-start.12 = (bf16[2048,256]{1,0:T(8,128)(2,1)S(1)}, bf16[2048,256]{1,0:T(8,128)(2,1)}, u32[]{:S(2)}, u32[]{:S(2)}) collective-permute-start(bf16[2048,256]{1,0:T(8,128)(2,1)S(1)} %copy-done.5), channel_id=1, source_target_pairs={{0,1},{1,2},{2,3},{3,0},{4,5},{5,6},{6,7},{7,4},{8,9},{9,10},{10,1... | collective-permute-start | bytes 3145736 | tf_op jit(solution)/shard_map/ppermute | solution.py:39
  102.8 49.8 %all-to-all-start.2 = ((bf16[64,32,128]{2,1,0:T(8,128)(2,1)}), bf16[64,32,128]{2,1,0:T(8,128)(2,1)S(1)}, u32[]{:S(2)}, u32[]{:S(2)}) async-start(bf16[64,32,128]{2,1,0:T(8,128)(2,1)} %get-tuple-element.27), calls=%async_computation.2 | async-start | bytes 1048576 | tf_op jit(solution)/shard_map/all_to_all | solution.py:581
  113.3 5.2 %copy-start.7 = (bf16[2048,256]{1,0:T(8,128)(2,1)}, bf16[2048,256]{1,0:T(8,128)(2,1)S(1)}, u32[]{:S(2)}) copy-start(bf16[2048,256]{1,0:T(8,128)(2,1)S(1)} %collective-permute-done.8.refs_8_) | copy-start | bytes 3145732
  113.3 39.3 %collective-permute-start.15 = (bf16[2048,256]{1,0:T(8,128)(2,1)S(1)}, bf16[2048,256]{1,0:T(8,128)(2,1)}, u32[]{:S(2)}, u32[]{:S(2)}) collective-permute-start(bf16[2048,256]{1,0:T(8,128)(2,1)S(1)} %collective-permute-done.8.refs_8_), channel_id=1, source_target_pairs={{0,3},{1,0},{2,1},{3,2},{4,7},{5,4},{6,5},{7,6},{8,11},{9,8},{10,9... | collective-permute-start | bytes 3145736 | tf_op jit(solution)/shard_map/ppermute | solution.py:39
  116.6 24.0 %collective-permute-start.13 = (bf16[1024,256]{1,0:T(8,128)(2,1)}, bf16[1024,256]{1,0:T(8,128)(2,1)S(1)}, u32[]{:S(2)}, u32[]{:S(2)}) collective-permute-start(bf16[1024,256]{1,0:T(8,128)(2,1)} %copy-done.8), channel_id=1, source_target_pairs={{0,1},{1,2},{2,3},{3,0},{4,5},{5,6},{6,7},{7,4},{8,9},{9,10},{10,1... | collective-permute-start | bytes 1572872 | tf_op jit(solution)/shard_map/ppermute | solution.py:39
  118.5 33.2 %collective-permute-start.14 = (bf16[1024,256]{1,0:T(8,128)(2,1)}, bf16[1024,256]{1,0:T(8,128)(2,1)S(1)}, u32[]{:S(2)}, u32[]{:S(2)}) collective-permute-start(bf16[1024,256]{1,0:T(8,128)(2,1)} %collective-permute-done.2.refs_4_), channel_id=1, source_target_pairs={{0,1},{1,2},{2,3},{3,0},{4,5},{5,6},{6,7},{7,4},{8,9},{9,10},{10,1... | collective-permute-start | bytes 1572872 | tf_op jit(solution)/shard_map/ppermute | solution.py:39
  140.5 11.2 %copy-start.9 = (bf16[1024,256]{1,0:T(8,128)(2,1)}, bf16[1024,256]{1,0:T(8,128)(2,1)S(1)}, u32[]{:S(2)}) copy-start(bf16[1024,256]{1,0:T(8,128)(2,1)S(1)} %collective-permute-done.13.refs_9_) | copy-start | bytes 1572868
  151.8 0.9 copy-start.10
  152.6 0.8 copy-start.6

commit v5 on v4

--- a/solution.py
+++ b/solution.py
@@ -41,6 +41,15 @@
 
 PARTS = 4
 UNROLL = 4
+
+
+def partner(patch, gap, npatch):
+    return (patch + gap - 2 * gap * ((patch // abs(gap)) % 2) + npatch) % npatch
+
+
+def swapped(value, gap, npatch):
+    pairs = [(source, partner(source, gap, npatch)) for source in range(npatch)]
+    return lax.ppermute(value, "patch", pairs)
 
 
 def order_tiles(owners, npatch):
@@ -173,30 +182,33 @@
     return ((source % b) * a + source // b == target).astype(F32).astype(BF)
 
 
-def sort_land(pos, land_rows, levels, skip, count):
+def sort_land(pos, land_rows, levels, begin, end):
     width, tiles = land_rows.shape
     span = tiles // PARTS
     block = 512
+    one = end - begin <= span and begin // span == (end - 1) // span
+    taken = span if one else tiles
+    shift = begin // span * span if one else 0
 
     def kernel(pos_ref, x_ref, out_ref):
         swap = lane_swap(width, width // levels, levels)
-        for at in range(0, count * span, block):
-            part = at // span
-            cut = slice(part * span, (part + 1) * span)
-            place = iota((block, span), 0) + (at - part * span)
+        for at in range(begin, end, block):
+            part = at // span * span
+            cut = slice(part - shift, part - shift + span)
+            place = iota((block, span), 0) + (at - part)
             hot = (place == pos_ref[:, cut]).astype(F32).astype(BF)
             moved = dot(hot, x_ref[:, cut], NT).astype(BF)
-            out_ref[at : at + block, :] = dot(moved, swap).astype(BF)
+            out_ref[at - begin : at - begin + block, :] = dot(moved, swap).astype(BF)
 
     return pl.pallas_call(
         kernel,
         grid=(1,),
-        out_shape=[jax.ShapeDtypeStruct((count * span, width), BF)],
+        out_shape=jax.ShapeDtypeStruct((end - begin, width), BF),
         in_specs=[
-            pl.BlockSpec((1, count * span), lambda i: (0, skip // count)),
-            pl.BlockSpec((width, count * span), lambda i: (0, skip // count)),
+            pl.BlockSpec((1, taken), lambda i: (0, shift // taken)),
+            pl.BlockSpec((width, taken), lambda i: (0, shift // taken)),
         ],
-        out_specs=[pl.BlockSpec((count * span, width), lambda i: (0, 0))],
+        out_specs=pl.BlockSpec((end - begin, width), lambda i: (0, 0)),
         compiler_params=params(60),
         name="sort_land",
     )(pos, land_rows)
@@ -443,7 +455,7 @@
     )(ensemble, obs_value, obs_error)
 
 
-def settle(own, near, listed, ids, offsets, local, npatch):
+def settle(own, near, listed, ids, gaps, local, npatch):
     members = own.shape[1]
     half = members // 2
     count = members // local
@@ -454,7 +466,7 @@
         cols_ref, out_ref, hold_ref = refs[len(near) :]
         total = own_ref[...]
         for d in range(len(near)):
-            source = (id_ref[0] - offsets[d] + npatch) % npatch
+            source = partner(id_ref[0], gaps[d], npatch)
             used = 0
             for i in range(names):
                 used = used + jnp.where(list_ref[0, i] == source, 1, 0)
@@ -552,13 +564,14 @@
     )
     received = lax.all_to_all(packed, "patch", split_axis=0, concat_axis=0, tiled=True)
 
-    (first,) = sort_land(pos, land_rows, layers, 0, 1)
+    early = (tiles // PARTS, 3 * tiles // (2 * PARTS))
+    first = sort_land(pos, land_rows, layers, 0, early[0])
     first_prev = shifted(first, "mem", 1)
     first_next = shifted(first, "mem", -1)
-    (second,) = sort_land(pos, land_rows, layers, 1, 1)
+    second = sort_land(pos, land_rows, layers, *early)
     second_prev = shifted(second, "mem", 1)
     second_next = shifted(second, "mem", -1)
-    (rest,) = sort_land(pos, land_rows, layers, PARTS // 2, PARTS // 2)
+    rest = sort_land(pos, land_rows, layers, early[1], tiles)
 
     forecast = screen_forecast(
         received, atmos_rows, levels, observation_column.reshape(-1, 1), mem_count
@@ -573,9 +586,9 @@
     second_far = shifted(second_prev, "mem", 1)
 
     own_stats = screen_stats(ensemble, obs_value.reshape(1, -1), obs_error.reshape(1, -1))
-    offsets = (row_width, -row_width, 1, -1)
-    near = [shifted(own_stats, "patch", o) for o in offsets]
-    own_cols, mixes = settle(own_stats, near, loc_blocks, ids, offsets, local, npatch)
+    gaps = (1, -1, row_width, -row_width)
+    near = [swapped(own_stats, gap, npatch) for gap in gaps]
+    own_cols, mixes = settle(own_stats, near, loc_blocks, ids, gaps, local, npatch)
     own_cols, rest_next = barrier((own_cols, rest_next))
     rest_far = shifted(rest_next, "mem", -1)
     all_mixes = lax.all_to_all(mixes, "patch", split_axis=0, concat_axis=0, tiled=True)

time: 177 us -> 185 us (1.045); the launches traced: 176 us -> 183 us
  starting transfers between devices: 52.7 us -> 59.3 us
  blocking collectives: 22 us -> 27.5 us
  waiting for transfers between devices: 36.6 us -> 31.4 us
    ppermute x0 -> x4, starting transfers between devices: none -> 12.3 us  [swapped(): return lax.ppermute(value, 'patch', pairs)]
    ppermute x16 -> x12, waiting for transfers between devices: 33.7 us -> 23.2 us  [shifted(): return lax.ppermute(value, axis, pairs)]
    all_to_all x1, blocking collectives: 22 us -> 27.5 us  [analysis(): lax.all_to_all(forecast, 'mem', split_axis=0, concat_axis=0, tiled=True)]
    ppermute x0 -> x4, waiting for transfers between devices: none -> 5.3 us  [swapped(): return lax.ppermute(value, 'patch', pairs)]
    ppermute x16 -> x12, starting transfers between devices: 29.1 us -> 24.3 us  [shifted(): return lax.ppermute(value, axis, pairs)]
  transfers between devices with their start and end apart: 18 -> 18, of which waited for: 4 -> 5; matrix products, arithmetic and copies ran while one was open for 4% -> 4% of each run, Pallas kernels for 12% -> 12%
where the time goes in v5:
time: 185 us; the launch traced here: 183 us
  starting transfers between devices  59.3 us (32%)
  Pallas kernels  54.9 us (30%)
  waiting for transfers between devices  31.4 us (17%)
  blocking collectives  27.5 us (15%)
  matrix products  6.24 us (3%)
  local copies, waits for them, and re-layouts  2.17 us (1%)
    all_to_all x1, blocking collectives, analysis(): lax.all_to_all(forecast, 'mem', split_axis=0, concat_axis=0, tiled=True)  27.5 us
    ppermute x12, starting transfers between devices, shifted(): return lax.ppermute(value, axis, pairs)  24.3 us
    ppermute x12, waiting for transfers between devices, shifted(): return lax.ppermute(value, axis, pairs)  23.2 us
    pallas_call x1, Pallas kernels, mix_land(): pl.pallas_call(kernel, grid=(PARTS,), out_shape=jax.ShapeDtypeStruct((wid...  22.8 us
    all_to_all x1, starting transfers between devices, analysis(): lax.all_to_all(packed, 'patch', split_axis=0, concat_axis=0, tiled=True)  13.1 us
    ppermute x4, starting transfers between devices, swapped(): return lax.ppermute(value, 'patch', pairs)  12.3 us
    pallas_call x3, Pallas kernels, sort_land(): pl.pallas_call(kernel, grid=(1,), out_shape=jax.ShapeDtypeStruct((end - b...  11.7 us
    all_to_all x1, starting transfers between devices, analysis(): lax.all_to_all(mixes, 'patch', split_axis=0, concat_axis=0, tiled=True)  9.52 us
  transfers between devices with their start and end apart: 18, of which 5 were waited for; matrix products, arithmetic and copies ran while one was open for 4% of the time, Pallas kernels for 12%

profile of v5, /device:TPU:1, one launch (start us, length us, event | category | flops | bytes accessed | tf_op | source)
XLA Modules:
  0.0 182.5 jit_solution(4865954182291733921)
XLA Ops:
  0.6 2.3 %order_tiles.1 = (s32[1,4096]{1,0:T(1,128)}, s32[1,4096]{1,0:T(1,128)}, s32[64,8]{1,0:T(8,128)}) custom-call(s32[1,4096]{1,0:T(1,128)} %bitcast.44), custom_call_target="tpu_custom_call" | custom-call | tf_op jit(solution)/shard_map/order_tiles/pallas_call | solution.py:84
  3.0 7.8 %bucket_tiles.1 = bf16[64,34,128]{2,1,0:T(8,128)(2,1)} custom-call(bf16[256,4096]{1,0:T(8,128)(2,1)} %bitcast.35, bf16[32,128]{1,0:T(8,128)(2,1)} %bitcast.47, s32[32,128]{1,0:T(8,128)} %bitcast.42, s32[1,4096]{1,0:T(1,128)} %bitcast.45, s32[1,4096]{1,0:T(1,128)} %get-tuple-element.15.rank_ref, s32[1,4096]{1,0:T(1,128)} %bitcast.46), custom_call_target="tpu_custom_call" | custom-call | tf_op jit(solution)/shard_map/bucket_tiles/pallas_call | solution.py:163
  10.7 13.1 %all-to-all-start = ((bf16[64,34,128]{2,1,0:T(8,128)(2,1)}), bf16[64,34,128]{2,1,0:T(8,128)(2,1)S(1)}, u32[]{:S(2)}, u32[]{:S(2)}) async-start(bf16[64,34,128]{2,1,0:T(8,128)(2,1)} %bucket_tiles.1), calls=%async_computation | async-start | bytes 1310720 | tf_op jit(solution)/shard_map/all_to_all | solution.py:565
  23.9 3.4 %sort_land.3.refs_0_ = bf16[1024,256]{1,0:T(8,128)(2,1)} custom-call(s32[1,4096]{1,0:T(1,128)} %get-tuple-element.16.pos_ref.refs_13_, bf16[256,4096]{1,0:T(8,128)(2,1)} %bitcast.36), custom_call_target="tpu_custom_call" | custom-call | tf_op jit(solution)/shard_map/sort_land/pallas_call | solution.py:203
  27.2 1.2 collective-permute-start
  28.4 1.5 collective-permute-start.1
  29.9 2.4 %sort_land.4.refs_1_ = bf16[512,256]{1,0:T(8,128)(2,1)} custom-call(s32[1,4096]{1,0:T(1,128)} %get-tuple-element.16.pos_ref.refs_13_, bf16[256,4096]{1,0:T(8,128)(2,1)} %bitcast.37), custom_call_target="tpu_custom_call" | custom-call | tf_op jit(solution)/shard_map/sort_land/pallas_call | solution.py:203
  32.3 2.7 %collective-permute-start.3 = (bf16[512,256]{1,0:T(8,128)(2,1)}, bf16[512,256]{1,0:T(8,128)(2,1)}, u32[]{:S(2)}, u32[]{:S(2)}) collective-permute-start(bf16[512,256]{1,0:T(8,128)(2,1)} %sort_land.4.refs_1_), channel_id=1, source_target_pairs={{0,3},{1,0},{2,1},{3,2},{4,7},{5,4},{6,5},{7,6},{8,11},{9,8},{10,9... | collective-permute-start | bytes 786440 | tf_op jit(solution)/shard_map/ppermute | solution.py:39
  35.0 5.9 %sort_land.5.refs_2_ = bf16[2560,256]{1,0:T(8,128)(2,1)} custom-call(s32[1,4096]{1,0:T(1,128)} %get-tuple-element.16.pos_ref.refs_13_, bf16[256,4096]{1,0:T(8,128)(2,1)} %bitcast.38), custom_call_target="tpu_custom_call" | custom-call | tf_op jit(solution)/shard_map/sort_land/pallas_call | solution.py:203
  40.9 0.1 copy.17.obs_ref
  41.1 2.9 %all-to-all-done.in_ref = bf16[64,34,128]{2,1,0:T(8,128)(2,1)S(1)} async-done(((bf16[64,34,128]{2,1,0:T(8,128)(2,1)}), bf16[64,34,128]{2,1,0:T(8,128)(2,1)S(1)}, u32[]{:S(2)}, u32[]{:S(2)}) %all-to-all-start) | async-done | bytes 557088 | tf_op jit(solution)/shard_map/all_to_all | solution.py:565
  44.0 3.0 %screen_forecast.1 = bf16[4,32,512]{2,1,0:T(8,128)(2,1)S(1)} custom-call(bf16[64,34,128]{2,1,0:T(8,128)(2,1)S(1)} %all-to-all-done.in_ref, bf16[256,1024]{1,0:T(8,128)(2,1)S(1)} %bitcast.29, s32[512,1]{1,0:T(8,128)S(1)} %copy.17.obs_ref), custom_call_target="tpu_custom_call" | custom-call | tf_op jit(solution)/shard_map/screen_forecast/pallas_call | solution.py:243
  47.0 0.3 collective-permute-done.2.refs_4_
  47.3 0.0 collective-permute-done.3.refs_7_
  47.3 0.0 collective-permute-done.refs_3_
  47.3 0.0 collective-permute-done.1.refs_6_
  47.3 2.6 %collective-permute-start.8 = (bf16[2560,256]{1,0:T(8,128)(2,1)S(1)}, bf16[2560,256]{1,0:T(8,128)(2,1)}, u32[]{:S(2)}, u32[]{:S(2)}) collective-permute-start(bf16[2560,256]{1,0:T(8,128)(2,1)S(1)} %copy-done.5), channel_id=1, source_target_pairs={{0,3},{1,0},{2,1},{3,2},{4,7},{5,4},{6,5},{7,6},{8,11},{9,8},{10,9... | collective-permute-start | bytes 3932168 | tf_op jit(solution)/shard_map/ppermute | solution.py:39
  49.9 27.5 %all_to_all.15.in_ref = bf16[4,32,512]{2,1,0:T(8,128)(2,1)S(1)} all-to-all(bf16[4,32,512]{2,1,0:T(8,128)(2,1)S(1)} %screen_forecast.1), channel_id=1, replica_groups=mesh['patch'=64,'mem'=4] {'mem'}, dimensions={0} | all-to-all | bytes 262144 | tf_op jit(solution)/shard_map/all_to_all | solution.py:582
  77.4 0.6 screen_stats.1.own_ref
  78.0 3.1 %collective-permute-start.4 = (f32[72,128]{1,0:T(8,128)S(1)}, f32[72,128]{1,0:T(8,128)S(1)}, u32[]{:S(2)}, u32[]{:S(2)}) collective-permute-start(f32[72,128]{1,0:T(8,128)S(1)} %screen_stats.1.own_ref), channel_id=1, source_target_pairs={{0,4},{4,0},{8,12},{12,8},{16,20},{20,16},{24,28},{28,24},{32,36},... | collective-permute-start | bytes 110600 | tf_op jit(solution)/shard_map/ppermute | solution.py:52
  81.1 1.5 collective-permute-start.9
  82.6 1.5 collective-permute-start.5
  84.1 4.2 %collective-permute-start.6 = (f32[72,128]{1,0:T(8,128)S(1)}, f32[72,128]{1,0:T(8,128)S(1)}, u32[]{:S(2)}, u32[]{:S(2)}) collective-permute-start(f32[72,128]{1,0:T(8,128)S(1)} %screen_stats.1.own_ref), channel_id=1, source_target_pairs={{0,32},{4,36},{8,40},{12,44},{16,48},{20,52},{24,56},{28,60},{32,0... | collective-permute-start | bytes 110600 | tf_op jit(solution)/shard_map/ppermute | solution.py:52
  88.3 0.0 collective-permute-done.4.refs_0_
  88.3 3.5 %collective-permute-start.7 = (f32[72,128]{1,0:T(8,128)S(1)}, f32[72,128]{1,0:T(8,128)S(1)}, u32[]{:S(2)}, u32[]{:S(2)}) collective-permute-start(f32[72,128]{1,0:T(8,128)S(1)} %screen_stats.1.own_ref), channel_id=1, source_target_pairs={{0,224},{4,228},{8,232},{12,236},{16,240},{20,244},{24,248},{28,25... | collective-permute-start | bytes 110600 | tf_op jit(solution)/shard_map/ppermute | solution.py:52
  91.8 0.1 pad_add_fusion.id_ref
  91.9 0.0 collective-permute-start.12
  91.9 5.3 %collective-permute-done.7.refs_3_ = f32[72,128]{1,0:T(8,128)S(1)} collective-permute-done((f32[72,128]{1,0:T(8,128)S(1)}, f32[72,128]{1,0:T(8,128)S(1)}, u32[]{:S(2)}, u32[]{:S(2)}) %collective-permute-start.7) | collective-permute-done | bytes 36896 | tf_op jit(solution)/shard_map/ppermute | solution.py:52
  97.2 6.7 %settle.1 = (bf16[32,128]{1,0:T(8,128)(2,1)S(1)}, bf16[64,32,128]{2,1,0:T(8,128)(2,1)}) custom-call(s32[1,4]{1,0:T(1,128)S(1)} %copy-done.4, s32[2]{0:T(128)S(1)} %pad_add_fusion.id_ref, f32[72,128]{1,0:T(8,128)S(1)} %screen_stats.1.own_ref, f32[72,128]{1,0:T(8,128)S(1)} %collective-permute-done.4.refs_0_, f32[72,128]{1,0:T(8,128)S(1)} %collective-permute-done.5.refs_1_, ...), custom_call_target="tpu_custom_call" | custom-call | tf_op jit(solution)/shard_map/settle/pallas_call | solution.py:511
  103.9 0.0 collective-permute-done.8.refs_8_
  103.9 2.0 %collective-permute-start.15 = (bf16[2560,256]{1,0:T(8,128)(2,1)}, bf16[2560,256]{1,0:T(8,128)(2,1)}, u32[]{:S(2)}, u32[]{:S(2)}) collective-permute-start(bf16[2560,256]{1,0:T(8,128)(2,1)} %collective-permute-done.8.refs_8_), channel_id=1, source_target_pairs={{0,3},{1,0},{2,1},{3,2},{4,7},{5,4},{6,5},{7,6},{8,11},{9,8},{10,9... | collective-permute-start | bytes 3932168 | tf_op jit(solution)/shard_map/ppermute | solution.py:39
  105.9 1.3 collective-permute-start.11
  107.2 0.6 collective-permute-start.10
  107.8 9.5 %all-to-all-start.2 = ((bf16[64,32,128]{2,1,0:T(8,128)(2,1)}), bf16[64,32,128]{2,1,0:T(8,128)(2,1)S(1)}, u32[]{:S(2)}, u32[]{:S(2)}) async-start(bf16[64,32,128]{2,1,0:T(8,128)(2,1)} %get-tuple-element.27), calls=%async_computation.2 | async-start | bytes 1048576 | tf_op jit(solution)/shard_map/all_to_all | solution.py:594
  117.3 0.8 fusion.6
  118.1 0.7 collective-permute-start.13
  118.9 1.8 convolution_add_fusion.1
  120.7 16.0 %collective-permute-done.11 = bf16[256,1024]{1,0:T(8,128)(2,1)} collective-permute-done((bf16[256,1024]{1,0:T(8,128)(2,1)S(1)}, bf16[256,1024]{1,0:T(8,128)(2,1)}, u32[]{:S(2)}, u32[]{:S(2)}) %collective-permute-start.11) | collective-permute-done | bytes 524320 | tf_op jit(solution)/shard_map/ppermute | solution.py:39
  136.7 10.3 %collective-permute-start.14 = (bf16[512,256]{1,0:T(8,128)(2,1)S(1)}, bf16[512,256]{1,0:T(8,128)(2,1)S(1)}, u32[]{:S(2)}, u32[]{:S(2)}) collective-permute-start(bf16[512,256]{1,0:T(8,128)(2,1)S(1)} %collective-permute-done.2.refs_4_), channel_id=1, source_target_pairs={{0,1},{1,2},{2,3},{3,0},{4,5},{5,6},{6,7},{7,4},{8,9},{9,10},{10,1... | collective-permute-start | bytes 786440 | tf_op jit(solution)/shard_map/ppermute | solution.py:39
  147.0 1.8 fusion.2
  148.8 6.8 %collective-permute-done.10 = bf16[256,1024]{1,0:T(8,128)(2,1)} collective-permute-done((bf16[256,1024]{1,0:T(8,128)(2,1)S(1)}, bf16[256,1024]{1,0:T(8,128)(2,1)}, u32[]{:S(2)}, u32[]{:S(2)}) %collective-permute-start.10) | collective-permute-done | bytes 524320 | tf_op jit(solution)/shard_map/ppermute | solution.py:39
  155.6 1.8 %fusion.1 = bf16[32,8,1024]{2,0,1:T(8,128)(2,1)S(1)} fusion(f32[32,8,1024]{2,0,1:T(8,128)S(1)} %fusion.2, f32[32,8,1024]{2,0,1:T(8,128)S(1)} %convolution_add_fusion.1, bf16[32,8,1024]{2,1,0:T(8,128)(2,1)} %bitcast.15, bf16[32,128]{1,0:T(8,128)(2,1)S(1)} %get-tuple-element.20, s32[]{:T(128)S(6)} %select_n.36), kind=kOutput, calls=%fused_computation.3 | convolution fusion | flops 17563648 | bytes 3153924 | tf_op jit(solution)/shard_map/jk,klc->jlc/dot_general | solution.py:600
  157.5 1.1 copy.22
  158.6 0.0 collective-permute-done.13.refs_9_
  158.6 0.0 collective-permute-done.15.refs_11_
  158.6 0.7 copy-done.9
  159.3 0.2 copy-done.6
  159.5 22.8 %mix_land.1 = bf16[256,4096]{1,0:T(8,128)(2,1)} custom-call(s32[2]{0:T(128)} %copy-done.3, s32[64,8]{1,0:T(8,128)} %get-tuple-element.21.start_ref, bf16[1024,256]{1,0:T(8,128)(2,1)} %sort_land.3.refs_0_, bf16[512,256]{1,0:T(8,128)(2,1)} %sort_land.4.refs_1_, bf16[2560,256]{1,0:T(8,128)(2,1)} %sort_land.5.refs_2_, bf16[1024,256]{1,0:T(8,128)(2,1)} %copy-done.7, ...), custom_call_target="tpu_custom_call" | custom-call | tf_op jit(solution)/shard_map/mix_land/pallas_call | solution.py:391
  (27 shorter events, 0.1 us)
Async XLA Ops:
  10.7 33.2 %all-to-all-start = ((bf16[64,34,128]{2,1,0:T(8,128)(2,1)}), bf16[64,34,128]{2,1,0:T(8,128)(2,1)S(1)}, u32[]{:S(2)}, u32[]{:S(2)}) async-start(bf16[64,34,128]{2,1,0:T(8,128)(2,1)} %bucket_tiles.1), calls=%async_computation | async-start | bytes 1310720 | tf_op jit(solution)/shard_map/all_to_all | solution.py:565
  27.2 20.1 %collective-permute-start = (bf16[1024,256]{1,0:T(8,128)(2,1)}, bf16[1024,256]{1,0:T(8,128)(2,1)S(1)}, u32[]{:S(2)}, u32[]{:S(2)}) collective-permute-start(bf16[1024,256]{1,0:T(8,128)(2,1)} %sort_land.3.refs_0_), channel_id=1, source_target_pairs={{0,1},{1,2},{2,3},{3,0},{4,5},{5,6},{6,7},{7,4},{8,9},{9,10},{10,1... | collective-permute-start | bytes 1572872 | tf_op jit(solution)/shard_map/ppermute | solution.py:39
  28.4 18.9 %collective-permute-start.1 = (bf16[1024,256]{1,0:T(8,128)(2,1)}, bf16[1024,256]{1,0:T(8,128)(2,1)}, u32[]{:S(2)}, u32[]{:S(2)}) collective-permute-start(bf16[1024,256]{1,0:T(8,128)(2,1)} %sort_land.3.refs_0_), channel_id=1, source_target_pairs={{0,3},{1,0},{2,1},{3,2},{4,7},{5,4},{6,5},{7,6},{8,11},{9,8},{10,9... | collective-permute-start | bytes 1572872 | tf_op jit(solution)/shard_map/ppermute | solution.py:39
  32.3 8.6 %copy-start.10 = (s32[512]{0:T(512)S(1)}, s32[512]{0:T(512)}, u32[]{:S(2)}) copy-start(s32[512]{0:T(512)} %param.17) | copy-start | bytes 6148
  32.3 11.6 %copy-start = (bf16[32,8,1024]{2,1,0:T(8,128)(2,1)S(1)}, bf16[32,8,1024]{2,1,0:T(8,128)(2,1)}, u32[]{:S(2)}) copy-start(bf16[32,8,1024]{2,1,0:T(8,128)(2,1)} %param.10) | copy-start | bytes 1572868
  32.3 15.0 %collective-permute-start.2 = (bf16[512,256]{1,0:T(8,128)(2,1)}, bf16[512,256]{1,0:T(8,128)(2,1)S(1)}, u32[]{:S(2)}, u32[]{:S(2)}) collective-permute-start(bf16[512,256]{1,0:T(8,128)(2,1)} %sort_land.4.refs_1_), channel_id=1, source_target_pairs={{0,1},{1,2},{2,3},{3,0},{4,5},{5,6},{6,7},{7,4},{8,9},{9,10},{10,1... | collective-permute-start | bytes 786440 | tf_op jit(solution)/shard_map/ppermute | solution.py:39
  32.3 15.0 %collective-permute-start.3 = (bf16[512,256]{1,0:T(8,128)(2,1)}, bf16[512,256]{1,0:T(8,128)(2,1)}, u32[]{:S(2)}, u32[]{:S(2)}) collective-permute-start(bf16[512,256]{1,0:T(8,128)(2,1)} %sort_land.4.refs_1_), channel_id=1, source_target_pairs={{0,3},{1,0},{2,1},{3,2},{4,7},{5,4},{6,5},{7,6},{8,11},{9,8},{10,9... | collective-permute-start | bytes 786440 | tf_op jit(solution)/shard_map/ppermute | solution.py:39
  40.9 6.4 %copy-start.5 = (bf16[2560,256]{1,0:T(8,128)(2,1)S(1)}, bf16[2560,256]{1,0:T(8,128)(2,1)}, u32[]{:S(2)}) copy-start(bf16[2560,256]{1,0:T(8,128)(2,1)} %sort_land.5.refs_2_) | copy-start | bytes 3932164
  40.9 36.5 %copy-start.1 = (f32[512]{0:T(512)S(1)}, f32[512]{0:T(512)}, u32[]{:S(2)}) copy-start(f32[512]{0:T(512)} %param.16) | copy-start | bytes 6148
  40.9 36.5 %copy-start.2 = (f32[512]{0:T(512)S(1)}, f32[512]{0:T(512)}, u32[]{:S(2)}) copy-start(f32[512]{0:T(512)} %param.18) | copy-start | bytes 6148
  40.9 56.3 %copy-start.4 = (s32[1,4]{1,0:T(1,128)S(1)}, s32[1,4]{1,0:T(1,128)}, u32[]{:S(2)}) copy-start(s32[1,4]{1,0:T(1,128)} %list_ref.1) | copy-start | bytes 52
  47.3 89.4 %copy-start.8 = (bf16[512,256]{1,0:T(8,128)(2,1)}, bf16[512,256]{1,0:T(8,128)(2,1)S(1)}, u32[]{:S(2)}) copy-start(bf16[512,256]{1,0:T(8,128)(2,1)S(1)} %collective-permute-done.2.refs_4_) | copy-start | bytes 786436
  47.3 70.8 %copy-start.7 = (bf16[1024,256]{1,0:T(8,128)(2,1)}, bf16[1024,256]{1,0:T(8,128)(2,1)S(1)}, u32[]{:S(2)}) copy-start(bf16[1024,256]{1,0:T(8,128)(2,1)S(1)} %collective-permute-done.refs_3_) | copy-start | bytes 1572868
  47.3 56.6 %collective-permute-start.8 = (bf16[2560,256]{1,0:T(8,128)(2,1)S(1)}, bf16[2560,256]{1,0:T(8,128)(2,1)}, u32[]{:S(2)}, u32[]{:S(2)}) collective-permute-start(bf16[2560,256]{1,0:T(8,128)(2,1)S(1)} %copy-done.5), channel_id=1, source_target_pairs={{0,3},{1,0},{2,1},{3,2},{4,7},{5,4},{6,5},{7,6},{8,11},{9,8},{10,9... | collective-permute-start | bytes 3932168 | tf_op jit(solution)/shard_map/ppermute | solution.py:39
  78.0 10.3 %collective-permute-start.4 = (f32[72,128]{1,0:T(8,128)S(1)}, f32[72,128]{1,0:T(8,128)S(1)}, u32[]{:S(2)}, u32[]{:S(2)}) collective-permute-start(f32[72,128]{1,0:T(8,128)S(1)} %screen_stats.1.own_ref), channel_id=1, source_target_pairs={{0,4},{4,0},{8,12},{12,8},{16,20},{20,16},{24,28},{28,24},{32,36},... | collective-permute-start | bytes 110600 | tf_op jit(solution)/shard_map/ppermute | solution.py:52
  81.1 37.0 %collective-permute-start.9 = (bf16[256,1024]{1,0:T(8,128)(2,1)S(1)}, bf16[256,1024]{1,0:T(8,128)(2,1)}, u32[]{:S(2)}, u32[]{:S(2)}) collective-permute-start(bf16[256,1024]{1,0:T(8,128)(2,1)S(1)} %bitcast.30), channel_id=1, source_target_pairs={{0,1},{1,2},{2,3},{3,0},{4,5},{5,6},{6,7},{7,4},{8,9},{9,10},{10,1... | collective-permute-start | bytes 1572872 | tf_op jit(solution)/shard_map/ppermute | solution.py:39
  82.6 9.3 %collective-permute-start.5 = (f32[72,128]{1,0:T(8,128)S(1)}, f32[72,128]{1,0:T(8,128)S(1)}, u32[]{:S(2)}, u32[]{:S(2)}) collective-permute-start(f32[72,128]{1,0:T(8,128)S(1)} %screen_stats.1.own_ref), channel_id=1, source_target_pairs={{0,252},{4,8},{8,4},{12,16},{16,12},{20,24},{24,20},{28,32},{32,28... | collective-permute-start | bytes 110600 | tf_op jit(solution)/shard_map/ppermute | solution.py:52
  84.1 7.8 %collective-permute-start.6 = (f32[72,128]{1,0:T(8,128)S(1)}, f32[72,128]{1,0:T(8,128)S(1)}, u32[]{:S(2)}, u32[]{:S(2)}) collective-permute-start(f32[72,128]{1,0:T(8,128)S(1)} %screen_stats.1.own_ref), channel_id=1, source_target_pairs={{0,32},{4,36},{8,40},{12,44},{16,48},{20,52},{24,56},{28,60},{32,0... | collective-permute-start | bytes 110600 | tf_op jit(solution)/shard_map/ppermute | solution.py:52
  88.3 8.9 %collective-permute-start.7 = (f32[72,128]{1,0:T(8,128)S(1)}, f32[72,128]{1,0:T(8,128)S(1)}, u32[]{:S(2)}, u32[]{:S(2)}) collective-permute-start(f32[72,128]{1,0:T(8,128)S(1)} %screen_stats.1.own_ref), channel_id=1, source_target_pairs={{0,224},{4,228},{8,232},{12,236},{16,240},{20,244},{24,248},{28,25... | collective-permute-start | bytes 110600 | tf_op jit(solution)/shard_map/ppermute | solution.py:52
  91.9 26.2 %copy-start.3 = (s32[2]{0:T(128)}, s32[2]{0:T(128)S(1)}, u32[]{:S(2)}) copy-start(s32[2]{0:T(128)S(1)} %pad_add_fusion.id_ref) | copy-start | bytes 28
  91.9 66.7 %collective-permute-start.12 = (bf16[2560,256]{1,0:T(8,128)(2,1)S(1)}, bf16[2560,256]{1,0:T(8,128)(2,1)}, u32[]{:S(2)}, u32[]{:S(2)}) collective-permute-start(bf16[2560,256]{1,0:T(8,128)(2,1)S(1)} %copy-done.5), channel_id=1, source_target_pairs={{0,1},{1,2},{2,3},{3,0},{4,5},{5,6},{6,7},{7,4},{8,9},{9,10},{10,1... | collective-permute-start | bytes 3932168 | tf_op jit(solution)/shard_map/ppermute | solution.py:39
  103.9 54.7 %collective-permute-start.15 = (bf16[2560,256]{1,0:T(8,128)(2,1)}, bf16[2560,256]{1,0:T(8,128)(2,1)}, u32[]{:S(2)}, u32[]{:S(2)}) collective-permute-start(bf16[2560,256]{1,0:T(8,128)(2,1)} %collective-permute-done.8.refs_8_), channel_id=1, source_target_pairs={{0,3},{1,0},{2,1},{3,2},{4,7},{5,4},{6,5},{7,6},{8,11},{9,8},{10,9... | collective-permute-start | bytes 3932168 | tf_op jit(solution)/shard_map/ppermute | solution.py:39
  105.9 30.8 %collective-permute-start.11 = (bf16[256,1024]{1,0:T(8,128)(2,1)S(1)}, bf16[256,1024]{1,0:T(8,128)(2,1)}, u32[]{:S(2)}, u32[]{:S(2)}) collective-permute-start(bf16[256,1024]{1,0:T(8,128)(2,1)S(1)} %bitcast.31), channel_id=1, source_target_pairs={{0,2},{1,3},{2,0},{3,1},{4,6},{5,7},{6,4},{7,5},{8,10},{9,11},{10,... | collective-permute-start | bytes 1572872 | tf_op jit(solution)/shard_map/ppermute | solution.py:39
  107.2 48.4 %collective-permute-start.10 = (bf16[256,1024]{1,0:T(8,128)(2,1)S(1)}, bf16[256,1024]{1,0:T(8,128)(2,1)}, u32[]{:S(2)}, u32[]{:S(2)}) collective-permute-start(bf16[256,1024]{1,0:T(8,128)(2,1)S(1)} %bitcast.32), channel_id=1, source_target_pairs={{0,3},{1,0},{2,1},{3,2},{4,7},{5,4},{6,5},{7,6},{8,11},{9,8},{10,9... | collective-permute-start | bytes 1572872 | tf_op jit(solution)/shard_map/ppermute | solution.py:39
  107.8 50.8 %all-to-all-start.2 = ((bf16[64,32,128]{2,1,0:T(8,128)(2,1)}), bf16[64,32,128]{2,1,0:T(8,128)(2,1)S(1)}, u32[]{:S(2)}, u32[]{:S(2)}) async-start(bf16[64,32,128]{2,1,0:T(8,128)(2,1)} %get-tuple-element.27), calls=%async_computation.2 | async-start | bytes 1048576 | tf_op jit(solution)/shard_map/all_to_all | solution.py:594
  118.1 40.4 %collective-permute-start.13 = (bf16[1024,256]{1,0:T(8,128)(2,1)S(1)}, bf16[1024,256]{1,0:T(8,128)(2,1)}, u32[]{:S(2)}, u32[]{:S(2)}) collective-permute-start(bf16[1024,256]{1,0:T(8,128)(2,1)S(1)} %collective-permute-done.refs_3_), channel_id=1, source_target_pairs={{0,1},{1,2},{2,3},{3,0},{4,5},{5,6},{6,7},{7,4},{8,9},{9,10},{10,1... | collective-permute-start | bytes 1572872 | tf_op jit(solution)/shard_map/ppermute | solution.py:39
  136.7 21.9 %collective-permute-start.14 = (bf16[512,256]{1,0:T(8,128)(2,1)S(1)}, bf16[512,256]{1,0:T(8,128)(2,1)S(1)}, u32[]{:S(2)}, u32[]{:S(2)}) collective-permute-start(bf16[512,256]{1,0:T(8,128)(2,1)S(1)} %collective-permute-done.2.refs_4_), channel_id=1, source_target_pairs={{0,1},{1,2},{2,3},{3,0},{4,5},{5,6},{6,7},{7,4},{8,9},{9,10},{10,1... | collective-permute-start | bytes 786440 | tf_op jit(solution)/shard_map/ppermute | solution.py:39
  158.6 0.7 copy-start.9
  158.6 0.9 copy-start.6

commit v6 on v5

--- a/solution.py
+++ b/solution.py
@@ -367,16 +367,21 @@
                 @pl.when(most > 0)
                 def _():
                     for o, (firsts, ends, bases) in zip(group, limits):
-                        for q in range(PARTS):
-
-                            def more(n, unused, o=o, q=q, first=firsts[q], end=ends[q], low=bases[q]):
-                                base = begin(low + (n + 1) * window)
-                                at = pl.multiple_of(q * span + base, 16)
-                                put(q, base, first, end, mixed(o, [at]))
-                                return unused
-
-                            lack = jnp.maximum(ends[q] - bases[q] - window, 0)
-                            lax.fori_loop(0, (lack + window - 1) // window, more, 0)
+                        lacks = [
+                            jnp.maximum(ends[q] - bases[q] - window, 0) for q in range(PARTS)
+                        ]
+
+                        @pl.when(lacks[0] + lacks[1] + lacks[2] + lacks[3] > 0)
+                        def _():
+                            for q in range(PARTS):
+
+                                def more(n, unused, q=q):
+                                    base = begin(bases[q] + (n + 1) * window)
+                                    at = pl.multiple_of(q * span + base, 16)
+                                    put(q, base, firsts[q], ends[q], mixed(o, [at]))
+                                    return unused
+
+                                lax.fori_loop(0, (lacks[q] + window - 1) // window, more, 0)
 
                 return unused
 
@@ -582,15 +587,16 @@
     ensemble = lax.all_to_all(forecast, "mem", split_axis=0, concat_axis=0, tiled=True)
     rest_prev = shifted(rest, "mem", 1)
     rest_next = shifted(rest, "mem", -1)
-    first_far = shifted(first_prev, "mem", 1)
+    first_far = shifted(first_next, "mem", -1)
     second_far = shifted(second_prev, "mem", 1)
 
     own_stats = screen_stats(ensemble, obs_value.reshape(1, -1), obs_error.reshape(1, -1))
     gaps = (1, -1, row_width, -row_width)
     near = [swapped(own_stats, gap, npatch) for gap in gaps]
     own_cols, mixes = settle(own_stats, near, loc_blocks, ids, gaps, local, npatch)
-    own_cols, rest_next = barrier((own_cols, rest_next))
-    rest_far = shifted(rest_next, "mem", -1)
+    own_cols, rest_prev, rest_next = barrier((own_cols, rest_prev, rest_next))
+    half = rest.shape[0] // 2
+    rest_far = [shifted(rest_prev[:half], "mem", 1), shifted(rest_next[half:], "mem", -1)]
     all_mixes = lax.all_to_all(mixes, "patch", split_axis=0, concat_axis=0, tiled=True)
 
     slot_source = [mem_rank, mem_rank - 1, mem_rank + 1, mem_rank - 2]
@@ -607,7 +613,7 @@
             [first, second, rest],
             [first_prev, second_prev, rest_prev],
             [first_next, second_next, rest_next],
-            [first_far, second_far, rest_far],
+            [first_far, second_far] + rest_far,
         ],
         ids,
         starts,

time: 185 us -> 177 us (0.957); the launches traced: 183 us -> 176 us
  blocking collectives: 27.5 us -> 40.5 us
  waiting for transfers between devices: 31.4 us -> 20.1 us
  starting transfers between devices: 59.3 us -> 49 us
  local copies, waits for them, and re-layouts: 2.17 us -> 5.21 us
    all_to_all x1, blocking collectives: 27.5 us -> 40.5 us  [analysis(): lax.all_to_all(forecast, 'mem', split_axis=0, concat_axis=0, tiled=True)]
    ppermute x12 -> x13, starting transfers between devices: 24.3 us -> 12.3 us  [shifted(): return lax.ppermute(value, axis, pairs)]
    ppermute x12 -> x13, waiting for transfers between devices: 23.2 us -> 13.7 us  [shifted(): return lax.ppermute(value, axis, pairs)]
    slice x0 -> x2, local copies, waits for them, and re-layouts: none -> 3.94 us  [the longest x1 1.97 us: analysis(): rest_next[half:]]
  transfers between devices with their start and end apart: 18 -> 19, of which waited for: 5 -> 5; matrix products, arithmetic and copies ran while one was open for 4% -> 7% of each run, Pallas kernels for 12% -> 12%
where the time goes in v6:
time: 177 us; the launch traced here: 176 us
  Pallas kernels  54.2 us (31%)
  starting transfers between devices  49 us (28%)
  blocking collectives  40.5 us (23%)
  waiting for transfers between devices  20.1 us (11%)
  matrix products  6.26 us (4%)
  local copies, waits for them, and re-layouts  5.21 us (3%)
    all_to_all x1, blocking collectives, analysis(): lax.all_to_all(forecast, 'mem', split_axis=0, concat_axis=0, tiled=True)  40.5 us
    pallas_call x1, Pallas kernels, mix_land(): pl.pallas_call(kernel, grid=(PARTS,), out_shape=jax.ShapeDtypeStruct((wid...  22.2 us
    ppermute x4, starting transfers between devices, swapped(): return lax.ppermute(value, 'patch', pairs)  13.9 us
    ppermute x13, waiting for transfers between devices, shifted(): return lax.ppermute(value, axis, pairs)  13.7 us
    all_to_all x1, starting transfers between devices, analysis(): lax.all_to_all(packed, 'patch', split_axis=0, concat_axis=0, tiled=True)  13.1 us
    ppermute x13, starting transfers between devices, shifted(): return lax.ppermute(value, axis, pairs)  12.3 us
    pallas_call x3, Pallas kernels, sort_land(): pl.pallas_call(kernel, grid=(1,), out_shape=jax.ShapeDtypeStruct((end - b...  11.7 us
    all_to_all x1, starting transfers between devices, analysis(): lax.all_to_all(mixes, 'patch', split_axis=0, concat_axis=0, tiled=True)  9.62 us
  transfers between devices with their start and end apart: 19, of which 5 were waited for; matrix products, arithmetic and copies ran while one was open for 7% of the time, Pallas kernels for 12%

profile of v6, /device:TPU:1, one launch (start us, length us, event | category | flops | bytes accessed | tf_op | source)
XLA Modules:
  0.0 176.5 jit_solution(13081083474949856274)
XLA Ops:
  0.6 2.3 %order_tiles.1 = (s32[1,4096]{1,0:T(1,128)}, s32[1,4096]{1,0:T(1,128)}, s32[64,8]{1,0:T(8,128)}) custom-call(s32[1,4096]{1,0:T(1,128)} %bitcast.44), custom_call_target="tpu_custom_call" | custom-call | tf_op jit(solution)/shard_map/order_tiles/pallas_call | solution.py:84
  2.9 7.8 %bucket_tiles.1 = bf16[64,34,128]{2,1,0:T(8,128)(2,1)} custom-call(bf16[256,4096]{1,0:T(8,128)(2,1)} %bitcast.35, bf16[32,128]{1,0:T(8,128)(2,1)} %bitcast.47, s32[32,128]{1,0:T(8,128)} %bitcast.42, s32[1,4096]{1,0:T(1,128)} %bitcast.45, s32[1,4096]{1,0:T(1,128)} %get-tuple-element.16.rank_ref, s32[1,4096]{1,0:T(1,128)} %bitcast.46), custom_call_target="tpu_custom_call" | custom-call | tf_op jit(solution)/shard_map/bucket_tiles/pallas_call | solution.py:163
  10.7 13.1 %all-to-all-start = ((bf16[64,34,128]{2,1,0:T(8,128)(2,1)}), bf16[64,34,128]{2,1,0:T(8,128)(2,1)S(1)}, u32[]{:S(2)}, u32[]{:S(2)}) async-start(bf16[64,34,128]{2,1,0:T(8,128)(2,1)} %bucket_tiles.1), calls=%async_computation | async-start | bytes 1310720 | tf_op jit(solution)/shard_map/all_to_all | solution.py:570
  23.9 3.4 %sort_land.3.refs_0_ = bf16[1024,256]{1,0:T(8,128)(2,1)} custom-call(s32[1,4096]{1,0:T(1,128)} %get-tuple-element.17.pos_ref.refs_14_, bf16[256,4096]{1,0:T(8,128)(2,1)} %bitcast.36), custom_call_target="tpu_custom_call" | custom-call | tf_op jit(solution)/shard_map/sort_land/pallas_call | solution.py:203
  27.2 1.2 collective-permute-start
  28.4 1.5 collective-permute-start.1
  29.9 2.4 %sort_land.4.refs_1_ = bf16[512,256]{1,0:T(8,128)(2,1)} custom-call(s32[1,4096]{1,0:T(1,128)} %get-tuple-element.17.pos_ref.refs_14_, bf16[256,4096]{1,0:T(8,128)(2,1)} %bitcast.37), custom_call_target="tpu_custom_call" | custom-call | tf_op jit(solution)/shard_map/sort_land/pallas_call | solution.py:203
  32.3 0.0 collective-permute-start.2
  32.3 2.7 %collective-permute-start.3 = (bf16[512,256]{1,0:T(8,128)(2,1)}, bf16[512,256]{1,0:T(8,128)(2,1)}, u32[]{:S(2)}, u32[]{:S(2)}) collective-permute-start(bf16[512,256]{1,0:T(8,128)(2,1)} %sort_land.4.refs_1_), channel_id=1, source_target_pairs={{0,3},{1,0},{2,1},{3,2},{4,7},{5,4},{6,5},{7,6},{8,11},{9,8},{10,9... | collective-permute-start | bytes 786440 | tf_op jit(solution)/shard_map/ppermute | solution.py:39
  35.0 5.9 %sort_land.5.refs_2_ = bf16[2560,256]{1,0:T(8,128)(2,1)} custom-call(s32[1,4096]{1,0:T(1,128)} %get-tuple-element.17.pos_ref.refs_14_, bf16[256,4096]{1,0:T(8,128)(2,1)} %bitcast.38), custom_call_target="tpu_custom_call" | custom-call | tf_op jit(solution)/shard_map/sort_land/pallas_call | solution.py:203
  40.9 0.1 copy.17.obs_ref
  41.0 2.9 %all-to-all-done.in_ref = bf16[64,34,128]{2,1,0:T(8,128)(2,1)S(1)} async-done(((bf16[64,34,128]{2,1,0:T(8,128)(2,1)}), bf16[64,34,128]{2,1,0:T(8,128)(2,1)S(1)}, u32[]{:S(2)}, u32[]{:S(2)}) %all-to-all-start) | async-done | bytes 557088 | tf_op jit(solution)/shard_map/all_to_all | solution.py:570
  43.9 3.0 %screen_forecast.1 = bf16[4,32,512]{2,1,0:T(8,128)(2,1)S(1)} custom-call(bf16[64,34,128]{2,1,0:T(8,128)(2,1)S(1)} %all-to-all-done.in_ref, bf16[256,1024]{1,0:T(8,128)(2,1)S(1)} %bitcast.29, s32[512,1]{1,0:T(8,128)S(1)} %copy.17.obs_ref), custom_call_target="tpu_custom_call" | custom-call | tf_op jit(solution)/shard_map/screen_forecast/pallas_call | solution.py:243
  46.9 0.5 collective-permute-done.2.refs_4_
  47.4 0.0 collective-permute-done.1.refs_6_
  47.4 1.0 collective-permute-start.8
  48.4 1.8 %collective-permute-start.9 = (bf16[2560,256]{1,0:T(8,128)(2,1)S(1)}, bf16[2560,256]{1,0:T(8,128)(2,1)}, u32[]{:S(2)}, u32[]{:S(2)}) collective-permute-start(bf16[2560,256]{1,0:T(8,128)(2,1)S(1)} %copy-done.5), channel_id=1, source_target_pairs={{0,3},{1,0},{2,1},{3,2},{4,7},{5,4},{6,5},{7,6},{8,11},{9,8},{10,9... | collective-permute-start | bytes 3932168 | tf_op jit(solution)/shard_map/ppermute | solution.py:39
  50.2 40.5 %all_to_all.15.in_ref = bf16[4,32,512]{2,1,0:T(8,128)(2,1)S(1)} all-to-all(bf16[4,32,512]{2,1,0:T(8,128)(2,1)S(1)} %screen_forecast.1), channel_id=1, replica_groups=mesh['patch'=64,'mem'=4] {'mem'}, dimensions={0} | all-to-all | bytes 262144 | tf_op jit(solution)/shard_map/all_to_all | solution.py:587
  90.7 0.6 screen_stats.1.own_ref
  91.4 2.8 %collective-permute-start.4 = (f32[72,128]{1,0:T(8,128)S(1)}, f32[72,128]{1,0:T(8,128)S(1)}, u32[]{:S(2)}, u32[]{:S(2)}) collective-permute-start(f32[72,128]{1,0:T(8,128)S(1)} %screen_stats.1.own_ref), channel_id=1, source_target_pairs={{0,4},{4,0},{8,12},{12,8},{16,20},{20,16},{24,28},{28,24},{32,36},... | collective-permute-start | bytes 110600 | tf_op jit(solution)/shard_map/ppermute | solution.py:52
  94.2 1.4 collective-permute-start.5
  95.6 0.0 collective-permute-done.4.refs_0_
  95.6 4.8 %collective-permute-start.6 = (f32[72,128]{1,0:T(8,128)S(1)}, f32[72,128]{1,0:T(8,128)S(1)}, u32[]{:S(2)}, u32[]{:S(2)}) collective-permute-start(f32[72,128]{1,0:T(8,128)S(1)} %screen_stats.1.own_ref), channel_id=1, source_target_pairs={{0,32},{4,36},{8,40},{12,44},{16,48},{20,52},{24,56},{28,60},{32,0... | collective-permute-start | bytes 110600 | tf_op jit(solution)/shard_map/ppermute | solution.py:52
  100.4 4.9 %collective-permute-start.7 = (f32[72,128]{1,0:T(8,128)S(1)}, f32[72,128]{1,0:T(8,128)S(1)}, u32[]{:S(2)}, u32[]{:S(2)}) collective-permute-start(f32[72,128]{1,0:T(8,128)S(1)} %screen_stats.1.own_ref), channel_id=1, source_target_pairs={{0,224},{4,228},{8,232},{12,236},{16,240},{20,244},{24,248},{28,25... | collective-permute-start | bytes 110600 | tf_op jit(solution)/shard_map/ppermute | solution.py:52
  105.3 0.1 pad_add_fusion.id_ref
  105.4 0.0 collective-permute-done.6.refs_2_
  105.4 0.4 collective-permute-start.12
  105.8 3.5 %collective-permute-done.7.refs_3_ = f32[72,128]{1,0:T(8,128)S(1)} collective-permute-done((f32[72,128]{1,0:T(8,128)S(1)}, f32[72,128]{1,0:T(8,128)S(1)}, u32[]{:S(2)}, u32[]{:S(2)}) %collective-permute-start.7) | collective-permute-done | bytes 36896 | tf_op jit(solution)/shard_map/ppermute | solution.py:52
  109.3 0.0 collective-permute-start.11
  109.3 6.7 %settle.1 = (bf16[32,128]{1,0:T(8,128)(2,1)S(1)}, bf16[64,32,128]{2,1,0:T(8,128)(2,1)}) custom-call(s32[1,4]{1,0:T(1,128)S(1)} %copy-done.4, s32[2]{0:T(128)S(1)} %pad_add_fusion.id_ref, f32[72,128]{1,0:T(8,128)S(1)} %screen_stats.1.own_ref, f32[72,128]{1,0:T(8,128)S(1)} %collective-permute-done.4.refs_0_, f32[72,128]{1,0:T(8,128)S(1)} %collective-permute-done.5.refs_1_, ...), custom_call_target="tpu_custom_call" | custom-call | tf_op jit(solution)/shard_map/settle/pallas_call | solution.py:516
  116.0 9.6 %all-to-all-start.2 = ((bf16[64,32,128]{2,1,0:T(8,128)(2,1)}), bf16[64,32,128]{2,1,0:T(8,128)(2,1)S(1)}, u32[]{:S(2)}, u32[]{:S(2)}) async-start(bf16[64,32,128]{2,1,0:T(8,128)(2,1)} %get-tuple-element.29), calls=%async_computation.2 | async-start | bytes 1048576 | tf_op jit(solution)/shard_map/all_to_all | solution.py:600
  125.6 0.0 collective-permute-done.8.refs_5_
  125.6 0.7 collective-permute-start.13
  126.4 0.0 collective-permute-done.9.refs_8_
  126.4 2.0 %slice.6 = bf16[1280,256]{1,0:T(8,128)(2,1)} slice(bf16[2560,256]{1,0:T(8,128)(2,1)} %collective-permute-done.8.refs_5_), slice={[0:1280], [0:256]} | slice | bytes 1310720 | tf_op jit(solution)/shard_map/slice | solution.py:599
  128.3 0.9 collective-permute-start.15
  129.2 2.0 %slice.7 = bf16[1280,256]{1,0:T(8,128)(2,1)} slice(bf16[2560,256]{1,0:T(8,128)(2,1)} %collective-permute-done.9.refs_8_), slice={[1280:2560], [0:256]} | slice | bytes 1310720 | tf_op jit(solution)/shard_map/slice | solution.py:599
  131.2 0.8 fusion.6
  132.0 0.0 collective-permute-done.10
  132.0 1.8 %collective-permute-start.16 = (bf16[1280,256]{1,0:T(8,128)(2,1)}, bf16[1280,256]{1,0:T(8,128)(2,1)}, u32[]{:S(2)}, u32[]{:S(2)}) collective-permute-start(bf16[1280,256]{1,0:T(8,128)(2,1)} %slice.7), channel_id=1, source_target_pairs={{0,3},{1,0},{2,1},{3,2},{4,7},{5,4},{6,5},{7,6},{8,11},{9,8},{10,9... | collective-permute-start | bytes 1966088 | tf_op jit(solution)/shard_map/ppermute | solution.py:39
  133.9 1.8 %convolution_add_fusion.1 = f32[32,8,1024]{2,0,1:T(8,128)S(1)} fusion(f32[32,8,1024]{2,0,1:T(8,128)S(1)} %fusion.6, bf16[32,8,1024]{2,1,0:T(8,128)(2,1)} %bitcast.13, bf16[32,128]{1,0:T(8,128)(2,1)S(1)} %get-tuple-element.21, s32[]{:T(128)S(6)} %select_n.34), kind=kOutput, calls=%fused_computation.2 | convolution fusion | flops 17039360 | bytes 2629636 | tf_op jit(solution)/shard_map/jk,klc->jlc/dot_general | solution.py:606
  135.7 0.3 collective-permute-start.14
  136.0 1.8 %fusion.2 = f32[32,8,1024]{2,0,1:T(8,128)S(1)} fusion(bf16[32,8,1024]{2,1,0:T(8,128)(2,1)} %bitcast.17, bf16[32,128]{1,0:T(8,128)(2,1)S(1)} %get-tuple-element.21, s32[]{:T(128)S(6)} %select_n.38), kind=kOutput, calls=%fused_computation.4 | convolution fusion | flops 16777216 | bytes 1581060 | tf_op jit(solution)/shard_map/jk,klc->jlc/dot_general | solution.py:606
  137.9 1.8 %fusion.1 = bf16[32,8,1024]{2,0,1:T(8,128)(2,1)S(1)} fusion(f32[32,8,1024]{2,0,1:T(8,128)S(1)} %fusion.2, f32[32,8,1024]{2,0,1:T(8,128)S(1)} %convolution_add_fusion.1, bf16[32,8,1024]{2,1,0:T(8,128)(2,1)} %bitcast.15, bf16[32,128]{1,0:T(8,128)(2,1)S(1)} %get-tuple-element.21, s32[]{:T(128)S(6)} %select_n.36), kind=kOutput, calls=%fused_computation.3 | convolution fusion | flops 17563648 | bytes 3153924 | tf_op jit(solution)/shard_map/jk,klc->jlc/dot_general | solution.py:606
  139.7 1.1 copy.22
  140.8 10.1 %collective-permute-done.14.refs_10_ = bf16[512,256]{1,0:T(8,128)(2,1)S(1)} collective-permute-done((bf16[512,256]{1,0:T(8,128)(2,1)}, bf16[512,256]{1,0:T(8,128)(2,1)S(1)}, u32[]{:S(2)}, u32[]{:S(2)}) %collective-permute-start.14) | collective-permute-done | bytes 262176 | tf_op jit(solution)/shard_map/ppermute | solution.py:39
  151.0 3.1 %collective-permute-done.16.refs_12_ = bf16[1280,256]{1,0:T(8,128)(2,1)} collective-permute-done((bf16[1280,256]{1,0:T(8,128)(2,1)}, bf16[1280,256]{1,0:T(8,128)(2,1)}, u32[]{:S(2)}, u32[]{:S(2)}) %collective-permute-start.16) | collective-permute-done | bytes 655392 | tf_op jit(solution)/shard_map/ppermute | solution.py:39
  154.1 22.2 %mix_land.1 = bf16[256,4096]{1,0:T(8,128)(2,1)} custom-call(s32[2]{0:T(128)} %copy-done.3, s32[64,8]{1,0:T(8,128)} %get-tuple-element.22.start_ref, bf16[1024,256]{1,0:T(8,128)(2,1)} %sort_land.3.refs_0_, bf16[512,256]{1,0:T(8,128)(2,1)} %sort_land.4.refs_1_, bf16[2560,256]{1,0:T(8,128)(2,1)} %sort_land.5.refs_2_, bf16[1024,256]{1,0:T(8,128)(2,1)} %copy-done.8, ...), custom_call_target="tpu_custom_call" | custom-call | tf_op jit(solution)/shard_map/mix_land/pallas_call | solution.py:396
  (31 shorter events, 0.1 us)
Async XLA Ops:
  10.7 33.2 %all-to-all-start = ((bf16[64,34,128]{2,1,0:T(8,128)(2,1)}), bf16[64,34,128]{2,1,0:T(8,128)(2,1)S(1)}, u32[]{:S(2)}, u32[]{:S(2)}) async-start(bf16[64,34,128]{2,1,0:T(8,128)(2,1)} %bucket_tiles.1), calls=%async_computation | async-start | bytes 1310720 | tf_op jit(solution)/shard_map/all_to_all | solution.py:570
  27.2 20.2 %collective-permute-start = (bf16[1024,256]{1,0:T(8,128)(2,1)}, bf16[1024,256]{1,0:T(8,128)(2,1)S(1)}, u32[]{:S(2)}, u32[]{:S(2)}) collective-permute-start(bf16[1024,256]{1,0:T(8,128)(2,1)} %sort_land.3.refs_0_), channel_id=1, source_target_pairs={{0,1},{1,2},{2,3},{3,0},{4,5},{5,6},{6,7},{7,4},{8,9},{9,10},{10,1... | collective-permute-start | bytes 1572872 | tf_op jit(solution)/shard_map/ppermute | solution.py:39
  28.4 19.0 %collective-permute-start.1 = (bf16[1024,256]{1,0:T(8,128)(2,1)}, bf16[1024,256]{1,0:T(8,128)(2,1)}, u32[]{:S(2)}, u32[]{:S(2)}) collective-permute-start(bf16[1024,256]{1,0:T(8,128)(2,1)} %sort_land.3.refs_0_), channel_id=1, source_target_pairs={{0,3},{1,0},{2,1},{3,2},{4,7},{5,4},{6,5},{7,6},{8,11},{9,8},{10,9... | collective-permute-start | bytes 1572872 | tf_op jit(solution)/shard_map/ppermute | solution.py:39
  32.3 8.6 %copy-start.10 = (s32[512]{0:T(512)S(1)}, s32[512]{0:T(512)}, u32[]{:S(2)}) copy-start(s32[512]{0:T(512)} %param.17) | copy-start | bytes 6148
  32.3 11.6 %copy-start = (bf16[32,8,1024]{2,1,0:T(8,128)(2,1)S(1)}, bf16[32,8,1024]{2,1,0:T(8,128)(2,1)}, u32[]{:S(2)}) copy-start(bf16[32,8,1024]{2,1,0:T(8,128)(2,1)} %param.10) | copy-start | bytes 1572868
  32.3 15.1 %collective-permute-start.2 = (bf16[512,256]{1,0:T(8,128)(2,1)}, bf16[512,256]{1,0:T(8,128)(2,1)}, u32[]{:S(2)}, u32[]{:S(2)}) collective-permute-start(bf16[512,256]{1,0:T(8,128)(2,1)} %sort_land.4.refs_1_), channel_id=1, source_target_pairs={{0,1},{1,2},{2,3},{3,0},{4,5},{5,6},{6,7},{7,4},{8,9},{9,10},{10,1... | collective-permute-start | bytes 786440 | tf_op jit(solution)/shard_map/ppermute | solution.py:39
  32.3 15.1 %collective-permute-start.3 = (bf16[512,256]{1,0:T(8,128)(2,1)}, bf16[512,256]{1,0:T(8,128)(2,1)}, u32[]{:S(2)}, u32[]{:S(2)}) collective-permute-start(bf16[512,256]{1,0:T(8,128)(2,1)} %sort_land.4.refs_1_), channel_id=1, source_target_pairs={{0,3},{1,0},{2,1},{3,2},{4,7},{5,4},{6,5},{7,6},{8,11},{9,8},{10,9... | collective-permute-start | bytes 786440 | tf_op jit(solution)/shard_map/ppermute | solution.py:39
  40.9 6.5 %copy-start.5 = (bf16[2560,256]{1,0:T(8,128)(2,1)S(1)}, bf16[2560,256]{1,0:T(8,128)(2,1)}, u32[]{:S(2)}) copy-start(bf16[2560,256]{1,0:T(8,128)(2,1)} %sort_land.5.refs_2_) | copy-start | bytes 3932164
  40.9 49.8 %copy-start.1 = (f32[512]{0:T(512)S(1)}, f32[512]{0:T(512)}, u32[]{:S(2)}) copy-start(f32[512]{0:T(512)} %param.16) | copy-start | bytes 6148
  40.9 49.8 %copy-start.2 = (f32[512]{0:T(512)S(1)}, f32[512]{0:T(512)}, u32[]{:S(2)}) copy-start(f32[512]{0:T(512)} %param.18) | copy-start | bytes 6148
  40.9 68.4 %copy-start.4 = (s32[1,4]{1,0:T(1,128)S(1)}, s32[1,4]{1,0:T(1,128)}, u32[]{:S(2)}) copy-start(s32[1,4]{1,0:T(1,128)} %list_ref.1) | copy-start | bytes 52
  47.4 79.0 %copy-start.8 = (bf16[1024,256]{1,0:T(8,128)(2,1)}, bf16[1024,256]{1,0:T(8,128)(2,1)S(1)}, u32[]{:S(2)}) copy-start(bf16[1024,256]{1,0:T(8,128)(2,1)S(1)} %collective-permute-done.refs_3_) | copy-start | bytes 1572868
  47.4 78.2 %collective-permute-start.8 = (bf16[2560,256]{1,0:T(8,128)(2,1)S(1)}, bf16[2560,256]{1,0:T(8,128)(2,1)}, u32[]{:S(2)}, u32[]{:S(2)}) collective-permute-start(bf16[2560,256]{1,0:T(8,128)(2,1)S(1)} %copy-done.5), channel_id=1, source_target_pairs={{0,1},{1,2},{2,3},{3,0},{4,5},{5,6},{6,7},{7,4},{8,9},{9,10},{10,1... | collective-permute-start | bytes 3932168 | tf_op jit(solution)/shard_map/ppermute | solution.py:39
  48.4 78.0 %collective-permute-start.9 = (bf16[2560,256]{1,0:T(8,128)(2,1)S(1)}, bf16[2560,256]{1,0:T(8,128)(2,1)}, u32[]{:S(2)}, u32[]{:S(2)}) collective-permute-start(bf16[2560,256]{1,0:T(8,128)(2,1)S(1)} %copy-done.5), channel_id=1, source_target_pairs={{0,3},{1,0},{2,1},{3,2},{4,7},{5,4},{6,5},{7,6},{8,11},{9,8},{10,9... | collective-permute-start | bytes 3932168 | tf_op jit(solution)/shard_map/ppermute | solution.py:39
  50.2 81.8 %collective-permute-start.10 = (bf16[256,1024]{1,0:T(8,128)(2,1)S(1)}, bf16[256,1024]{1,0:T(8,128)(2,1)}, u32[]{:S(2)}, u32[]{:S(2)}) collective-permute-start(bf16[256,1024]{1,0:T(8,128)(2,1)S(1)} %bitcast.30), channel_id=1, source_target_pairs={{0,1},{1,2},{2,3},{3,0},{4,5},{5,6},{6,7},{7,4},{8,9},{9,10},{10,1... | collective-permute-start | bytes 1572872 | tf_op jit(solution)/shard_map/ppermute | solution.py:39
  91.4 4.2 %collective-permute-start.4 = (f32[72,128]{1,0:T(8,128)S(1)}, f32[72,128]{1,0:T(8,128)S(1)}, u32[]{:S(2)}, u32[]{:S(2)}) collective-permute-start(f32[72,128]{1,0:T(8,128)S(1)} %screen_stats.1.own_ref), channel_id=1, source_target_pairs={{0,4},{4,0},{8,12},{12,8},{16,20},{20,16},{24,28},{28,24},{32,36},... | collective-permute-start | bytes 110600 | tf_op jit(solution)/shard_map/ppermute | solution.py:52
  94.2 6.2 %collective-permute-start.5 = (f32[72,128]{1,0:T(8,128)S(1)}, f32[72,128]{1,0:T(8,128)S(1)}, u32[]{:S(2)}, u32[]{:S(2)}) collective-permute-start(f32[72,128]{1,0:T(8,128)S(1)} %screen_stats.1.own_ref), channel_id=1, source_target_pairs={{0,252},{4,8},{8,4},{12,16},{16,12},{20,24},{24,20},{28,32},{32,28... | collective-permute-start | bytes 110600 | tf_op jit(solution)/shard_map/ppermute | solution.py:52
  95.6 9.8 %collective-permute-start.6 = (f32[72,128]{1,0:T(8,128)S(1)}, f32[72,128]{1,0:T(8,128)S(1)}, u32[]{:S(2)}, u32[]{:S(2)}) collective-permute-start(f32[72,128]{1,0:T(8,128)S(1)} %screen_stats.1.own_ref), channel_id=1, source_target_pairs={{0,32},{4,36},{8,40},{12,44},{16,48},{20,52},{24,56},{28,60},{32,0... | collective-permute-start | bytes 110600 | tf_op jit(solution)/shard_map/ppermute | solution.py:52
  100.4 8.9 %collective-permute-start.7 = (f32[72,128]{1,0:T(8,128)S(1)}, f32[72,128]{1,0:T(8,128)S(1)}, u32[]{:S(2)}, u32[]{:S(2)}) collective-permute-start(f32[72,128]{1,0:T(8,128)S(1)} %screen_stats.1.own_ref), channel_id=1, source_target_pairs={{0,224},{4,228},{8,232},{12,236},{16,240},{20,244},{24,248},{28,25... | collective-permute-start | bytes 110600 | tf_op jit(solution)/shard_map/ppermute | solution.py:52
  105.4 23.0 %copy-start.3 = (s32[2]{0:T(128)}, s32[2]{0:T(128)S(1)}, u32[]{:S(2)}) copy-start(s32[2]{0:T(128)S(1)} %pad_add_fusion.id_ref) | copy-start | bytes 28
  105.4 30.3 %collective-permute-start.12 = (bf16[256,1024]{1,0:T(8,128)(2,1)S(1)}, bf16[256,1024]{1,0:T(8,128)(2,1)}, u32[]{:S(2)}, u32[]{:S(2)}) collective-permute-start(bf16[256,1024]{1,0:T(8,128)(2,1)S(1)} %bitcast.31), channel_id=1, source_target_pairs={{0,2},{1,3},{2,0},{3,1},{4,6},{5,7},{6,4},{7,5},{8,10},{9,11},{10,... | collective-permute-start | bytes 1572872 | tf_op jit(solution)/shard_map/ppermute | solution.py:39
  109.3 28.6 %collective-permute-start.11 = (bf16[256,1024]{1,0:T(8,128)(2,1)S(1)}, bf16[256,1024]{1,0:T(8,128)(2,1)}, u32[]{:S(2)}, u32[]{:S(2)}) collective-permute-start(bf16[256,1024]{1,0:T(8,128)(2,1)S(1)} %bitcast.32), channel_id=1, source_target_pairs={{0,3},{1,0},{2,1},{3,2},{4,7},{5,4},{6,5},{7,6},{8,11},{9,8},{10,9... | collective-permute-start | bytes 1572872 | tf_op jit(solution)/shard_map/ppermute | solution.py:39
  116.0 35.0 %all-to-all-start.2 = ((bf16[64,32,128]{2,1,0:T(8,128)(2,1)}), bf16[64,32,128]{2,1,0:T(8,128)(2,1)S(1)}, u32[]{:S(2)}, u32[]{:S(2)}) async-start(bf16[64,32,128]{2,1,0:T(8,128)(2,1)} %get-tuple-element.29), calls=%async_computation.2 | async-start | bytes 1048576 | tf_op jit(solution)/shard_map/all_to_all | solution.py:600
  125.6 25.3 %collective-permute-start.13 = (bf16[1024,256]{1,0:T(8,128)(2,1)}, bf16[1024,256]{1,0:T(8,128)(2,1)}, u32[]{:S(2)}, u32[]{:S(2)}) collective-permute-start(bf16[1024,256]{1,0:T(8,128)(2,1)} %collective-permute-done.1.refs_6_), channel_id=1, source_target_pairs={{0,3},{1,0},{2,1},{3,2},{4,7},{5,4},{6,5},{7,6},{8,11},{9,8},{10,9... | collective-permute-start | bytes 1572872 | tf_op jit(solution)/shard_map/ppermute | solution.py:39
  128.3 22.6 %collective-permute-start.15 = (bf16[1280,256]{1,0:T(8,128)(2,1)}, bf16[1280,256]{1,0:T(8,128)(2,1)S(1)}, u32[]{:S(2)}, u32[]{:S(2)}) collective-permute-start(bf16[1280,256]{1,0:T(8,128)(2,1)} %slice.6), channel_id=1, source_target_pairs={{0,1},{1,2},{2,3},{3,0},{4,5},{5,6},{6,7},{7,4},{8,9},{9,10},{10,1... | collective-permute-start | bytes 1966088 | tf_op jit(solution)/shard_map/ppermute | solution.py:39
  132.0 22.1 %collective-permute-start.16 = (bf16[1280,256]{1,0:T(8,128)(2,1)}, bf16[1280,256]{1,0:T(8,128)(2,1)}, u32[]{:S(2)}, u32[]{:S(2)}) collective-permute-start(bf16[1280,256]{1,0:T(8,128)(2,1)} %slice.7), channel_id=1, source_target_pairs={{0,3},{1,0},{2,1},{3,2},{4,7},{5,4},{6,5},{7,6},{8,11},{9,8},{10,9... | collective-permute-start | bytes 1966088 | tf_op jit(solution)/shard_map/ppermute | solution.py:39
  135.7 15.2 %collective-permute-start.14 = (bf16[512,256]{1,0:T(8,128)(2,1)}, bf16[512,256]{1,0:T(8,128)(2,1)S(1)}, u32[]{:S(2)}, u32[]{:S(2)}) collective-permute-start(bf16[512,256]{1,0:T(8,128)(2,1)} %collective-permute-done.2.refs_4_), channel_id=1, source_target_pairs={{0,1},{1,2},{2,3},{3,0},{4,5},{5,6},{6,7},{7,4},{8,9},{9,10},{10,1... | collective-permute-start | bytes 786440 | tf_op jit(solution)/shard_map/ppermute | solution.py:39
  150.9 3.2 %copy-start.9 = (bf16[512,256]{1,0:T(8,128)(2,1)}, bf16[512,256]{1,0:T(8,128)(2,1)S(1)}, u32[]{:S(2)}) copy-start(bf16[512,256]{1,0:T(8,128)(2,1)S(1)} %collective-permute-done.14.refs_10_) | copy-start | bytes 786436
  150.9 3.1 %copy-start.6 = (bf16[64,32,128]{2,1,0:T(8,128)(2,1)}, bf16[64,32,128]{2,1,0:T(8,128)(2,1)S(1)}, u32[]{:S(2)}) copy-start(bf16[64,32,128]{2,1,0:T(8,128)(2,1)S(1)} %all-to-all-done.2) | copy-start | bytes 1572868
  151.0 3.1 %copy-start.7 = (bf16[1280,256]{1,0:T(8,128)(2,1)}, bf16[1280,256]{1,0:T(8,128)(2,1)S(1)}, u32[]{:S(2)}) copy-start(bf16[1280,256]{1,0:T(8,128)(2,1)S(1)} %collective-permute-done.15.refs_11_) | copy-start | bytes 1966084

commit v7 on v6

--- a/solution.py
+++ b/solution.py
@@ -182,33 +182,36 @@
     return ((source % b) * a + source // b == target).astype(F32).astype(BF)
 
 
-def sort_land(pos, land_rows, levels, begin, end):
+def sort_land(pos, land_rows, levels, *cuts):
     width, tiles = land_rows.shape
     span = tiles // PARTS
     block = 512
-    one = end - begin <= span and begin // span == (end - 1) // span
+    begin, end = cuts[0], cuts[-1]
+    one = begin // span == (end - 1) // span
     taken = span if one else tiles
     shift = begin // span * span if one else 0
-
-    def kernel(pos_ref, x_ref, out_ref):
+    sizes = [b - a for a, b in zip(cuts, cuts[1:])]
+
+    def kernel(pos_ref, x_ref, *out_refs):
         swap = lane_swap(width, width // levels, levels)
-        for at in range(begin, end, block):
-            part = at // span * span
-            cut = slice(part - shift, part - shift + span)
-            place = iota((block, span), 0) + (at - part)
-            hot = (place == pos_ref[:, cut]).astype(F32).astype(BF)
-            moved = dot(hot, x_ref[:, cut], NT).astype(BF)
-            out_ref[at - begin : at - begin + block, :] = dot(moved, swap).astype(BF)
+        for out_ref, first, last in zip(out_refs, cuts, cuts[1:]):
+            for at in range(first, last, block):
+                part = at // span * span
+                cut = slice(part - shift, part - shift + span)
+                place = iota((block, span), 0) + (at - part)
+                hot = (place == pos_ref[:, cut]).astype(F32).astype(BF)
+                moved = dot(hot, x_ref[:, cut], NT).astype(BF)
+                out_ref[at - first : at - first + block, :] = dot(moved, swap).astype(BF)
 
     return pl.pallas_call(
         kernel,
         grid=(1,),
-        out_shape=jax.ShapeDtypeStruct((end - begin, width), BF),
+        out_shape=[jax.ShapeDtypeStruct((size, width), BF) for size in sizes],
         in_specs=[
             pl.BlockSpec((1, taken), lambda i: (0, shift // taken)),
             pl.BlockSpec((width, taken), lambda i: (0, shift // taken)),
         ],
-        out_specs=pl.BlockSpec((end - begin, width), lambda i: (0, 0)),
+        out_specs=[pl.BlockSpec((size, width), lambda i: (0, 0)) for size in sizes],
         compiler_params=params(60),
         name="sort_land",
     )(pos, land_rows)
@@ -527,6 +530,20 @@
     )(listed, ids, own, *near)
 
 
+def repeat(value):
+    def kernel(in_ref, out_ref):
+        out_ref[...] = in_ref[...]
+
+    return pl.pallas_call(
+        kernel,
+        out_shape=jax.ShapeDtypeStruct(value.shape, value.dtype),
+        in_specs=[VMEM],
+        out_specs=VMEM,
+        compiler_params=params(1),
+        name="repeat",
+    )(value)
+
+
 def analysis(
     atmos,
     land,
@@ -570,33 +587,36 @@
     received = lax.all_to_all(packed, "patch", split_axis=0, concat_axis=0, tiled=True)
 
     early = (tiles // PARTS, 3 * tiles // (2 * PARTS))
-    first = sort_land(pos, land_rows, layers, 0, early[0])
+    late = 3 * tiles // PARTS
+    (first,) = sort_land(pos, land_rows, layers, 0, early[0])
     first_prev = shifted(first, "mem", 1)
     first_next = shifted(first, "mem", -1)
-    second = sort_land(pos, land_rows, layers, *early)
+    (second,) = sort_land(pos, land_rows, layers, *early)
     second_prev = shifted(second, "mem", 1)
     second_next = shifted(second, "mem", -1)
-    rest = sort_land(pos, land_rows, layers, early[1], tiles)
+    third, fourth = sort_land(pos, land_rows, layers, early[1], late, tiles)
 
     forecast = screen_forecast(
         received, atmos_rows, levels, observation_column.reshape(-1, 1), mem_count
     )
-    forecast, first_prev, first_next, second_prev, second_next, rest = barrier(
-        (forecast, first_prev, first_next, second_prev, second_next, rest)
+    forecast, first_prev, first_next, second_prev, second_next, third, fourth = barrier(
+        (forecast, first_prev, first_next, second_prev, second_next, third, fourth)
     )
     ensemble = lax.all_to_all(forecast, "mem", split_axis=0, concat_axis=0, tiled=True)
-    rest_prev = shifted(rest, "mem", 1)
-    rest_next = shifted(rest, "mem", -1)
+    third_prev = shifted(third, "mem", 1)
+    third_next = shifted(third, "mem", -1)
+    fourth_prev = shifted(fourth, "mem", 1)
+    fourth_next = shifted(fourth, "mem", -1)
     first_far = shifted(first_next, "mem", -1)
     second_far = shifted(second_prev, "mem", 1)
+    third_far = shifted(third_prev, "mem", 1)
 
     own_stats = screen_stats(ensemble, obs_value.reshape(1, -1), obs_error.reshape(1, -1))
     gaps = (1, -1, row_width, -row_width)
     near = [swapped(own_stats, gap, npatch) for gap in gaps]
     own_cols, mixes = settle(own_stats, near, loc_blocks, ids, gaps, local, npatch)
-    own_cols, rest_prev, rest_next = barrier((own_cols, rest_prev, rest_next))
-    half = rest.shape[0] // 2
-    rest_far = [shifted(rest_prev[:half], "mem", 1), shifted(rest_next[half:], "mem", -1)]
+    own_cols = repeat(own_cols)
+    fourth_far = shifted(fourth_next, "mem", -1)
     all_mixes = lax.all_to_all(mixes, "patch", split_axis=0, concat_axis=0, tiled=True)
 
     slot_source = [mem_rank, mem_rank - 1, mem_rank + 1, mem_rank - 2]
@@ -610,10 +630,10 @@
 
     land_out = mix_land(
         [
-            [first, second, rest],
-            [first_prev, second_prev, rest_prev],
-            [first_next, second_next, rest_next],
-            [first_far, second_far] + rest_far,
+            [first, second, third, fourth],
+            [first_prev, second_prev, third_prev, fourth_prev],
+            [first_next, second_next, third_next, fourth_next],
+            [first_far, second_far, third_far, fourth_far],
         ],
         ids,
         starts,

time: 177 us -> 194 us (1.096)
  waiting for transfers between devices: 20.1 us -> 36.9 us
    ppermute x13 -> x15, waiting for transfers between devices: 13.7 us -> 29.9 us  [shifted(): return lax.ppermute(value, axis, pairs)]
    slice x2 -> x0, local copies, waits for them, and re-layouts: 3.94 us -> none  [the longest x1 1.97 us: analysis(): rest_next[half:]]
    unnamed x23 -> x35, local copies, waits for them, and re-layouts: 1.13 us -> 3.98 us
    ppermute x13 -> x15, starting transfers between devices: 12.3 us -> 14.4 us  [shifted(): return lax.ppermute(value, axis, pairs)]
    pallas_call x3 -> x4, Pallas kernels: 11.7 us -> 11.4 us  [the longest x3 11.4 us: sort_land(): pl.pallas_call(kernel, grid=(1,), out_shape=[jax.ShapeDtypeStruct((size,...]
  transfers between devices with their start and end apart: 19 -> 21, of which waited for: 5 -> 6; matrix products, arithmetic and copies ran while one was open for 7% -> 4% of each run, Pallas kernels for 12% -> 11%
where the time goes in v7:
time: 194 us; the launch traced here: 193 us
  Pallas kernels  53.9 us (28%)
  starting transfers between devices  50.8 us (26%)
  blocking collectives  39.9 us (21%)
  waiting for transfers between devices  36.9 us (19%)
  matrix products  6.25 us (3%)
  local copies, waits for them, and re-layouts  4.12 us (2%)
    all_to_all x1, blocking collectives, analysis(): lax.all_to_all(forecast, 'mem', split_axis=0, concat_axis=0, tiled=True)  39.9 us
    ppermute x15, waiting for transfers between devices, shifted(): return lax.ppermute(value, axis, pairs)  29.9 us
    pallas_call x1, Pallas kernels, mix_land(): pl.pallas_call(kernel, grid=(PARTS,), out_shape=jax.ShapeDtypeStruct((wid...  22.1 us
    ppermute x15, starting transfers between devices, shifted(): return lax.ppermute(value, axis, pairs)  14.4 us
    ppermute x4, starting transfers between devices, swapped(): return lax.ppermute(value, 'patch', pairs)  13.6 us
    all_to_all x1, starting transfers between devices, analysis(): lax.all_to_all(packed, 'patch', split_axis=0, concat_axis=0, tiled=True)  13.1 us
    pallas_call x3, Pallas kernels, sort_land(): pl.pallas_call(kernel, grid=(1,), out_shape=[jax.ShapeDtypeStruct((size,...  11.4 us
    all_to_all x1, starting transfers between devices, analysis(): lax.all_to_all(mixes, 'patch', split_axis=0, concat_axis=0, tiled=True)  9.63 us
  transfers between devices with their start and end apart: 21, of which 6 were waited for; matrix products, arithmetic and copies ran while one was open for 4% of the time, Pallas kernels for 11%

profile of v7, /device:TPU:1, one launch (start us, length us, event | category | flops | bytes accessed | tf_op | source)
XLA Modules:
  0.0 193.0 jit_solution(13610577262333980765)
XLA Ops:
  0.6 2.3 %order_tiles.1 = (s32[1,4096]{1,0:T(1,128)}, s32[1,4096]{1,0:T(1,128)}, s32[64,8]{1,0:T(8,128)}) custom-call(s32[1,4096]{1,0:T(1,128)} %bitcast.44), custom_call_target="tpu_custom_call" | custom-call | tf_op jit(solution)/shard_map/order_tiles/pallas_call | solution.py:84
  2.9 7.7 %bucket_tiles.1 = bf16[64,34,128]{2,1,0:T(8,128)(2,1)} custom-call(bf16[256,4096]{1,0:T(8,128)(2,1)} %bitcast.35, bf16[32,128]{1,0:T(8,128)(2,1)} %bitcast.47, s32[32,128]{1,0:T(8,128)} %bitcast.42, s32[1,4096]{1,0:T(1,128)} %bitcast.45, s32[1,4096]{1,0:T(1,128)} %get-tuple-element.16.rank_ref, s32[1,4096]{1,0:T(1,128)} %bitcast.46), custom_call_target="tpu_custom_call" | custom-call | tf_op jit(solution)/shard_map/bucket_tiles/pallas_call | solution.py:163
  10.7 13.1 %all-to-all-start = ((bf16[64,34,128]{2,1,0:T(8,128)(2,1)}), bf16[64,34,128]{2,1,0:T(8,128)(2,1)S(1)}, u32[]{:S(2)}, u32[]{:S(2)}) async-start(bf16[64,34,128]{2,1,0:T(8,128)(2,1)} %bucket_tiles.1), calls=%async_computation | async-start | bytes 1310720 | tf_op jit(solution)/shard_map/all_to_all | solution.py:587
  23.8 3.3 %sort_land.3.refs_0_ = bf16[1024,256]{1,0:T(8,128)(2,1)} custom-call(s32[1,4096]{1,0:T(1,128)} %get-tuple-element.17.pos_ref.refs_17_, bf16[256,4096]{1,0:T(8,128)(2,1)} %bitcast.36), custom_call_target="tpu_custom_call" | custom-call | tf_op jit(solution)/shard_map/sort_land/pallas_call | solution.py:206
  27.2 1.2 collective-permute-start
  28.4 1.5 collective-permute-start.1
  29.9 2.5 %sort_land.4.refs_1_ = bf16[512,256]{1,0:T(8,128)(2,1)} custom-call(s32[1,4096]{1,0:T(1,128)} %get-tuple-element.17.pos_ref.refs_17_, bf16[256,4096]{1,0:T(8,128)(2,1)} %bitcast.37), custom_call_target="tpu_custom_call" | custom-call | tf_op jit(solution)/shard_map/sort_land/pallas_call | solution.py:206
  32.3 2.7 %collective-permute-start.3 = (bf16[512,256]{1,0:T(8,128)(2,1)}, bf16[512,256]{1,0:T(8,128)(2,1)S(1)}, u32[]{:S(2)}, u32[]{:S(2)}) collective-permute-start(bf16[512,256]{1,0:T(8,128)(2,1)} %sort_land.4.refs_1_), channel_id=1, source_target_pairs={{0,3},{1,0},{2,1},{3,2},{4,7},{5,4},{6,5},{7,6},{8,11},{9,8},{10,9... | collective-permute-start | bytes 786440 | tf_op jit(solution)/shard_map/ppermute | solution.py:39
  35.0 5.6 %sort_land.5 = (bf16[1536,256]{1,0:T(8,128)(2,1)}, bf16[1024,256]{1,0:T(8,128)(2,1)}) custom-call(s32[1,4096]{1,0:T(1,128)} %get-tuple-element.17.pos_ref.refs_17_, bf16[256,4096]{1,0:T(8,128)(2,1)} %bitcast.38), custom_call_target="tpu_custom_call" | custom-call | tf_op jit(solution)/shard_map/sort_land/pallas_call | solution.py:206
  40.6 0.1 copy.17.obs_ref
  40.8 3.2 %all-to-all-done.in_ref = bf16[64,34,128]{2,1,0:T(8,128)(2,1)S(1)} async-done(((bf16[64,34,128]{2,1,0:T(8,128)(2,1)}), bf16[64,34,128]{2,1,0:T(8,128)(2,1)S(1)}, u32[]{:S(2)}, u32[]{:S(2)}) %all-to-all-start) | async-done | bytes 557088 | tf_op jit(solution)/shard_map/all_to_all | solution.py:587
  43.9 3.0 %screen_forecast.1 = bf16[4,32,512]{2,1,0:T(8,128)(2,1)S(1)} custom-call(bf16[64,34,128]{2,1,0:T(8,128)(2,1)S(1)} %all-to-all-done.in_ref, bf16[256,1024]{1,0:T(8,128)(2,1)S(1)} %bitcast.29, s32[512,1]{1,0:T(8,128)S(1)} %copy.17.obs_ref), custom_call_target="tpu_custom_call" | custom-call | tf_op jit(solution)/shard_map/screen_forecast/pallas_call | solution.py:246
  46.9 0.3 collective-permute-done.2.refs_5_
  47.3 0.8 copy-done.9
  48.1 0.2 copy-done.10
  48.3 0.9 collective-permute-start.11
  49.2 1.2 collective-permute-start.8
  50.4 1.8 collective-permute-start.10
  52.2 39.9 %all_to_all.15.in_ref = bf16[4,32,512]{2,1,0:T(8,128)(2,1)S(1)} all-to-all(bf16[4,32,512]{2,1,0:T(8,128)(2,1)S(1)} %screen_forecast.1), channel_id=1, replica_groups=mesh['patch'=64,'mem'=4] {'mem'}, dimensions={0} | all-to-all | bytes 262144 | tf_op jit(solution)/shard_map/all_to_all | solution.py:605
  92.0 0.6 screen_stats.1.own_ref
  92.7 2.5 %collective-permute-start.4 = (f32[72,128]{1,0:T(8,128)S(1)}, f32[72,128]{1,0:T(8,128)S(1)}, u32[]{:S(2)}, u32[]{:S(2)}) collective-permute-start(f32[72,128]{1,0:T(8,128)S(1)} %screen_stats.1.own_ref), channel_id=1, source_target_pairs={{0,4},{4,0},{8,12},{12,8},{16,20},{20,16},{24,28},{28,24},{32,36},... | collective-permute-start | bytes 110600 | tf_op jit(solution)/shard_map/ppermute | solution.py:52
  95.2 1.4 collective-permute-start.5
  96.6 4.8 %collective-permute-start.6 = (f32[72,128]{1,0:T(8,128)S(1)}, f32[72,128]{1,0:T(8,128)S(1)}, u32[]{:S(2)}, u32[]{:S(2)}) collective-permute-start(f32[72,128]{1,0:T(8,128)S(1)} %screen_stats.1.own_ref), channel_id=1, source_target_pairs={{0,32},{4,36},{8,40},{12,44},{16,48},{20,52},{24,56},{28,60},{32,0... | collective-permute-start | bytes 110600 | tf_op jit(solution)/shard_map/ppermute | solution.py:52
  101.4 4.9 %collective-permute-start.7 = (f32[72,128]{1,0:T(8,128)S(1)}, f32[72,128]{1,0:T(8,128)S(1)}, u32[]{:S(2)}, u32[]{:S(2)}) collective-permute-start(f32[72,128]{1,0:T(8,128)S(1)} %screen_stats.1.own_ref), channel_id=1, source_target_pairs={{0,224},{4,228},{8,232},{12,236},{16,240},{20,244},{24,248},{28,25... | collective-permute-start | bytes 110600 | tf_op jit(solution)/shard_map/ppermute | solution.py:52
  106.3 0.1 pad_add_fusion.id_ref
  106.4 0.1 collective-permute-start.9
  106.5 3.8 %collective-permute-done.7.refs_3_ = f32[72,128]{1,0:T(8,128)S(1)} collective-permute-done((f32[72,128]{1,0:T(8,128)S(1)}, f32[72,128]{1,0:T(8,128)S(1)}, u32[]{:S(2)}, u32[]{:S(2)}) %collective-permute-start.7) | collective-permute-done | bytes 36896 | tf_op jit(solution)/shard_map/ppermute | solution.py:52
  110.3 0.0 collective-permute-start.14
  110.3 6.7 %settle.1 = (bf16[32,128]{1,0:T(8,128)(2,1)S(1)}, bf16[64,32,128]{2,1,0:T(8,128)(2,1)}) custom-call(s32[1,4]{1,0:T(1,128)S(1)} %copy-done.4, s32[2]{0:T(128)S(1)} %pad_add_fusion.id_ref, f32[72,128]{1,0:T(8,128)S(1)} %screen_stats.1.own_ref, f32[72,128]{1,0:T(8,128)S(1)} %collective-permute-done.4.refs_0_, f32[72,128]{1,0:T(8,128)S(1)} %collective-permute-done.5.refs_1_, ...), custom_call_target="tpu_custom_call" | custom-call | tf_op jit(solution)/shard_map/settle/pallas_call | solution.py:519
  117.0 9.6 %all-to-all-start.2 = ((bf16[64,32,128]{2,1,0:T(8,128)(2,1)}), bf16[64,32,128]{2,1,0:T(8,128)(2,1)S(1)}, u32[]{:S(2)}, u32[]{:S(2)}) async-start(bf16[64,32,128]{2,1,0:T(8,128)(2,1)} %get-tuple-element.29), calls=%async_computation.2 | async-start | bytes 1048576 | tf_op jit(solution)/shard_map/all_to_all | solution.py:620
  126.6 0.8 fusion.6
  127.5 0.8 collective-permute-start.13
  128.3 0.9 collective-permute-start.16
  129.2 1.4 collective-permute-start.17
  130.6 1.8 convolution_add_fusion.1
  132.4 0.4 collective-permute-start.12
  132.8 4.2 %collective-permute-done.16.refs_13_ = bf16[512,256]{1,0:T(8,128)(2,1)} collective-permute-done((bf16[512,256]{1,0:T(8,128)(2,1)}, bf16[512,256]{1,0:T(8,128)(2,1)}, u32[]{:S(2)}, u32[]{:S(2)}) %collective-permute-start.16) | collective-permute-done | bytes 262176 | tf_op jit(solution)/shard_map/ppermute | solution.py:39
  136.9 0.5 collective-permute-start.15
  137.4 1.2 collective-permute-start.18
  138.6 1.8 fusion.2
  140.4 1.8 fusion.1
  142.3 1.1 copy.22
  143.4 21.6 %collective-permute-done.12.refs_7_ = bf16[1024,256]{1,0:T(8,128)(2,1)S(1)} collective-permute-done((bf16[1024,256]{1,0:T(8,128)(2,1)}, bf16[1024,256]{1,0:T(8,128)(2,1)S(1)}, u32[]{:S(2)}, u32[]{:S(2)}) %collective-permute-start.12) | collective-permute-done | bytes 524320 | tf_op jit(solution)/shard_map/ppermute | solution.py:39
  164.9 0.8 copy-done.12
  165.7 0.2 copy-done.13
  165.9 3.9 %collective-permute-done.18.refs_15_ = bf16[1024,256]{1,0:T(8,128)(2,1)} collective-permute-done((bf16[1024,256]{1,0:T(8,128)(2,1)}, bf16[1024,256]{1,0:T(8,128)(2,1)}, u32[]{:S(2)}, u32[]{:S(2)}) %collective-permute-start.18) | collective-permute-done | bytes 524320 | tf_op jit(solution)/shard_map/ppermute | solution.py:39
  169.8 0.8 copy-done.5
  170.6 22.1 %mix_land.1 = bf16[256,4096]{1,0:T(8,128)(2,1)} custom-call(s32[2]{0:T(128)} %copy-done.3, s32[64,8]{1,0:T(8,128)} %get-tuple-element.22.start_ref, bf16[1024,256]{1,0:T(8,128)(2,1)} %sort_land.3.refs_0_, bf16[512,256]{1,0:T(8,128)(2,1)} %sort_land.4.refs_1_, bf16[1536,256]{1,0:T(8,128)(2,1)} %get-tuple-element.23.refs_2_, ...), custom_call_target="tpu_custom_call" | custom-call | tf_op jit(solution)/shard_map/mix_land/pallas_call | solution.py:399
  (46 shorter events, 0.1 us)
Async XLA Ops:
  10.7 33.2 %all-to-all-start = ((bf16[64,34,128]{2,1,0:T(8,128)(2,1)}), bf16[64,34,128]{2,1,0:T(8,128)(2,1)S(1)}, u32[]{:S(2)}, u32[]{:S(2)}) async-start(bf16[64,34,128]{2,1,0:T(8,128)(2,1)} %bucket_tiles.1), calls=%async_computation | async-start | bytes 1310720 | tf_op jit(solution)/shard_map/all_to_all | solution.py:587
  27.2 13.4 %copy-start.16 = (s32[512]{0:T(512)S(1)}, s32[512]{0:T(512)}, u32[]{:S(2)}) copy-start(s32[512]{0:T(512)} %param.17) | copy-start | bytes 6148
  27.2 16.8 %copy-start = (bf16[32,8,1024]{2,1,0:T(8,128)(2,1)S(1)}, bf16[32,8,1024]{2,1,0:T(8,128)(2,1)}, u32[]{:S(2)}) copy-start(bf16[32,8,1024]{2,1,0:T(8,128)(2,1)} %param.10) | copy-start | bytes 1572868
  27.2 20.1 %collective-permute-start = (bf16[1024,256]{1,0:T(8,128)(2,1)}, bf16[1024,256]{1,0:T(8,128)(2,1)S(1)}, u32[]{:S(2)}, u32[]{:S(2)}) collective-permute-start(bf16[1024,256]{1,0:T(8,128)(2,1)} %sort_land.3.refs_0_), channel_id=1, source_target_pairs={{0,1},{1,2},{2,3},{3,0},{4,5},{5,6},{6,7},{7,4},{8,9},{9,10},{10,1... | collective-permute-start | bytes 1572872 | tf_op jit(solution)/shard_map/ppermute | solution.py:39
  28.4 18.9 %collective-permute-start.1 = (bf16[1024,256]{1,0:T(8,128)(2,1)}, bf16[1024,256]{1,0:T(8,128)(2,1)S(1)}, u32[]{:S(2)}, u32[]{:S(2)}) collective-permute-start(bf16[1024,256]{1,0:T(8,128)(2,1)} %sort_land.3.refs_0_), channel_id=1, source_target_pairs={{0,3},{1,0},{2,1},{3,2},{4,7},{5,4},{6,5},{7,6},{8,11},{9,8},{10,9... | collective-permute-start | bytes 1572872 | tf_op jit(solution)/shard_map/ppermute | solution.py:39
  32.3 59.7 %copy-start.1 = (f32[512]{0:T(512)S(1)}, f32[512]{0:T(512)}, u32[]{:S(2)}) copy-start(f32[512]{0:T(512)} %param.16) | copy-start | bytes 6148
  32.3 59.7 %copy-start.2 = (f32[512]{0:T(512)S(1)}, f32[512]{0:T(512)}, u32[]{:S(2)}) copy-start(f32[512]{0:T(512)} %param.18) | copy-start | bytes 6148
  32.3 78.0 %copy-start.4 = (s32[1,4]{1,0:T(1,128)S(1)}, s32[1,4]{1,0:T(1,128)}, u32[]{:S(2)}) copy-start(s32[1,4]{1,0:T(1,128)} %list_ref.1) | copy-start | bytes 52
  32.3 14.9 %collective-permute-start.2 = (bf16[512,256]{1,0:T(8,128)(2,1)}, bf16[512,256]{1,0:T(8,128)(2,1)S(1)}, u32[]{:S(2)}, u32[]{:S(2)}) collective-permute-start(bf16[512,256]{1,0:T(8,128)(2,1)} %sort_land.4.refs_1_), channel_id=1, source_target_pairs={{0,1},{1,2},{2,3},{3,0},{4,5},{5,6},{6,7},{7,4},{8,9},{9,10},{10,1... | collective-permute-start | bytes 786440 | tf_op jit(solution)/shard_map/ppermute | solution.py:39
  32.3 14.9 %collective-permute-start.3 = (bf16[512,256]{1,0:T(8,128)(2,1)}, bf16[512,256]{1,0:T(8,128)(2,1)S(1)}, u32[]{:S(2)}, u32[]{:S(2)}) collective-permute-start(bf16[512,256]{1,0:T(8,128)(2,1)} %sort_land.4.refs_1_), channel_id=1, source_target_pairs={{0,3},{1,0},{2,1},{3,2},{4,7},{5,4},{6,5},{7,6},{8,11},{9,8},{10,9... | collective-permute-start | bytes 786440 | tf_op jit(solution)/shard_map/ppermute | solution.py:39
  46.9 80.5 %copy-start.6 = (bf16[1536,256]{1,0:T(8,128)(2,1)S(1)}, bf16[1536,256]{1,0:T(8,128)(2,1)}, u32[]{:S(2)}) copy-start(bf16[1536,256]{1,0:T(8,128)(2,1)} %get-tuple-element.23.refs_2_) | copy-start | bytes 2359300
  47.2 80.2 %copy-start.14 = (bf16[512,256]{1,0:T(8,128)(2,1)}, bf16[512,256]{1,0:T(8,128)(2,1)S(1)}, u32[]{:S(2)}) copy-start(bf16[512,256]{1,0:T(8,128)(2,1)S(1)} %collective-permute-done.2.refs_5_) | copy-start | bytes 786436
  47.3 80.2 %copy-start.15 = (bf16[512,256]{1,0:T(8,128)(2,1)}, bf16[512,256]{1,0:T(8,128)(2,1)S(1)}, u32[]{:S(2)}) copy-start(bf16[512,256]{1,0:T(8,128)(2,1)S(1)} %collective-permute-done.3.refs_9_) | copy-start | bytes 786436
  47.3 0.8 copy-start.9
  47.3 1.0 copy-start.10
  48.3 80.9 %collective-permute-start.11 = (bf16[1536,256]{1,0:T(8,128)(2,1)}, bf16[1536,256]{1,0:T(8,128)(2,1)S(1)}, u32[]{:S(2)}, u32[]{:S(2)}) collective-permute-start(bf16[1536,256]{1,0:T(8,128)(2,1)} %get-tuple-element.23.refs_2_), channel_id=1, source_target_pairs={{0,1},{1,2},{2,3},{3,0},{4,5},{5,6},{6,7},{7,4},{8,9},{9,10},{10,1... | collective-permute-start | bytes 2359304 | tf_op jit(solution)/shard_map/ppermute | solution.py:39
  49.2 78.2 %collective-permute-start.8 = (bf16[256,1024]{1,0:T(8,128)(2,1)S(1)}, bf16[256,1024]{1,0:T(8,128)(2,1)}, u32[]{:S(2)}, u32[]{:S(2)}) collective-permute-start(bf16[256,1024]{1,0:T(8,128)(2,1)S(1)} %bitcast.30), channel_id=1, source_target_pairs={{0,1},{1,2},{2,3},{3,0},{4,5},{5,6},{6,7},{7,4},{8,9},{9,10},{10,1... | collective-permute-start | bytes 1572872 | tf_op jit(solution)/shard_map/ppermute | solution.py:39
  50.4 77.9 %collective-permute-start.10 = (bf16[256,1024]{1,0:T(8,128)(2,1)S(1)}, bf16[256,1024]{1,0:T(8,128)(2,1)}, u32[]{:S(2)}, u32[]{:S(2)}) collective-permute-start(bf16[256,1024]{1,0:T(8,128)(2,1)S(1)} %bitcast.31), channel_id=1, source_target_pairs={{0,2},{1,3},{2,0},{3,1},{4,6},{5,7},{6,4},{7,5},{8,10},{9,11},{10,... | collective-permute-start | bytes 1572872 | tf_op jit(solution)/shard_map/ppermute | solution.py:39
  92.7 3.9 %collective-permute-start.4 = (f32[72,128]{1,0:T(8,128)S(1)}, f32[72,128]{1,0:T(8,128)S(1)}, u32[]{:S(2)}, u32[]{:S(2)}) collective-permute-start(f32[72,128]{1,0:T(8,128)S(1)} %screen_stats.1.own_ref), channel_id=1, source_target_pairs={{0,4},{4,0},{8,12},{12,8},{16,20},{20,16},{24,28},{28,24},{32,36},... | collective-permute-start | bytes 110600 | tf_op jit(solution)/shard_map/ppermute | solution.py:52
  95.2 6.2 %collective-permute-start.5 = (f32[72,128]{1,0:T(8,128)S(1)}, f32[72,128]{1,0:T(8,128)S(1)}, u32[]{:S(2)}, u32[]{:S(2)}) collective-permute-start(f32[72,128]{1,0:T(8,128)S(1)} %screen_stats.1.own_ref), channel_id=1, source_target_pairs={{0,252},{4,8},{8,4},{12,16},{16,12},{20,24},{24,20},{28,32},{32,28... | collective-permute-start | bytes 110600 | tf_op jit(solution)/shard_map/ppermute | solution.py:52
  96.6 9.8 %collective-permute-start.6 = (f32[72,128]{1,0:T(8,128)S(1)}, f32[72,128]{1,0:T(8,128)S(1)}, u32[]{:S(2)}, u32[]{:S(2)}) collective-permute-start(f32[72,128]{1,0:T(8,128)S(1)} %screen_stats.1.own_ref), channel_id=1, source_target_pairs={{0,32},{4,36},{8,40},{12,44},{16,48},{20,52},{24,56},{28,60},{32,0... | collective-permute-start | bytes 110600 | tf_op jit(solution)/shard_map/ppermute | solution.py:52
  101.4 8.9 %collective-permute-start.7 = (f32[72,128]{1,0:T(8,128)S(1)}, f32[72,128]{1,0:T(8,128)S(1)}, u32[]{:S(2)}, u32[]{:S(2)}) collective-permute-start(f32[72,128]{1,0:T(8,128)S(1)} %screen_stats.1.own_ref), channel_id=1, source_target_pairs={{0,224},{4,228},{8,232},{12,236},{16,240},{20,244},{24,248},{28,25... | collective-permute-start | bytes 110600 | tf_op jit(solution)/shard_map/ppermute | solution.py:52
  106.4 26.0 %copy-start.3 = (s32[2]{0:T(128)}, s32[2]{0:T(128)S(1)}, u32[]{:S(2)}) copy-start(s32[2]{0:T(128)S(1)} %pad_add_fusion.id_ref) | copy-start | bytes 28
  106.4 26.0 %collective-permute-start.9 = (bf16[256,1024]{1,0:T(8,128)(2,1)S(1)}, bf16[256,1024]{1,0:T(8,128)(2,1)}, u32[]{:S(2)}, u32[]{:S(2)}) collective-permute-start(bf16[256,1024]{1,0:T(8,128)(2,1)S(1)} %bitcast.32), channel_id=1, source_target_pairs={{0,3},{1,0},{2,1},{3,2},{4,7},{5,4},{6,5},{7,6},{8,11},{9,8},{10,9... | collective-permute-start | bytes 1572872 | tf_op jit(solution)/shard_map/ppermute | solution.py:39
  110.3 27.1 %collective-permute-start.14 = (bf16[1024,256]{1,0:T(8,128)(2,1)}, bf16[1024,256]{1,0:T(8,128)(2,1)}, u32[]{:S(2)}, u32[]{:S(2)}) collective-permute-start(bf16[1024,256]{1,0:T(8,128)(2,1)} %get-tuple-element.24.refs_3_), channel_id=1, source_target_pairs={{0,3},{1,0},{2,1},{3,2},{4,7},{5,4},{6,5},{7,6},{8,11},{9,8},{10,9... | collective-permute-start | bytes 1572872 | tf_op jit(solution)/shard_map/ppermute | solution.py:39
  117.0 52.8 %all-to-all-start.2 = ((bf16[64,32,128]{2,1,0:T(8,128)(2,1)}), bf16[64,32,128]{2,1,0:T(8,128)(2,1)S(1)}, u32[]{:S(2)}, u32[]{:S(2)}) async-start(bf16[64,32,128]{2,1,0:T(8,128)(2,1)} %get-tuple-element.29), calls=%async_computation.2 | async-start | bytes 1048576 | tf_op jit(solution)/shard_map/all_to_all | solution.py:620
  126.6 10.3 %copy-start.11 = (bf16[1024,256]{1,0:T(8,128)(2,1)S(1)}, bf16[1024,256]{1,0:T(8,128)(2,1)}, u32[]{:S(2)}) copy-start(bf16[1024,256]{1,0:T(8,128)(2,1)} %copy-done.10) | copy-start | bytes 1572868
  127.5 37.5 %collective-permute-start.13 = (bf16[1536,256]{1,0:T(8,128)(2,1)S(1)}, bf16[1536,256]{1,0:T(8,128)(2,1)S(1)}, u32[]{:S(2)}, u32[]{:S(2)}) collective-permute-start(bf16[1536,256]{1,0:T(8,128)(2,1)S(1)} %copy-done.6), channel_id=1, source_target_pairs={{0,3},{1,0},{2,1},{3,2},{4,7},{5,4},{6,5},{7,6},{8,11},{9,8},{10,9... | collective-permute-start | bytes 2359304 | tf_op jit(solution)/shard_map/ppermute | solution.py:39
  128.3 8.7 %collective-permute-start.16 = (bf16[512,256]{1,0:T(8,128)(2,1)}, bf16[512,256]{1,0:T(8,128)(2,1)}, u32[]{:S(2)}, u32[]{:S(2)}) collective-permute-start(bf16[512,256]{1,0:T(8,128)(2,1)} %copy-done.14), channel_id=1, source_target_pairs={{0,1},{1,2},{2,3},{3,0},{4,5},{5,6},{6,7},{7,4},{8,9},{9,10},{10,1... | collective-permute-start | bytes 786440 | tf_op jit(solution)/shard_map/ppermute | solution.py:39
  129.2 11.2 %copy-start.7 = (bf16[1536,256]{1,0:T(8,128)(2,1)}, bf16[1536,256]{1,0:T(8,128)(2,1)S(1)}, u32[]{:S(2)}) copy-start(bf16[1536,256]{1,0:T(8,128)(2,1)S(1)} %collective-permute-done.11.refs_6_) | copy-start | bytes 2359300
  129.2 40.6 %collective-permute-start.17 = (bf16[1536,256]{1,0:T(8,128)(2,1)S(1)}, bf16[1536,256]{1,0:T(8,128)(2,1)}, u32[]{:S(2)}, u32[]{:S(2)}) collective-permute-start(bf16[1536,256]{1,0:T(8,128)(2,1)S(1)} %collective-permute-done.11.refs_6_), channel_id=1, source_target_pairs={{0,1},{1,2},{2,3},{3,0},{4,5},{5,6},{6,7},{7,4},{8,9},{9,10},{10,1... | collective-permute-start | bytes 2359304 | tf_op jit(solution)/shard_map/ppermute | solution.py:39
  132.4 32.5 %collective-permute-start.12 = (bf16[1024,256]{1,0:T(8,128)(2,1)}, bf16[1024,256]{1,0:T(8,128)(2,1)S(1)}, u32[]{:S(2)}, u32[]{:S(2)}) collective-permute-start(bf16[1024,256]{1,0:T(8,128)(2,1)} %get-tuple-element.24.refs_3_), channel_id=1, source_target_pairs={{0,1},{1,2},{2,3},{3,0},{4,5},{5,6},{6,7},{7,4},{8,9},{9,10},{10,1... | collective-permute-start | bytes 1572872 | tf_op jit(solution)/shard_map/ppermute | solution.py:39
  136.9 28.0 %collective-permute-start.15 = (bf16[1024,256]{1,0:T(8,128)(2,1)S(1)}, bf16[1024,256]{1,0:T(8,128)(2,1)S(1)}, u32[]{:S(2)}, u32[]{:S(2)}) collective-permute-start(bf16[1024,256]{1,0:T(8,128)(2,1)S(1)} %copy-done.11), channel_id=1, source_target_pairs={{0,3},{1,0},{2,1},{3,2},{4,7},{5,4},{6,5},{7,6},{8,11},{9,8},{10,9... | collective-permute-start | bytes 1572872 | tf_op jit(solution)/shard_map/ppermute | solution.py:39
  137.4 32.3 %collective-permute-start.18 = (bf16[1024,256]{1,0:T(8,128)(2,1)}, bf16[1024,256]{1,0:T(8,128)(2,1)}, u32[]{:S(2)}, u32[]{:S(2)}) collective-permute-start(bf16[1024,256]{1,0:T(8,128)(2,1)} %collective-permute-done.14.refs_11_), channel_id=1, source_target_pairs={{0,3},{1,0},{2,1},{3,2},{4,7},{5,4},{6,5},{7,6},{8,11},{9,8},{10,9... | collective-permute-start | bytes 1572872 | tf_op jit(solution)/shard_map/ppermute | solution.py:39
  164.9 0.8 copy-start.12
  164.9 1.0 copy-start.13
  165.9 3.9 %copy-start.8 = (bf16[1536,256]{1,0:T(8,128)(2,1)}, bf16[1536,256]{1,0:T(8,128)(2,1)S(1)}, u32[]{:S(2)}) copy-start(bf16[1536,256]{1,0:T(8,128)(2,1)S(1)} %collective-permute-done.13.refs_10_) | copy-start | bytes 2359300
  169.8 0.9 copy-start.5

commit v8 on v7

--- a/solution.py
+++ b/solution.py
@@ -624,7 +624,10 @@
     for part, source in zip([atmos_rows] + atmos_parts, slot_source):
         rows = lax.dynamic_slice_in_dim(own_cols, (source % mem_count) * local, local, 1)
         atmos_out = atmos_out + jnp.einsum(
-            "jk,klc->jlc", rows, part.reshape(local, levels, columns), preferred_element_type=F32
+            "jk,klc->jlc",
+            rows,
+            part.reshape(local, levels, columns),
+            preferred_element_type=F32,
         )
     atmos_analysis = atmos_out.astype(BF)
 

time: 194 us -> 194 us (level)
  no operation moved by 1% of the time
where the time goes in v8:
time: 194 us; the launch traced here: 193 us
  Pallas kernels  53.9 us (28%)
  starting transfers between devices  50.8 us (26%)
  blocking collectives  39.9 us (21%)
  waiting for transfers between devices  36.9 us (19%)
  matrix products  6.25 us (3%)
  local copies, waits for them, and re-layouts  4.12 us (2%)
    all_to_all x1, blocking collectives, analysis(): lax.all_to_all(forecast, 'mem', split_axis=0, concat_axis=0, tiled=True)  39.9 us
    ppermute x15, waiting for transfers between devices, shifted(): return lax.ppermute(value, axis, pairs)  29.9 us
    pallas_call x1, Pallas kernels, mix_land(): pl.pallas_call(kernel, grid=(PARTS,), out_shape=jax.ShapeDtypeStruct((wid...  22.1 us
    ppermute x15, starting transfers between devices, shifted(): return lax.ppermute(value, axis, pairs)  14.4 us
    ppermute x4, starting transfers between devices, swapped(): return lax.ppermute(value, 'patch', pairs)  13.6 us
    all_to_all x1, starting transfers between devices, analysis(): lax.all_to_all(packed, 'patch', split_axis=0, concat_axis=0, tiled=True)  13.1 us
    pallas_call x3, Pallas kernels, sort_land(): pl.pallas_call(kernel, grid=(1,), out_shape=[jax.ShapeDtypeStruct((size,...  11.4 us
    all_to_all x1, starting transfers between devices, analysis(): lax.all_to_all(mixes, 'patch', split_axis=0, concat_axis=0, tiled=True)  9.63 us
  transfers between devices with their start and end apart: 21, of which 6 were waited for; matrix products, arithmetic and copies ran while one was open for 4% of the time, Pallas kernels for 11%

profile of v8, /device:TPU:1, one launch (start us, length us, event | category | flops | bytes accessed | tf_op | source)
XLA Modules:
  0.0 193.0 jit_solution(13610577262333980765)
XLA Ops:
  0.6 2.3 %order_tiles.1 = (s32[1,4096]{1,0:T(1,128)}, s32[1,4096]{1,0:T(1,128)}, s32[64,8]{1,0:T(8,128)}) custom-call(s32[1,4096]{1,0:T(1,128)} %bitcast.44), custom_call_target="tpu_custom_call" | custom-call | tf_op jit(solution)/shard_map/order_tiles/pallas_call | solution.py:84
  2.9 7.7 %bucket_tiles.1 = bf16[64,34,128]{2,1,0:T(8,128)(2,1)} custom-call(bf16[256,4096]{1,0:T(8,128)(2,1)} %bitcast.35, bf16[32,128]{1,0:T(8,128)(2,1)} %bitcast.47, s32[32,128]{1,0:T(8,128)} %bitcast.42, s32[1,4096]{1,0:T(1,128)} %bitcast.45, s32[1,4096]{1,0:T(1,128)} %get-tuple-element.16.rank_ref, s32[1,4096]{1,0:T(1,128)} %bitcast.46), custom_call_target="tpu_custom_call" | custom-call | tf_op jit(solution)/shard_map/bucket_tiles/pallas_call | solution.py:163
  10.7 13.1 %all-to-all-start = ((bf16[64,34,128]{2,1,0:T(8,128)(2,1)}), bf16[64,34,128]{2,1,0:T(8,128)(2,1)S(1)}, u32[]{:S(2)}, u32[]{:S(2)}) async-start(bf16[64,34,128]{2,1,0:T(8,128)(2,1)} %bucket_tiles.1), calls=%async_computation | async-start | bytes 1310720 | tf_op jit(solution)/shard_map/all_to_all | solution.py:587
  23.8 3.3 %sort_land.3.refs_0_ = bf16[1024,256]{1,0:T(8,128)(2,1)} custom-call(s32[1,4096]{1,0:T(1,128)} %get-tuple-element.17.pos_ref.refs_17_, bf16[256,4096]{1,0:T(8,128)(2,1)} %bitcast.36), custom_call_target="tpu_custom_call" | custom-call | tf_op jit(solution)/shard_map/sort_land/pallas_call | solution.py:206
  27.2 1.2 collective-permute-start
  28.4 1.5 collective-permute-start.1
  29.9 2.5 %sort_land.4.refs_1_ = bf16[512,256]{1,0:T(8,128)(2,1)} custom-call(s32[1,4096]{1,0:T(1,128)} %get-tuple-element.17.pos_ref.refs_17_, bf16[256,4096]{1,0:T(8,128)(2,1)} %bitcast.37), custom_call_target="tpu_custom_call" | custom-call | tf_op jit(solution)/shard_map/sort_land/pallas_call | solution.py:206
  32.3 2.7 %collective-permute-start.3 = (bf16[512,256]{1,0:T(8,128)(2,1)}, bf16[512,256]{1,0:T(8,128)(2,1)S(1)}, u32[]{:S(2)}, u32[]{:S(2)}) collective-permute-start(bf16[512,256]{1,0:T(8,128)(2,1)} %sort_land.4.refs_1_), channel_id=1, source_target_pairs={{0,3},{1,0},{2,1},{3,2},{4,7},{5,4},{6,5},{7,6},{8,11},{9,8},{10,9... | collective-permute-start | bytes 786440 | tf_op jit(solution)/shard_map/ppermute | solution.py:39
  35.0 5.6 %sort_land.5 = (bf16[1536,256]{1,0:T(8,128)(2,1)}, bf16[1024,256]{1,0:T(8,128)(2,1)}) custom-call(s32[1,4096]{1,0:T(1,128)} %get-tuple-element.17.pos_ref.refs_17_, bf16[256,4096]{1,0:T(8,128)(2,1)} %bitcast.38), custom_call_target="tpu_custom_call" | custom-call | tf_op jit(solution)/shard_map/sort_land/pallas_call | solution.py:206
  40.6 0.1 copy.17.obs_ref
  40.8 3.2 %all-to-all-done.in_ref = bf16[64,34,128]{2,1,0:T(8,128)(2,1)S(1)} async-done(((bf16[64,34,128]{2,1,0:T(8,128)(2,1)}), bf16[64,34,128]{2,1,0:T(8,128)(2,1)S(1)}, u32[]{:S(2)}, u32[]{:S(2)}) %all-to-all-start) | async-done | bytes 557088 | tf_op jit(solution)/shard_map/all_to_all | solution.py:587
  43.9 3.0 %screen_forecast.1 = bf16[4,32,512]{2,1,0:T(8,128)(2,1)S(1)} custom-call(bf16[64,34,128]{2,1,0:T(8,128)(2,1)S(1)} %all-to-all-done.in_ref, bf16[256,1024]{1,0:T(8,128)(2,1)S(1)} %bitcast.29, s32[512,1]{1,0:T(8,128)S(1)} %copy.17.obs_ref), custom_call_target="tpu_custom_call" | custom-call | tf_op jit(solution)/shard_map/screen_forecast/pallas_call | solution.py:246
  46.9 0.3 collective-permute-done.2.refs_5_
  47.3 0.8 copy-done.9
  48.1 0.2 copy-done.10
  48.3 0.9 collective-permute-start.11
  49.2 1.2 collective-permute-start.8
  50.4 1.8 collective-permute-start.10
  52.2 39.9 %all_to_all.15.in_ref = bf16[4,32,512]{2,1,0:T(8,128)(2,1)S(1)} all-to-all(bf16[4,32,512]{2,1,0:T(8,128)(2,1)S(1)} %screen_forecast.1), channel_id=1, replica_groups=mesh['patch'=64,'mem'=4] {'mem'}, dimensions={0} | all-to-all | bytes 262144 | tf_op jit(solution)/shard_map/all_to_all | solution.py:605
  92.0 0.6 screen_stats.1.own_ref
  92.7 2.5 %collective-permute-start.4 = (f32[72,128]{1,0:T(8,128)S(1)}, f32[72,128]{1,0:T(8,128)S(1)}, u32[]{:S(2)}, u32[]{:S(2)}) collective-permute-start(f32[72,128]{1,0:T(8,128)S(1)} %screen_stats.1.own_ref), channel_id=1, source_target_pairs={{0,4},{4,0},{8,12},{12,8},{16,20},{20,16},{24,28},{28,24},{32,36},... | collective-permute-start | bytes 110600 | tf_op jit(solution)/shard_map/ppermute | solution.py:52
  95.2 1.4 collective-permute-start.5
  96.6 4.8 %collective-permute-start.6 = (f32[72,128]{1,0:T(8,128)S(1)}, f32[72,128]{1,0:T(8,128)S(1)}, u32[]{:S(2)}, u32[]{:S(2)}) collective-permute-start(f32[72,128]{1,0:T(8,128)S(1)} %screen_stats.1.own_ref), channel_id=1, source_target_pairs={{0,32},{4,36},{8,40},{12,44},{16,48},{20,52},{24,56},{28,60},{32,0... | collective-permute-start | bytes 110600 | tf_op jit(solution)/shard_map/ppermute | solution.py:52
  101.4 4.9 %collective-permute-start.7 = (f32[72,128]{1,0:T(8,128)S(1)}, f32[72,128]{1,0:T(8,128)S(1)}, u32[]{:S(2)}, u32[]{:S(2)}) collective-permute-start(f32[72,128]{1,0:T(8,128)S(1)} %screen_stats.1.own_ref), channel_id=1, source_target_pairs={{0,224},{4,228},{8,232},{12,236},{16,240},{20,244},{24,248},{28,25... | collective-permute-start | bytes 110600 | tf_op jit(solution)/shard_map/ppermute | solution.py:52
  106.3 0.1 pad_add_fusion.id_ref
  106.4 0.1 collective-permute-start.9
  106.5 3.8 %collective-permute-done.7.refs_3_ = f32[72,128]{1,0:T(8,128)S(1)} collective-permute-done((f32[72,128]{1,0:T(8,128)S(1)}, f32[72,128]{1,0:T(8,128)S(1)}, u32[]{:S(2)}, u32[]{:S(2)}) %collective-permute-start.7) | collective-permute-done | bytes 36896 | tf_op jit(solution)/shard_map/ppermute | solution.py:52
  110.3 0.0 collective-permute-start.14
  110.3 6.7 %settle.1 = (bf16[32,128]{1,0:T(8,128)(2,1)S(1)}, bf16[64,32,128]{2,1,0:T(8,128)(2,1)}) custom-call(s32[1,4]{1,0:T(1,128)S(1)} %copy-done.4, s32[2]{0:T(128)S(1)} %pad_add_fusion.id_ref, f32[72,128]{1,0:T(8,128)S(1)} %screen_stats.1.own_ref, f32[72,128]{1,0:T(8,128)S(1)} %collective-permute-done.4.refs_0_, f32[72,128]{1,0:T(8,128)S(1)} %collective-permute-done.5.refs_1_, ...), custom_call_target="tpu_custom_call" | custom-call | tf_op jit(solution)/shard_map/settle/pallas_call | solution.py:519
  117.0 9.6 %all-to-all-start.2 = ((bf16[64,32,128]{2,1,0:T(8,128)(2,1)}), bf16[64,32,128]{2,1,0:T(8,128)(2,1)S(1)}, u32[]{:S(2)}, u32[]{:S(2)}) async-start(bf16[64,32,128]{2,1,0:T(8,128)(2,1)} %get-tuple-element.29), calls=%async_computation.2 | async-start | bytes 1048576 | tf_op jit(solution)/shard_map/all_to_all | solution.py:620
  126.6 0.8 fusion.6
  127.5 0.8 collective-permute-start.13
  128.3 0.9 collective-permute-start.16
  129.2 1.4 collective-permute-start.17
  130.6 1.8 convolution_add_fusion.1
  132.4 0.4 collective-permute-start.12
  132.8 4.2 %collective-permute-done.16.refs_13_ = bf16[512,256]{1,0:T(8,128)(2,1)} collective-permute-done((bf16[512,256]{1,0:T(8,128)(2,1)}, bf16[512,256]{1,0:T(8,128)(2,1)}, u32[]{:S(2)}, u32[]{:S(2)}) %collective-permute-start.16) | collective-permute-done | bytes 262176 | tf_op jit(solution)/shard_map/ppermute | solution.py:39
  136.9 0.5 collective-permute-start.15
  137.4 1.2 collective-permute-start.18
  138.6 1.8 fusion.2
  140.4 1.8 fusion.1
  142.3 1.1 copy.22
  143.4 21.6 %collective-permute-done.12.refs_7_ = bf16[1024,256]{1,0:T(8,128)(2,1)S(1)} collective-permute-done((bf16[1024,256]{1,0:T(8,128)(2,1)}, bf16[1024,256]{1,0:T(8,128)(2,1)S(1)}, u32[]{:S(2)}, u32[]{:S(2)}) %collective-permute-start.12) | collective-permute-done | bytes 524320 | tf_op jit(solution)/shard_map/ppermute | solution.py:39
  164.9 0.8 copy-done.12
  165.7 0.2 copy-done.13
  165.9 3.9 %collective-permute-done.18.refs_15_ = bf16[1024,256]{1,0:T(8,128)(2,1)} collective-permute-done((bf16[1024,256]{1,0:T(8,128)(2,1)}, bf16[1024,256]{1,0:T(8,128)(2,1)}, u32[]{:S(2)}, u32[]{:S(2)}) %collective-permute-start.18) | collective-permute-done | bytes 524320 | tf_op jit(solution)/shard_map/ppermute | solution.py:39
  169.8 0.8 copy-done.5
  170.6 22.1 %mix_land.1 = bf16[256,4096]{1,0:T(8,128)(2,1)} custom-call(s32[2]{0:T(128)} %copy-done.3, s32[64,8]{1,0:T(8,128)} %get-tuple-element.22.start_ref, bf16[1024,256]{1,0:T(8,128)(2,1)} %sort_land.3.refs_0_, bf16[512,256]{1,0:T(8,128)(2,1)} %sort_land.4.refs_1_, bf16[1536,256]{1,0:T(8,128)(2,1)} %get-tuple-element.23.refs_2_, ...), custom_call_target="tpu_custom_call" | custom-call | tf_op jit(solution)/shard_map/mix_land/pallas_call | solution.py:399
  (46 shorter events, 0.1 us)
Async XLA Ops:
  10.7 33.2 %all-to-all-start = ((bf16[64,34,128]{2,1,0:T(8,128)(2,1)}), bf16[64,34,128]{2,1,0:T(8,128)(2,1)S(1)}, u32[]{:S(2)}, u32[]{:S(2)}) async-start(bf16[64,34,128]{2,1,0:T(8,128)(2,1)} %bucket_tiles.1), calls=%async_computation | async-start | bytes 1310720 | tf_op jit(solution)/shard_map/all_to_all | solution.py:587
  27.2 13.4 %copy-start.16 = (s32[512]{0:T(512)S(1)}, s32[512]{0:T(512)}, u32[]{:S(2)}) copy-start(s32[512]{0:T(512)} %param.17) | copy-start | bytes 6148
  27.2 16.8 %copy-start = (bf16[32,8,1024]{2,1,0:T(8,128)(2,1)S(1)}, bf16[32,8,1024]{2,1,0:T(8,128)(2,1)}, u32[]{:S(2)}) copy-start(bf16[32,8,1024]{2,1,0:T(8,128)(2,1)} %param.10) | copy-start | bytes 1572868
  27.2 20.1 %collective-permute-start = (bf16[1024,256]{1,0:T(8,128)(2,1)}, bf16[1024,256]{1,0:T(8,128)(2,1)S(1)}, u32[]{:S(2)}, u32[]{:S(2)}) collective-permute-start(bf16[1024,256]{1,0:T(8,128)(2,1)} %sort_land.3.refs_0_), channel_id=1, source_target_pairs={{0,1},{1,2},{2,3},{3,0},{4,5},{5,6},{6,7},{7,4},{8,9},{9,10},{10,1... | collective-permute-start | bytes 1572872 | tf_op jit(solution)/shard_map/ppermute | solution.py:39
  28.4 18.9 %collective-permute-start.1 = (bf16[1024,256]{1,0:T(8,128)(2,1)}, bf16[1024,256]{1,0:T(8,128)(2,1)S(1)}, u32[]{:S(2)}, u32[]{:S(2)}) collective-permute-start(bf16[1024,256]{1,0:T(8,128)(2,1)} %sort_land.3.refs_0_), channel_id=1, source_target_pairs={{0,3},{1,0},{2,1},{3,2},{4,7},{5,4},{6,5},{7,6},{8,11},{9,8},{10,9... | collective-permute-start | bytes 1572872 | tf_op jit(solution)/shard_map/ppermute | solution.py:39
  32.3 59.7 %copy-start.1 = (f32[512]{0:T(512)S(1)}, f32[512]{0:T(512)}, u32[]{:S(2)}) copy-start(f32[512]{0:T(512)} %param.16) | copy-start | bytes 6148
  32.3 59.7 %copy-start.2 = (f32[512]{0:T(512)S(1)}, f32[512]{0:T(512)}, u32[]{:S(2)}) copy-start(f32[512]{0:T(512)} %param.18) | copy-start | bytes 6148
  32.3 78.0 %copy-start.4 = (s32[1,4]{1,0:T(1,128)S(1)}, s32[1,4]{1,0:T(1,128)}, u32[]{:S(2)}) copy-start(s32[1,4]{1,0:T(1,128)} %list_ref.1) | copy-start | bytes 52
  32.3 14.9 %collective-permute-start.2 = (bf16[512,256]{1,0:T(8,128)(2,1)}, bf16[512,256]{1,0:T(8,128)(2,1)S(1)}, u32[]{:S(2)}, u32[]{:S(2)}) collective-permute-start(bf16[512,256]{1,0:T(8,128)(2,1)} %sort_land.4.refs_1_), channel_id=1, source_target_pairs={{0,1},{1,2},{2,3},{3,0},{4,5},{5,6},{6,7},{7,4},{8,9},{9,10},{10,1... | collective-permute-start | bytes 786440 | tf_op jit(solution)/shard_map/ppermute | solution.py:39
  32.3 14.9 %collective-permute-start.3 = (bf16[512,256]{1,0:T(8,128)(2,1)}, bf16[512,256]{1,0:T(8,128)(2,1)S(1)}, u32[]{:S(2)}, u32[]{:S(2)}) collective-permute-start(bf16[512,256]{1,0:T(8,128)(2,1)} %sort_land.4.refs_1_), channel_id=1, source_target_pairs={{0,3},{1,0},{2,1},{3,2},{4,7},{5,4},{6,5},{7,6},{8,11},{9,8},{10,9... | collective-permute-start | bytes 786440 | tf_op jit(solution)/shard_map/ppermute | solution.py:39
  46.9 80.5 %copy-start.6 = (bf16[1536,256]{1,0:T(8,128)(2,1)S(1)}, bf16[1536,256]{1,0:T(8,128)(2,1)}, u32[]{:S(2)}) copy-start(bf16[1536,256]{1,0:T(8,128)(2,1)} %get-tuple-element.23.refs_2_) | copy-start | bytes 2359300
  47.2 80.2 %copy-start.14 = (bf16[512,256]{1,0:T(8,128)(2,1)}, bf16[512,256]{1,0:T(8,128)(2,1)S(1)}, u32[]{:S(2)}) copy-start(bf16[512,256]{1,0:T(8,128)(2,1)S(1)} %collective-permute-done.2.refs_5_) | copy-start | bytes 786436
  47.3 80.2 %copy-start.15 = (bf16[512,256]{1,0:T(8,128)(2,1)}, bf16[512,256]{1,0:T(8,128)(2,1)S(1)}, u32[]{:S(2)}) copy-start(bf16[512,256]{1,0:T(8,128)(2,1)S(1)} %collective-permute-done.3.refs_9_) | copy-start | bytes 786436
  47.3 0.8 copy-start.9
  47.3 1.0 copy-start.10
  48.3 80.9 %collective-permute-start.11 = (bf16[1536,256]{1,0:T(8,128)(2,1)}, bf16[1536,256]{1,0:T(8,128)(2,1)S(1)}, u32[]{:S(2)}, u32[]{:S(2)}) collective-permute-start(bf16[1536,256]{1,0:T(8,128)(2,1)} %get-tuple-element.23.refs_2_), channel_id=1, source_target_pairs={{0,1},{1,2},{2,3},{3,0},{4,5},{5,6},{6,7},{7,4},{8,9},{9,10},{10,1... | collective-permute-start | bytes 2359304 | tf_op jit(solution)/shard_map/ppermute | solution.py:39
  49.2 78.2 %collective-permute-start.8 = (bf16[256,1024]{1,0:T(8,128)(2,1)S(1)}, bf16[256,1024]{1,0:T(8,128)(2,1)}, u32[]{:S(2)}, u32[]{:S(2)}) collective-permute-start(bf16[256,1024]{1,0:T(8,128)(2,1)S(1)} %bitcast.30), channel_id=1, source_target_pairs={{0,1},{1,2},{2,3},{3,0},{4,5},{5,6},{6,7},{7,4},{8,9},{9,10},{10,1... | collective-permute-start | bytes 1572872 | tf_op jit(solution)/shard_map/ppermute | solution.py:39
  50.4 77.9 %collective-permute-start.10 = (bf16[256,1024]{1,0:T(8,128)(2,1)S(1)}, bf16[256,1024]{1,0:T(8,128)(2,1)}, u32[]{:S(2)}, u32[]{:S(2)}) collective-permute-start(bf16[256,1024]{1,0:T(8,128)(2,1)S(1)} %bitcast.31), channel_id=1, source_target_pairs={{0,2},{1,3},{2,0},{3,1},{4,6},{5,7},{6,4},{7,5},{8,10},{9,11},{10,... | collective-permute-start | bytes 1572872 | tf_op jit(solution)/shard_map/ppermute | solution.py:39
  92.7 3.9 %collective-permute-start.4 = (f32[72,128]{1,0:T(8,128)S(1)}, f32[72,128]{1,0:T(8,128)S(1)}, u32[]{:S(2)}, u32[]{:S(2)}) collective-permute-start(f32[72,128]{1,0:T(8,128)S(1)} %screen_stats.1.own_ref), channel_id=1, source_target_pairs={{0,4},{4,0},{8,12},{12,8},{16,20},{20,16},{24,28},{28,24},{32,36},... | collective-permute-start | bytes 110600 | tf_op jit(solution)/shard_map/ppermute | solution.py:52
  95.2 6.2 %collective-permute-start.5 = (f32[72,128]{1,0:T(8,128)S(1)}, f32[72,128]{1,0:T(8,128)S(1)}, u32[]{:S(2)}, u32[]{:S(2)}) collective-permute-start(f32[72,128]{1,0:T(8,128)S(1)} %screen_stats.1.own_ref), channel_id=1, source_target_pairs={{0,252},{4,8},{8,4},{12,16},{16,12},{20,24},{24,20},{28,32},{32,28... | collective-permute-start | bytes 110600 | tf_op jit(solution)/shard_map/ppermute | solution.py:52
  96.6 9.8 %collective-permute-start.6 = (f32[72,128]{1,0:T(8,128)S(1)}, f32[72,128]{1,0:T(8,128)S(1)}, u32[]{:S(2)}, u32[]{:S(2)}) collective-permute-start(f32[72,128]{1,0:T(8,128)S(1)} %screen_stats.1.own_ref), channel_id=1, source_target_pairs={{0,32},{4,36},{8,40},{12,44},{16,48},{20,52},{24,56},{28,60},{32,0... | collective-permute-start | bytes 110600 | tf_op jit(solution)/shard_map/ppermute | solution.py:52
  101.4 8.9 %collective-permute-start.7 = (f32[72,128]{1,0:T(8,128)S(1)}, f32[72,128]{1,0:T(8,128)S(1)}, u32[]{:S(2)}, u32[]{:S(2)}) collective-permute-start(f32[72,128]{1,0:T(8,128)S(1)} %screen_stats.1.own_ref), channel_id=1, source_target_pairs={{0,224},{4,228},{8,232},{12,236},{16,240},{20,244},{24,248},{28,25... | collective-permute-start | bytes 110600 | tf_op jit(solution)/shard_map/ppermute | solution.py:52
  106.4 26.0 %copy-start.3 = (s32[2]{0:T(128)}, s32[2]{0:T(128)S(1)}, u32[]{:S(2)}) copy-start(s32[2]{0:T(128)S(1)} %pad_add_fusion.id_ref) | copy-start | bytes 28
  106.4 26.0 %collective-permute-start.9 = (bf16[256,1024]{1,0:T(8,128)(2,1)S(1)}, bf16[256,1024]{1,0:T(8,128)(2,1)}, u32[]{:S(2)}, u32[]{:S(2)}) collective-permute-start(bf16[256,1024]{1,0:T(8,128)(2,1)S(1)} %bitcast.32), channel_id=1, source_target_pairs={{0,3},{1,0},{2,1},{3,2},{4,7},{5,4},{6,5},{7,6},{8,11},{9,8},{10,9... | collective-permute-start | bytes 1572872 | tf_op jit(solution)/shard_map/ppermute | solution.py:39
  110.3 27.1 %collective-permute-start.14 = (bf16[1024,256]{1,0:T(8,128)(2,1)}, bf16[1024,256]{1,0:T(8,128)(2,1)}, u32[]{:S(2)}, u32[]{:S(2)}) collective-permute-start(bf16[1024,256]{1,0:T(8,128)(2,1)} %get-tuple-element.24.refs_3_), channel_id=1, source_target_pairs={{0,3},{1,0},{2,1},{3,2},{4,7},{5,4},{6,5},{7,6},{8,11},{9,8},{10,9... | collective-permute-start | bytes 1572872 | tf_op jit(solution)/shard_map/ppermute | solution.py:39
  117.0 52.8 %all-to-all-start.2 = ((bf16[64,32,128]{2,1,0:T(8,128)(2,1)}), bf16[64,32,128]{2,1,0:T(8,128)(2,1)S(1)}, u32[]{:S(2)}, u32[]{:S(2)}) async-start(bf16[64,32,128]{2,1,0:T(8,128)(2,1)} %get-tuple-element.29), calls=%async_computation.2 | async-start | bytes 1048576 | tf_op jit(solution)/shard_map/all_to_all | solution.py:620
  126.6 10.3 %copy-start.11 = (bf16[1024,256]{1,0:T(8,128)(2,1)S(1)}, bf16[1024,256]{1,0:T(8,128)(2,1)}, u32[]{:S(2)}) copy-start(bf16[1024,256]{1,0:T(8,128)(2,1)} %copy-done.10) | copy-start | bytes 1572868
  127.5 37.5 %collective-permute-start.13 = (bf16[1536,256]{1,0:T(8,128)(2,1)S(1)}, bf16[1536,256]{1,0:T(8,128)(2,1)S(1)}, u32[]{:S(2)}, u32[]{:S(2)}) collective-permute-start(bf16[1536,256]{1,0:T(8,128)(2,1)S(1)} %copy-done.6), channel_id=1, source_target_pairs={{0,3},{1,0},{2,1},{3,2},{4,7},{5,4},{6,5},{7,6},{8,11},{9,8},{10,9... | collective-permute-start | bytes 2359304 | tf_op jit(solution)/shard_map/ppermute | solution.py:39
  128.3 8.7 %collective-permute-start.16 = (bf16[512,256]{1,0:T(8,128)(2,1)}, bf16[512,256]{1,0:T(8,128)(2,1)}, u32[]{:S(2)}, u32[]{:S(2)}) collective-permute-start(bf16[512,256]{1,0:T(8,128)(2,1)} %copy-done.14), channel_id=1, source_target_pairs={{0,1},{1,2},{2,3},{3,0},{4,5},{5,6},{6,7},{7,4},{8,9},{9,10},{10,1... | collective-permute-start | bytes 786440 | tf_op jit(solution)/shard_map/ppermute | solution.py:39
  129.2 11.2 %copy-start.7 = (bf16[1536,256]{1,0:T(8,128)(2,1)}, bf16[1536,256]{1,0:T(8,128)(2,1)S(1)}, u32[]{:S(2)}) copy-start(bf16[1536,256]{1,0:T(8,128)(2,1)S(1)} %collective-permute-done.11.refs_6_) | copy-start | bytes 2359300
  129.2 40.6 %collective-permute-start.17 = (bf16[1536,256]{1,0:T(8,128)(2,1)S(1)}, bf16[1536,256]{1,0:T(8,128)(2,1)}, u32[]{:S(2)}, u32[]{:S(2)}) collective-permute-start(bf16[1536,256]{1,0:T(8,128)(2,1)S(1)} %collective-permute-done.11.refs_6_), channel_id=1, source_target_pairs={{0,1},{1,2},{2,3},{3,0},{4,5},{5,6},{6,7},{7,4},{8,9},{9,10},{10,1... | collective-permute-start | bytes 2359304 | tf_op jit(solution)/shard_map/ppermute | solution.py:39
  132.4 32.5 %collective-permute-start.12 = (bf16[1024,256]{1,0:T(8,128)(2,1)}, bf16[1024,256]{1,0:T(8,128)(2,1)S(1)}, u32[]{:S(2)}, u32[]{:S(2)}) collective-permute-start(bf16[1024,256]{1,0:T(8,128)(2,1)} %get-tuple-element.24.refs_3_), channel_id=1, source_target_pairs={{0,1},{1,2},{2,3},{3,0},{4,5},{5,6},{6,7},{7,4},{8,9},{9,10},{10,1... | collective-permute-start | bytes 1572872 | tf_op jit(solution)/shard_map/ppermute | solution.py:39
  136.9 28.0 %collective-permute-start.15 = (bf16[1024,256]{1,0:T(8,128)(2,1)S(1)}, bf16[1024,256]{1,0:T(8,128)(2,1)S(1)}, u32[]{:S(2)}, u32[]{:S(2)}) collective-permute-start(bf16[1024,256]{1,0:T(8,128)(2,1)S(1)} %copy-done.11), channel_id=1, source_target_pairs={{0,3},{1,0},{2,1},{3,2},{4,7},{5,4},{6,5},{7,6},{8,11},{9,8},{10,9... | collective-permute-start | bytes 1572872 | tf_op jit(solution)/shard_map/ppermute | solution.py:39
  137.4 32.3 %collective-permute-start.18 = (bf16[1024,256]{1,0:T(8,128)(2,1)}, bf16[1024,256]{1,0:T(8,128)(2,1)}, u32[]{:S(2)}, u32[]{:S(2)}) collective-permute-start(bf16[1024,256]{1,0:T(8,128)(2,1)} %collective-permute-done.14.refs_11_), channel_id=1, source_target_pairs={{0,3},{1,0},{2,1},{3,2},{4,7},{5,4},{6,5},{7,6},{8,11},{9,8},{10,9... | collective-permute-start | bytes 1572872 | tf_op jit(solution)/shard_map/ppermute | solution.py:39
  164.9 0.8 copy-start.12
  164.9 1.0 copy-start.13
  165.9 3.9 %copy-start.8 = (bf16[1536,256]{1,0:T(8,128)(2,1)}, bf16[1536,256]{1,0:T(8,128)(2,1)S(1)}, u32[]{:S(2)}) copy-start(bf16[1536,256]{1,0:T(8,128)(2,1)S(1)} %collective-permute-done.13.refs_10_) | copy-start | bytes 2359300
  169.8 0.9 copy-start.5
